TPU v7x, 32 devices: a whole 2x2x4 slice. The times are simulated.
32 devices in a mesh: groups: 2 (over y), ctx: 16 (over z, x, core).
Axes of the slice: x: 2, y: 2, z: 4, core: 2. Of those that a mesh axis runs over, the one named last changes fastest.
Arguments:
- self_qkv: bfloat16 [3, 8192, 2048], P(None, ('groups', 'ctx')), parts along dimension 1, may hold values from -64 to 64
- windows: int32 [16], replicated, may hold values from 256 to 2048, as said below
- k_gain: float32 [2048], replicated, may hold values from 0.25 to 1.75
- cont_qkv: bfloat16 [3, 256, 2048], P(None, ('groups', 'ctx')), parts along dimension 1, may hold values from -64 to 64
- starts: int32 [32], P('groups'), parts along dimension 0, may hold values from 1 to 4096
Outputs:
- self_out: bfloat16 [8192, 2048], P(('groups', 'ctx')), parts along dimension 0
- cross_out: bfloat16 [256, 2048], P(('groups', 'ctx')), parts along dimension 0
There are 2 independent parts, one for each index of `groups`. A program takes and returns all parts, laid end to end along the dimension named above; an argument that names none is the same for every part. Nothing has to cross between parts.
Inputs may be any that keep to these rules, and one draw needn't show every extreme that they name: `windows`: some head has a window of exactly 2048.
All inputs are finite; a program needn't handle non-finite values.
Results may differ from a plain program's by a relative error of at most 0.0055.
Values may be sent and summed in bfloat16 or wider, within the bound.
No kernel may reach another device: no remote copies, remote signals or barrier semaphores. Data moves between devices by JAX's collectives and lax.ppermute only.
A program may use at most 128 MiB of HBM per device.

v0:
```python
import math

import jax
import jax.numpy as jnp
from jax import lax
from jax.sharding import PartitionSpec as P

WIN = 2048
CLEN = 8


EPSILON = 1e-06
NEGATIVE = -1e30


def shifted(value, axis, steps):
    count = lax.axis_size(axis)
    initial, last = (max(0, -steps), min(count, count - steps))
    return lax.ppermute(value, axis, [(source, source + steps) for source in range(initial, last)])


def finish_rows(cache_high, cache_totals, weighted, own_rows):
    rows_here = own_rows.shape[1]
    features = own_rows.shape[2]
    head_count = cache_high.shape[1]
    head_dim = features // head_count
    groups_here = rows_here // CLEN
    parts = own_rows.reshape(3, groups_here, CLEN, head_count, head_dim)
    scaling = 1.0 / math.sqrt(head_dim)
    scores = (
        jnp.einsum("cihd,cjhd->hcij", parts[0], parts[1], preferred_element_type=jnp.float32)
        * scaling
    )
    causal = (jnp.arange(CLEN)[None, :] <= jnp.arange(CLEN)[:, None])[None, None]
    scores = jnp.where(causal, scores, NEGATIVE)
    prior_high = cache_high.T.reshape(head_count, groups_here, CLEN)
    final = jnp.maximum(prior_high, jnp.max(scores, axis=-1))
    rescale = jnp.exp(prior_high - final)
    expo = jnp.where(causal, jnp.exp(scores - final[..., None]), 0.0)
    totals = rescale * cache_totals.T.reshape(head_count, groups_here, CLEN) + jnp.sum(
        expo, axis=-1
    )
    own_sum = jnp.einsum(
        "hcij,cjhd->cihd", expo.astype(jnp.bfloat16), parts[2], preferred_element_type=jnp.float32
    )
    merged = (
        weighted.reshape(groups_here, CLEN, head_count, head_dim)
        * jnp.transpose(rescale, (1, 2, 0))[..., None]
        + own_sum
    )
    result = merged / jnp.transpose(totals, (1, 2, 0))[..., None]
    return result.reshape(rows_here, features).astype(jnp.bfloat16)


def per_device(self_qkv, windows, k_gain, cont_qkv, starts):
    length = self_qkv.shape[1]
    features = self_qkv.shape[2]
    head_count = windows.shape[0]
    head_dim = features // head_count
    scaling = 1.0 / math.sqrt(head_dim)
    anchor = lax.axis_index("ctx") * length
    reach = WIN // length
    width = (reach + 1) * length
    key_value = self_qkv[1:3]
    earlier = []
    for distance in range(1, reach + 1):
        earlier.append(shifted(key_value, "ctx", distance))
    band = jnp.concatenate(earlier[::-1] + [key_value], axis=1)
    distance_grid = (
        jnp.arange(length, dtype=jnp.int32)[:, None]
        + reach * length
        - jnp.arange(width, dtype=jnp.int32)[None, :]
    )
    key_position = anchor - reach * length + jnp.arange(width, dtype=jnp.int32)

    def one_head(head):
        offset = head * head_dim
        queries = lax.dynamic_slice_in_dim(self_qkv[0], offset, head_dim, 1)
        keys = lax.dynamic_slice_in_dim(band[0], offset, head_dim, 1)
        values = lax.dynamic_slice_in_dim(band[1], offset, head_dim, 1)
        scores = (
            jnp.einsum("id,jd->ij", queries, keys, preferred_element_type=jnp.float32) * scaling
        )
        visible = (
            (distance_grid >= 0) & (distance_grid < windows[head]) & (key_position >= 0)[None, :]
        )
        scores = jnp.where(visible, scores, NEGATIVE)
        highest = jnp.max(scores, axis=-1, keepdims=True)
        expo = jnp.where(visible, jnp.exp(scores - highest), 0.0)
        weights = (expo / jnp.sum(expo, axis=-1, keepdims=True)).astype(jnp.bfloat16)
        return jnp.dot(weights, values, preferred_element_type=jnp.float32).astype(jnp.bfloat16)

    attended = lax.map(one_head, jnp.arange(head_count, dtype=jnp.int32))
    self_out = jnp.transpose(attended, (1, 0, 2)).reshape(length, features)
    hidden = self_out.astype(jnp.float32).reshape(length, head_count, head_dim)
    normed = hidden * lax.rsqrt(jnp.mean(hidden * hidden, axis=-1, keepdims=True) + EPSILON)
    cache_keys = (
        (normed.reshape(length, features) * k_gain)
        .astype(jnp.bfloat16)
        .reshape(length, head_count, head_dim)
    )
    cache_values = self_out.reshape(length, head_count, head_dim)
    gathered = lax.all_gather(cont_qkv[0], "ctx", axis=0, tiled=True)
    rows_all = gathered.shape[0]
    rows_here = cont_qkv.shape[1]
    conts_all = starts.shape[0]
    row_start = jnp.broadcast_to(starts[:, None], (conts_all, rows_all // conts_all)).reshape(
        rows_all
    )
    positions = anchor + jnp.arange(length, dtype=jnp.int32)
    block = math.gcd(rows_all, 512)
    block_count = rows_all // block
    query_blocks = gathered.reshape(block_count, block, head_count, head_dim)
    start_blocks = row_start.reshape(block_count, block)

    def block_scores(query_block, start_block):
        raw = (
            jnp.einsum("ihd,jhd->hij", query_block, cache_keys, preferred_element_type=jnp.float32)
            * scaling
        )
        seen = (positions[None, :] < start_block[:, None])[None]
        return (jnp.where(seen, raw, NEGATIVE), seen)

    def local_part(inputs):
        query_block, start_block = inputs
        masked, seen = block_scores(query_block, start_block)
        peak = jnp.max(masked, axis=-1)
        local_expo = jnp.where(seen, jnp.exp(masked - peak[..., None]), 0.0)
        totals = jnp.sum(local_expo, axis=-1)
        summed = jnp.einsum(
            "hij,jhd->ihd",
            local_expo.astype(jnp.bfloat16),
            cache_values,
            preferred_element_type=jnp.float32,
        )
        return (summed.reshape(block, features), peak.T, totals.T)

    summed, peaks, totals = lax.map(local_part, (query_blocks, start_blocks))
    sources = lax.axis_size("ctx")
    summed = summed.reshape(sources, rows_here, features)
    peaks = peaks.reshape(sources, rows_here, head_count)
    totals = totals.reshape(sources, rows_here, head_count)
    summed_in, peaks_in, totals_in = (
        lax.all_to_all(
            summed.astype(jnp.bfloat16), "ctx", split_axis=0, concat_axis=0, tiled=True
        ).astype(summed.dtype),
        lax.all_to_all(
            peaks.astype(jnp.bfloat16), "ctx", split_axis=0, concat_axis=0, tiled=True
        ).astype(peaks.dtype),
        lax.all_to_all(
            totals.astype(jnp.bfloat16), "ctx", split_axis=0, concat_axis=0, tiled=True
        ).astype(totals.dtype),
    )
    cache_high = jnp.max(peaks_in, axis=0)
    rescale = jnp.exp(peaks_in - cache_high[None])
    weighted = jnp.sum(
        summed_in.reshape(sources, rows_here, head_count, head_dim) * rescale[..., None], axis=0
    )
    cache_totals = jnp.sum(rescale * totals_in, axis=0)
    cross_out = finish_rows(cache_high, cache_totals, weighted, cont_qkv)
    return (self_out, cross_out)


def solution(mesh):
    in_specs = (
        P(None, ("groups", "ctx"), None),
        P(),
        P(),
        P(None, ("groups", "ctx"), None),
        P("groups"),
    )
    out_specs = (P(("groups", "ctx"), None), P(("groups", "ctx"), None))
    return jax.shard_map(
        per_device, mesh=mesh, in_specs=in_specs, out_specs=out_specs, check_vma=False
    )
```

profile of v0, /device:TPU:0, one launch (start us, length us, event | category | flops | bytes accessed | tf_op | source)
XLA Modules:
  0.0 854.6 jit_solution(9346026822741052805)
XLA Ops:
  0.7 3.2 slice.25
  3.9 7.3 collective-permute-start
  11.2 4.9 collective-permute-start.1
  16.1 3.5 collective-permute-start.2
  23.8 32.4 %collective-permute-done = bf16[2,256,2048]{2,1,0:T(8,128)(2,1)} collective-permute-done((bf16[2,256,2048]{2,1,0:T(8,128)(2,1)}, bf16[2,256,2048]{2,1,0:T(8,128)(2,1)}, u32[]{:S(2)}, u32[]{:S(2)}) %collective-permute-start) | collective-permute-done | bytes 2097184 | tf_op jit(solution)/shard_map/ppermute | solution.py:19
  59.1 301.0 %all-gather = bf16[1,128,2048]{2,1,0:T(8,128)(2,1)S(1)} all-gather(bf16[1,8,2048]{2,1,0:T(8,128)(2,1)S(1)} %slice-done), channel_id=2, replica_groups=mesh['groups'=2,'ctx'=16] {'ctx'}, dimensions={1}, use_global_device_ids=true | all-gather | bytes 557056 | tf_op jit(solution)/shard_map/all_gather | solution.py:103
  360.0 3.6 collective-permute-start.6
  376.9 30.9 %collective-permute-done.6 = bf16[2,256,2048]{2,1,0:T(8,128)(2,1)} collective-permute-done((bf16[2,256,2048]{2,1,0:T(8,128)(2,1)}, bf16[2,256,2048]{2,1,0:T(8,128)(2,1)}, u32[]{:S(2)}, u32[]{:S(2)}) %collective-permute-start.6) | collective-permute-done | bytes 2097184 | tf_op jit(solution)/shard_map/ppermute | solution.py:19
  412.3 6.5 copy-done
  418.7 278.3 %while.8 = (s32[]{:T(128)}, bf16[16,256,128]{2,1,0:T(8,128)(2,1)}, s32[16]{0:T(128)S(1)}, s32[16]{0:T(128)S(1)}, bf16[3,256,2048]{2,1,0:T(8,128)(2,1)S(1)}, /*in...) while((s32[]{:T(128)}, bf16[16,256,128]{2,1,0:T(8,128)(2,1)}, ...), condition=%wide.region_3.4_spmd.clone.clone, body=%wide.region_0.3_spmd.clone.clone.sunk | while | flops 316772352 | bytes 48255728 | solution.py:93
  422.0 8.1 fusion.75
  439.4 8.1 fusion.75
  456.8 8.1 fusion.75
  474.2 8.1 fusion.75
  491.6 8.1 fusion.75
  509.0 8.1 fusion.75
  526.4 8.1 fusion.75
  543.8 8.1 fusion.75
  561.2 8.1 fusion.75
  578.6 8.1 fusion.75
  595.9 8.1 fusion.75
  613.3 8.1 fusion.75
  630.8 8.1 fusion.75
  648.1 8.1 fusion.75
  665.5 8.1 fusion.75
  682.9 8.1 fusion.75
  702.3 116.6 %all-to-all-start.2 = ((bf16[16,8,16]{2,1,0:T(8,128)(2,1)}), bf16[16,8,16]{2,1,0:T(8,128)(2,1)S(1)}, u32[]{:S(2)}, u32[]{:S(2)}) async-start(bf16[16,8,16]{2,1,0:T(8,128)(2,1)} %bitcast.20), calls=%async_computation.2 | async-start | bytes 65536 | tf_op jit(solution)/shard_map/all_to_all | solution.py:150
  819.7 5.9 all-to-all-done.2
  825.6 3.5 all-to-all-start.1
  832.6 3.1 all-to-all-done.1
  835.7 3.6 all-to-all-start
  842.2 11.3 %all-to-all-done = bf16[16,8,2048]{2,1,0:T(8,128)(2,1)S(1)} async-done(((bf16[16,8,2048]{2,1,0:T(8,128)(2,1)}), bf16[16,8,2048]{2,1,0:T(8,128)(2,1)S(1)}, u32[]{:S(2)}, u32[]{:S(2)}) %all-to-all-start) | async-done | bytes 524320 | tf_op jit(solution)/shard_map/all_to_all | solution.py:144
  (179 shorter events, 151.1 us)
Async XLA Ops:
  0.6 23.0 %copy-start.2 = (bf16[3,8,2048]{2,1,0:T(8,128)(2,1)S(1)}, bf16[3,8,2048]{2,1,0:T(8,128)(2,1)}, u32[]{:S(2)}) copy-start(bf16[3,8,2048]{2,1,0:T(8,128)(2,1)} %param.10) | copy-start | bytes 294916
  0.6 58.4 %slice-start = ((bf16[3,8,2048]{2,1,0:T(8,128)(2,1)}), bf16[1,8,2048]{2,1,0:T(8,128)(2,1)S(1)}, s32[]{:S(2)}) async-start(bf16[3,8,2048]{2,1,0:T(8,128)(2,1)} %param.10), calls=%async_computation.3 | async-start | bytes 65536 | tf_op jit(solution)/shard_map/slice | solution.py:103
  0.7 58.2 %copy-start.3 = (s32[16]{0:T(128)S(1)}, s32[16]{0:T(128)}, u32[]{:S(2)}) copy-start(s32[16]{0:T(128)} %param.11) | copy-start | bytes 196
  3.9 52.3 %collective-permute-start = (bf16[2,256,2048]{2,1,0:T(8,128)(2,1)}, bf16[2,256,2048]{2,1,0:T(8,128)(2,1)}, u32[]{:S(2)}, u32[]{:S(2)}) collective-permute-start(bf16[2,256,2048]{2,1,0:T(8,128)(2,1)} %slice.25), channel_id=1, source_target_pairs={{0,8},{1,9},{2,10},{3,11},{4,12},{5,13},{6,14},{7,15},{16,24},{17,... | collective-permute-start | bytes 6291464 | tf_op jit(solution)/shard_map/ppermute | solution.py:19
  11.2 348.9 %collective-permute-start.1 = (bf16[2,256,2048]{2,1,0:T(8,128)(2,1)}, bf16[2,256,2048]{2,1,0:T(8,128)(2,1)}, u32[]{:S(2)}, u32[]{:S(2)}) collective-permute-start(bf16[2,256,2048]{2,1,0:T(8,128)(2,1)} %slice.25), channel_id=1, source_target_pairs={{0,7},{1,8},{2,9},{3,10},{4,11},{5,12},{6,13},{7,14},{8,15},{16,23... | collective-permute-start | bytes 6291464 | tf_op jit(solution)/shard_map/ppermute | solution.py:19
  16.1 347.7 %collective-permute-start.2 = (bf16[2,256,2048]{2,1,0:T(8,128)(2,1)}, bf16[2,256,2048]{2,1,0:T(8,128)(2,1)}, u32[]{:S(2)}, u32[]{:S(2)}) collective-permute-start(bf16[2,256,2048]{2,1,0:T(8,128)(2,1)} %slice.25), channel_id=1, source_target_pairs={{0,6},{1,7},{2,8},{3,9},{4,10},{5,11},{6,12},{7,13},{8,14},{9,15},... | collective-permute-start | bytes 6291464 | tf_op jit(solution)/shard_map/ppermute | solution.py:19
  19.6 353.7 %collective-permute-start.3 = (bf16[2,256,2048]{2,1,0:T(8,128)(2,1)}, bf16[2,256,2048]{2,1,0:T(8,128)(2,1)}, u32[]{:S(2)}, u32[]{:S(2)}) collective-permute-start(bf16[2,256,2048]{2,1,0:T(8,128)(2,1)} %slice.25), channel_id=1, source_target_pairs={{0,5},{1,6},{2,7},{3,8},{4,9},{5,10},{6,11},{7,12},{8,13},{9,14},{... | collective-permute-start | bytes 6291464 | tf_op jit(solution)/shard_map/ppermute | solution.py:19
  22.2 352.8 %collective-permute-start.4 = (bf16[2,256,2048]{2,1,0:T(8,128)(2,1)}, bf16[2,256,2048]{2,1,0:T(8,128)(2,1)S(1)}, u32[]{:S(2)}, u32[]{:S(2)}) collective-permute-start(bf16[2,256,2048]{2,1,0:T(8,128)(2,1)} %slice.25), channel_id=1, source_target_pairs={{0,4},{1,5},{2,6},{3,7},{4,8},{5,9},{6,10},{7,11},{8,12},{9,13},{1... | collective-permute-start | bytes 6291464 | tf_op jit(solution)/shard_map/ppermute | solution.py:19
  56.2 319.0 %collective-permute-start.5 = (bf16[2,256,2048]{2,1,0:T(8,128)(2,1)}, bf16[2,256,2048]{2,1,0:T(8,128)(2,1)}, u32[]{:S(2)}, u32[]{:S(2)}) collective-permute-start(bf16[2,256,2048]{2,1,0:T(8,128)(2,1)} %slice.25), channel_id=1, source_target_pairs={{0,3},{1,4},{2,5},{3,6},{4,7},{5,8},{6,9},{7,10},{8,11},{9,12},{10... | collective-permute-start | bytes 6291464 | tf_op jit(solution)/shard_map/ppermute | solution.py:19
  360.0 47.8 %collective-permute-start.6 = (bf16[2,256,2048]{2,1,0:T(8,128)(2,1)}, bf16[2,256,2048]{2,1,0:T(8,128)(2,1)}, u32[]{:S(2)}, u32[]{:S(2)}) collective-permute-start(bf16[2,256,2048]{2,1,0:T(8,128)(2,1)} %slice.25), channel_id=1, source_target_pairs={{0,2},{1,3},{2,4},{3,5},{4,6},{5,7},{6,8},{7,9},{8,10},{9,11},{10,... | collective-permute-start | bytes 6291464 | tf_op jit(solution)/shard_map/ppermute | solution.py:19
  363.8 45.8 %collective-permute-start.7 = (bf16[2,256,2048]{2,1,0:T(8,128)(2,1)}, bf16[2,256,2048]{2,1,0:T(8,128)(2,1)}, u32[]{:S(2)}, u32[]{:S(2)}) collective-permute-start(bf16[2,256,2048]{2,1,0:T(8,128)(2,1)} %slice.25), channel_id=1, source_target_pairs={{0,1},{1,2},{2,3},{3,4},{4,5},{5,6},{6,7},{7,8},{8,9},{9,10},{10,1... | collective-permute-start | bytes 6291464 | tf_op jit(solution)/shard_map/ppermute | solution.py:19
  409.6 2.5 copy-start.1
  412.1 6.6 copy-start.5
  412.3 6.5 copy-start
  418.7 280.1 %copy-start.4 = (f32[2048]{0:T(1024)S(1)}, f32[2048]{0:T(1024)}, u32[]{:S(2)}) copy-start(f32[2048]{0:T(1024)} %param.9) | copy-start | bytes 24580
  702.3 123.3 %all-to-all-start.2 = ((bf16[16,8,16]{2,1,0:T(8,128)(2,1)}), bf16[16,8,16]{2,1,0:T(8,128)(2,1)S(1)}, u32[]{:S(2)}, u32[]{:S(2)}) async-start(bf16[16,8,16]{2,1,0:T(8,128)(2,1)} %bitcast.20), calls=%async_computation.2 | async-start | bytes 65536 | tf_op jit(solution)/shard_map/all_to_all | solution.py:150
  825.6 10.1 %all-to-all-start.1 = ((bf16[16,8,16]{2,1,0:T(8,128)(2,1)}), bf16[16,8,16]{2,1,0:T(8,128)(2,1)S(1)}, u32[]{:S(2)}, u32[]{:S(2)}) async-start(bf16[16,8,16]{2,1,0:T(8,128)(2,1)} %bitcast.6), calls=%async_computation.1 | async-start | bytes 65536 | tf_op jit(solution)/shard_map/all_to_all | solution.py:147
  835.7 17.8 %all-to-all-start = ((bf16[16,8,2048]{2,1,0:T(8,128)(2,1)}), bf16[16,8,2048]{2,1,0:T(8,128)(2,1)S(1)}, u32[]{:S(2)}, u32[]{:S(2)}) async-start(bf16[16,8,2048]{2,1,0:T(8,128)(2,1)} %convert_element_type.69), calls=%async_computation | async-start | bytes 1048576 | tf_op jit(solution)/shard_map/all_to_all | solution.py:144
where the time goes:
time: 856 us; the launch traced here: 855 us
  blocking collectives  301 us (35%)
  local copies, waits for them, and re-layouts  179 us (21%)
  starting transfers between devices  153 us (18%)
  waiting for transfers between devices  83.7 us (10%)
  matrix products  71.8 us (8%)
  loops' own time  35.4 us (4%)
  other arithmetic  30.3 us (4%)
    all_gather x1, blocking collectives, per_device(): gathered = lax.all_gather(cont_qkv[0], 'ctx', axis=0, tiled=True)  301 us
    slice x16, local copies, waits for them, and re-layouts, one_head(): values = lax.dynamic_slice_in_dim(band[1], offset, head_dim, 1)  130 us
    all_to_all x1, starting transfers between devices, per_device(): lax.all_to_all(totals.astype(jnp.bfloat16), 'ctx', split_axis=0, concat_a...  117 us
    ppermute x8, waiting for transfers between devices, shifted(): lax.ppermute(value, axis, [(source, source + steps) for source in range(i...  63.4 us
    dot_general x16, matrix products, one_head(): jnp.dot(weights, values, preferred_element_type=jnp.float32)  39.7 us
    another operation x1, loops' own time, per_device(): attended = lax.map(one_head, jnp.arange(head_count, dtype=jnp.int32))  35.4 us
    ppermute x8, starting transfers between devices, shifted(): lax.ppermute(value, axis, [(source, source + steps) for source in range(i...  29.1 us
    reduce_sum x16, other arithmetic, one_head(): jnp.sum(expo, axis=-1, keepdims=True)  27.1 us
  transfers between devices with their start and end apart: 11, of which 5 were waited for; matrix products, arithmetic and copies ran while one was open for 2% of the time, Pallas kernels for 0%

commit v1 on v0

v1 whole, which is shorter than its diff:
```python
import functools
import math

import jax
import jax.numpy as jnp
from jax import lax
from jax.experimental import pallas as pl
from jax.experimental.pallas import tpu as pltpu
from jax.sharding import PartitionSpec as P


WIN = 2048
CLEN = 8

EPSILON = 1e-06
NEGATIVE = -1e30
FLOOR = -1e29
BF16 = jnp.bfloat16
F32 = jnp.float32

SMEM = pl.BlockSpec(memory_space=pltpu.SMEM)
VMEM = pl.BlockSpec(memory_space=pltpu.VMEM)
ANY = pl.BlockSpec(memory_space=pl.ANY)


def cost(micros):
    return pl.CostEstimate(flops=int(micros * 1.15e9), bytes_accessed=0, transcendentals=0)


def pieces(value):
    high = value.astype(BF16)
    rest = value - high.astype(F32)
    middle = rest.astype(BF16)
    low = (rest - middle.astype(F32)).astype(BF16)
    return high, middle, low


def dot(left, right, contract):
    return lax.dot_general(left, right, ((contract[:1], contract[1:]), ((), ())), preferred_element_type=F32)


def lanes(head, head_dim):
    return pl.ds(pl.multiple_of(head * head_dim, head_dim), head_dim)


def pack_kernel(dims, axis, order, qkv, *outs):
    group, slots, near, head_dim = dims
    step = pl.program_id(0)
    far = slots - near
    mine = lax.rem(lax.axis_index(axis), group)
    for k in range(group):
        kv_far, q_near, rest = outs[k], outs[group + k], outs[2 * group + k]
        first = jnp.bitwise_xor(mine, k) * slots

        def move(target, spot, start, heads):
            for c in range(heads):
                column = slice(c * head_dim, (c + 1) * head_dim)
                target[spot + (slice(None), column)] = qkv[0, :, lanes(order[start + c], head_dim)]

        @pl.when(step == 2)
        def _():
            move(q_near, (), first, near)
            move(rest, (0,), first + near, far)

        @pl.when(step < 2)
        def _():
            move(rest, (0,), first, near)
            move(kv_far, (0,), first + near, far)


def gather_kernel(axis, *refs):
    group = len(refs) - 2
    blocks, out, sems = refs[:group], refs[group], refs[group + 1]
    mine = lax.rem(lax.axis_index(axis), group)
    copies = [
        pltpu.make_async_copy(block, out.at[jnp.bitwise_xor(mine, k)], sems.at[k]) for k, block in enumerate(blocks)
    ]
    for copy in copies:
        copy.start()
    for copy in copies:
        copy.wait()


def pack_rows_kernel(dims, order, rows, out):
    group, slots, _, head_dim = dims
    for device in range(out.shape[0]):
        for c in range(slots):
            out[device, :, c * head_dim : (c + 1) * head_dim] = rows[
                0, :, lanes(order[(device % group) * slots + c], head_dim)
            ]


def attend(kv, queries, window, head, part, base, high_limit, key_parts, state, block, head_dim):
    peak, total, acc = state
    shards = block // kv.shape[2]
    factor = math.log2(math.e) / math.sqrt(head_dim)
    column = lanes(head, head_dim)
    row_index = lax.broadcasted_iota(jnp.int32, (block, block), 1)
    key_index = lax.broadcasted_iota(jnp.int32, (block, block), 0)

    def step(distance, diagonal):
        spot = pl.ds((base + part - distance) * shards, shards)
        keys = kv[spot, 0, :, column].reshape(block, head_dim)
        values = kv[spot, 1, :, column].reshape(block, head_dim)
        q = queries[pl.ds(part * shards, shards), :, column].reshape(block, head_dim)
        scores = dot(keys, q, (1, 1))
        gap = row_index - key_index
        visible = gap < window - distance * block
        if diagonal:
            visible = visible & (gap >= 0)
        scores = jnp.where(visible, scores, NEGATIVE)
        old = peak[0:1, :]
        new = jnp.maximum(old, jnp.max(scores, axis=0, keepdims=True))
        fade = jnp.exp2((old - new) * factor)
        expo = jnp.exp2((scores - new) * factor)
        total[0:1, :] = total[0:1, :] * fade + jnp.sum(expo, axis=0, keepdims=True)
        peak[0:1, :] = new
        acc[...] = acc[...] * fade + dot(values, expo.astype(BF16), (0, 0))

    reach = jnp.minimum((window + block - 2) // block, high_limit)
    low = jnp.maximum(base + part - (key_parts - 1), 0)

    if base - (key_parts - 1) <= 0:

        @pl.when(low == 0)
        def _():
            step(0, True)

    def loop(distance, carry):
        step(distance, False)
        return carry

    lax.fori_loop(jnp.maximum(low, 1), jnp.minimum(reach, base + part) + 1, loop, 0)


def cross_part(out, rows, starts, gain, order, first, offset, anchor, result, head_dim, base=0):
    heads = out.shape[2] // head_dim
    keys_here = out.shape[0] * out.shape[1]
    clen = rows.shape[1]
    devices = rows.shape[0]
    block = min(devices * clen, 128)
    per = block // clen
    factor = math.log2(math.e) / math.sqrt(head_dim)
    tail = slice(base + heads * head_dim, base + (heads + 1) * head_dim)
    for c in range(heads):
        column = slice(c * head_dim, (c + 1) * head_dim)
        values = out[:, :, column].reshape(keys_here, head_dim)
        hidden = values.astype(F32)
        norm = hidden * lax.rsqrt(jnp.mean(hidden * hidden, axis=-1, keepdims=True) + EPSILON)
        keys = (norm * gain[pl.ds(order[first + c], 1), :]).astype(BF16)

        def blocks(index, carry):
            spot = pl.ds(index * per, per)
            q = rows[spot, :, offset + c * head_dim : offset + (c + 1) * head_dim].reshape(block, head_dim)
            scores = dot(q, keys, (1, 1))
            position = anchor + lax.broadcasted_iota(jnp.int32, (block, keys_here), 1)
            seen = position < starts[pl.ds(index * block, block), :]
            scores = jnp.where(seen, scores, NEGATIVE)
            high = jnp.maximum(jnp.max(scores, axis=1, keepdims=True), FLOOR)
            expo = jnp.exp2((scores - high) * factor)
            total = jnp.sum(expo, axis=1, keepdims=True)
            summed = dot(expo.astype(BF16), values, (1, 0))
            result[spot, :, base + c * head_dim : base + (c + 1) * head_dim] = summed.astype(BF16).reshape(
                per, clen, head_dim
            )
            lane = lax.broadcasted_iota(jnp.int32, (block, head_dim), 1)
            stats = jnp.zeros((block, head_dim), F32) if c == 0 else None
            for k, piece in enumerate(pieces(high) + pieces(total)):
                value = jnp.broadcast_to(piece.astype(F32), (block, head_dim))
                if stats is None:
                    stats = result[spot, :, tail].reshape(block, head_dim).astype(F32)
                stats = jnp.where(lane == c * 6 + k, value, stats)
            result[spot, :, tail] = stats.astype(BF16).reshape(per, clen, head_dim)
            return carry

        lax.fori_loop(0, devices * clen // block, blocks, 0)


def scatter_blocks(axis, value, outs):
    mine = lax.rem(lax.axis_index(axis), len(outs))
    for k, out in enumerate(outs):
        out[...] = value[jnp.bitwise_xor(mine, k)]


def reset(peak, total, acc):
    peak[...] = jnp.full(peak.shape, FLOOR, F32)
    total[...] = jnp.zeros(total.shape, F32)
    acc[...] = jnp.zeros(acc.shape, F32)


def far_kernel(dims, axis, order, windows, q, kv0, kv1, kv2, rows, starts, gain, *refs):
    group, slots, near, head_dim, block = dims
    outs, (result, out, kv, peak, total, acc, sems) = refs[:group], refs[group:]
    device = lax.axis_index(axis)
    row = device // group
    mine = lax.rem(device, group) * slots + near
    copies = [
        pltpu.make_async_copy(source, kv.at[pl.ds(k * group, group)], sems.at[k])
        for k, source in enumerate((kv2, kv1, kv0))
    ]
    for copy in copies:
        copy.start()
    for copy in copies:
        copy.wait()
    length = out.shape[1]
    parts = group * length // block
    shards = block // length

    def one(index, carry):
        head = index // parts
        part = lax.rem(index, parts)
        window = windows[order[mine + head]]
        reset(peak, total, acc)
        attend(
            kv, q, window, head, part, 2 * parts, row * parts + part, 3 * parts, (peak, total, acc), block, head_dim
        )
        done = (acc[...] / total[0:1, :]).astype(BF16).T
        out[pl.ds(part * shards, shards), :, lanes(head, head_dim)] = done.reshape(shards, length, head_dim)
        return carry

    lax.fori_loop(0, parts * (slots - near), one, 0)
    scatter_blocks(axis, out, outs)
    cross_part(out, rows, starts, gain, order, mine, near * head_dim, row * group * length, result, head_dim)


def near_kernel(dims, axis, delta, count, order, windows, q, kv, *refs):
    group, slots, near, head_dim, block = dims
    device = lax.axis_index(axis)
    row = device // group
    mine = lax.rem(device, group) * slots
    length = q.shape[1]
    parts = group * length // block
    if delta == 2:
        state, peak, total, acc = refs
    else:
        sums, stats_out, peak, total, acc = refs

    def one(index, carry):
        head = index // parts
        part = lax.rem(index, parts)
        window = windows[order[mine + head]]
        span = pl.ds(pl.multiple_of(part * block, block), block)
        reset(peak, total, acc)
        limit = jnp.where(row + delta < count, 2 * WIN, -1) if delta > 0 else 2 * WIN
        attend(kv, q, window, head, part, delta * parts, limit, parts, (peak, total, acc), block, head_dim)
        if delta == 2:
            write_state(state, head, span, peak[0:1, :], total[0:1, :], acc[...], head_dim)
        else:
            sums[head, :, span] = acc[...]
            stats_out[head, 0:1, span] = peak[0:1, :]
            stats_out[head, 1:2, span] = total[0:1, :]
        return carry

    lax.fori_loop(0, parts * near, one, 0)


def write_state(state, head, span, peak, total, acc, head_dim):
    state[head, 0:head_dim, span] = acc.astype(BF16)
    width = peak.shape[1]
    index = lax.broadcasted_iota(jnp.int32, (16, width), 0)
    stats = jnp.zeros((16, width), F32)
    for k, piece in enumerate(pieces(peak) + pieces(total)):
        stats = jnp.where(index == k, piece.astype(F32), stats)
    state[head, head_dim : head_dim + 16, span] = stats.astype(BF16)


def merged_state(state, sums, stats, head, span, valid, head_dim):
    factor = math.log2(math.e) / math.sqrt(head_dim)
    arrived = state[head, head_dim : head_dim + 16, span].astype(F32)
    far_peak = jnp.where(valid, arrived[0:1] + arrived[1:2] + arrived[2:3], FLOOR)
    far_total = jnp.where(valid, arrived[3:4] + arrived[4:5] + arrived[5:6], 0.0)
    peak, total = stats[head, 0:1, span], stats[head, 1:2, span]
    high = jnp.maximum(peak, far_peak)
    here = jnp.exp2((peak - high) * factor)
    there = jnp.where(valid, jnp.exp2((far_peak - high) * factor), 0.0)
    acc = sums[head, :, span] * here
    arrived_sum = jnp.where(valid, state[head, 0:head_dim, span].astype(F32), 0.0)
    return high, total * here + far_total * there, acc + arrived_sum * there


def merge_kernel(dims, axis, arrived, sums, stats, state):
    group, _, near, head_dim, block = dims
    valid = lax.axis_index(axis) // group >= 1
    width = sums.shape[2]

    def one(index, carry):
        head = index // (width // block)
        span = pl.ds(pl.multiple_of(lax.rem(index, width // block) * block, block), block)
        peak, total, acc = merged_state(arrived, sums, stats, head, span, valid, head_dim)
        write_state(state, head, span, peak, total, acc, head_dim)
        return carry

    lax.fori_loop(0, near * (width // block), one, 0)


def last_kernel(dims, axis, order, arrived, sums, stats, rows, starts, gain, other, *refs):
    group, slots, near, head_dim, block = dims
    outs, (result, out) = refs[:group], refs[group:]
    row = lax.axis_index(axis) // group
    mine = lax.rem(lax.axis_index(axis), group) * slots
    length = out.shape[1]
    parts = group * length // block
    shards = block // length

    def one(index, carry):
        head = index // parts
        part = lax.rem(index, parts)
        span = pl.ds(pl.multiple_of(part * block, block), block)
        _, total, acc = merged_state(arrived, sums, stats, head, span, row >= 1, head_dim)
        done = (acc / total).astype(BF16).T
        out[pl.ds(part * shards, shards), :, lanes(head, head_dim)] = done.reshape(shards, length, head_dim)
        return carry

    lax.fori_loop(0, parts * near, one, 0)
    scatter_blocks(axis, out, outs)
    width = other.shape[2]
    result[:, :, 0:width] = other[...]
    cross_part(
        out, rows, starts, gain, order, mine, 0, row * group * length, result, head_dim, base=width
    )


def finish_kernel(dims, axis, order, cross, cont, *refs):
    group, slots, near, head_dim = dims
    far_out, near_out, (self_out, cross_out) = refs[:group], refs[group : 2 * group], refs[2 * group :]
    mine = lax.rem(lax.axis_index(axis), group)
    far = slots - near
    for k in range(group):
        first = jnp.bitwise_xor(mine, k) * slots
        for slot in range(slots):
            source, c = (near_out, slot) if slot < near else (far_out, slot - near)
            self_out[:, lanes(order[first + slot], head_dim)] = source[k][:, c * head_dim : (c + 1) * head_dim]
    factor = math.log2(math.e) / math.sqrt(head_dim)
    clen = cont.shape[1]
    row_index = lax.broadcasted_iota(jnp.int32, (clen, clen), 0)
    key_index = lax.broadcasted_iota(jnp.int32, (clen, clen), 1)
    visible = (key_index <= row_index) & (key_index // CLEN == row_index // CLEN)
    for g in range(group):
        for slot in range(slots):
            column = lanes(order[g * slots + slot], head_dim)
            base, c, heads = ((far + 1) * head_dim, slot, near) if slot < near else (0, slot - near, far)
            tail = base + heads * head_dim
            stats = cross[:, g, :, tail : tail + head_dim].astype(F32)
            k = 6 * c
            high = stats[:, :, k : k + 1] + stats[:, :, k + 1 : k + 2] + stats[:, :, k + 2 : k + 3]
            total = stats[:, :, k + 3 : k + 4] + stats[:, :, k + 4 : k + 5] + stats[:, :, k + 5 : k + 6]
            scores = jnp.where(visible, dot(cont[0, :, column], cont[1, :, column], (1, 1)), NEGATIVE)
            final = jnp.maximum(jnp.max(high, axis=0), jnp.max(scores, axis=1, keepdims=True))
            weight = jnp.exp2((high - final[None]) * factor)
            expo = jnp.exp2((scores - final) * factor)
            own = dot(expo.astype(BF16), cont[2, :, column], (1, 0))
            denominator = jnp.sum(weight * total, axis=0) + jnp.sum(expo, axis=1, keepdims=True)
            summed = cross[:, g, :, base + c * head_dim : base + (c + 1) * head_dim].astype(F32) * weight
            merged = jnp.sum(summed, axis=0) + own
            cross_out[:, column] = (merged / denominator).astype(BF16)


def per_device(self_qkv, windows, k_gain, cont_qkv, starts):
    axis = "ctx"
    length, features = self_qkv.shape[1:]
    head_count = windows.shape[0]
    head_dim = features // head_count
    devices = lax.axis_size(axis)
    group = WIN // (2 * length)
    slots = head_count // group
    near = slots // 2
    far = slots - near
    count = devices // group
    block = 2 * length
    rows_here = cont_qkv.shape[1]
    rows_all = rows_here * devices
    nearby, distant = near * head_dim, far * head_dim
    dims = (group, slots, near, head_dim)
    big = dims + (block,)
    index = jnp.arange(head_count, dtype=jnp.int32)
    above = (windows[None, :] > windows[:, None]) | (
        (windows[None, :] == windows[:, None]) & (index[None, :] < index[:, None])
    )
    rank = jnp.sum(above.astype(jnp.int32), axis=1)
    place = lax.rem(rank, group) * slots + rank // group
    order = jnp.sum(jnp.where(place[None, :] == index[:, None], index[None, :], 0), axis=1)

    def exchange(blocks):
        got = [blocks[0]]
        for k in range(1, group):
            got.append(lax.ppermute(blocks[k], axis, [(source, source ^ k) for source in range(devices)]))
        return got

    def gather(blocks, micros):
        return pl.pallas_call(
            functools.partial(gather_kernel, axis),
            out_shape=jax.ShapeDtypeStruct((group,) + blocks[0].shape, BF16),
            in_specs=[ANY] * group,
            out_specs=VMEM,
            scratch_shapes=[pltpu.SemaphoreType.DMA((group,))],
            cost_estimate=cost(micros),
        )(*blocks)

    def up(value):
        return lax.ppermute(value, axis, [(k, k + group) for k in range(devices - group)])

    def down(value):
        return lax.ppermute(value, axis, [(k + group, k) for k in range(devices - group)])

    def call(kernel, micros, shapes, *operands, smem=2, **more):
        return pl.pallas_call(
            kernel,
            out_shape=shapes,
            in_specs=[SMEM] * smem + [VMEM] * (len(operands) - smem),
            out_specs=jax.tree.map(lambda _: VMEM, shapes),
            cost_estimate=cost(micros),
            **more,
        )(*operands)

    def shape(*sizes, dtype=BF16):
        return jax.ShapeDtypeStruct(sizes, dtype)

    packed = pl.pallas_call(
        functools.partial(pack_kernel, dims, axis),
        grid=(3, 2),
        out_shape=(shape(2, length, distant),) * group
        + (shape(length, nearby),) * group
        + (shape(3, length, nearby),) * group,
        in_specs=[SMEM, pl.BlockSpec((1, length // 2, features), lambda i, j: (lax.rem(i + 1, 3), j, 0))],
        out_specs=(
            pl.BlockSpec(
                (1, length // 2, distant), lambda i, j: (jnp.minimum(i, 1), jnp.where(i < 2, j, 1), 0)
            ),
        )
        * group
        + (pl.BlockSpec((length // 2, nearby), lambda i, j: (jnp.where(i < 2, 0, j), 0)),) * group
        + (pl.BlockSpec((1, length // 2, nearby), lambda i, j: (i, j, 0)),) * group,
        name="pack",
        cost_estimate=cost(4),
    )(order, self_qkv)
    q_near0 = gather(exchange(packed[group : 2 * group]), 1)
    kv_far0 = gather(exchange(packed[:group]), 2)
    rest0 = gather(exchange(packed[2 * group :]), 2)
    rows_sent = call(
        functools.partial(pack_rows_kernel, dims), 2, shape(devices, rows_here, slots * head_dim), order,
        cont_qkv, smem=1,
    )
    rows = lax.all_to_all(rows_sent, axis, 0, 0, tiled=True)
    row_starts = jnp.broadcast_to(starts[:, None], (starts.shape[0], rows_all // starts.shape[0])).reshape(rows_all, 1)
    gain = k_gain.reshape(head_count, head_dim)

    kv_far1 = up(kv_far0)
    q_near1 = down(q_near0)
    kv_far2 = up(kv_far1)
    q_near2 = down(q_near1)

    state_scratch = [
        pltpu.VMEM((8, block), F32),
        pltpu.VMEM((8, block), F32),
        pltpu.VMEM((head_dim, block), F32),
    ]
    state_shape = shape(near, head_dim + 16, group * length)
    local_shape = (shape(near, head_dim, group * length, dtype=F32), shape(near, 8, group * length, dtype=F32))

    def near_step(delta, q):
        return call(
            functools.partial(near_kernel, big, axis, delta, count), 7,
            state_shape if delta == 2 else local_shape, order, windows, q, rest0, scratch_shapes=state_scratch,
        )

    def merge(kernel, micros, shapes, *operands, **more):
        return call(functools.partial(kernel, big, axis), micros, shapes, *operands, **more)

    state2 = up(near_step(2, q_near2))
    state1 = up(merge(merge_kernel, 1, state_shape, state2, *near_step(1, q_near1), smem=0))
    local0 = near_step(0, q_near0)

    *far_out, far_cross = pl.pallas_call(
        functools.partial(far_kernel, big, axis),
        out_shape=(shape(length, distant),) * group + (shape(devices, rows_here, distant + head_dim),),
        in_specs=[SMEM, SMEM, VMEM, ANY, ANY, ANY, VMEM, VMEM, VMEM],
        out_specs=(VMEM,) * (group + 1),
        scratch_shapes=[pltpu.VMEM((group, length, distant), BF16), pltpu.VMEM((3 * group, 2, length, distant), BF16)]
        + state_scratch
        + [pltpu.SemaphoreType.DMA((3,))],
        name="far",
        cost_estimate=cost(14),
    )(order, windows, rest0[:, 2], kv_far0, kv_far1, kv_far2, rows, row_starts, gain)
    far_back = exchange(far_out)
    *near_out, cross = merge(
        last_kernel, 4,
        (shape(length, nearby),) * group + (shape(devices, rows_here, distant + nearby + 2 * head_dim),),
        order, state1, *local0, rows, row_starts, gain, far_cross, smem=1,
        scratch_shapes=[pltpu.VMEM((group, length, nearby), BF16)],
    )
    near_back = exchange(near_out)
    cross = lax.all_to_all(cross, axis, 0, 0, tiled=True).reshape((count, group) + cross.shape[1:])
    return call(
        functools.partial(finish_kernel, dims, axis), 4, (shape(length, features), shape(rows_here, features)),
        order, cross, cont_qkv, *far_back, *near_back, smem=1,
    )


def solution(mesh):
    in_specs = (
        P(None, ("groups", "ctx"), None),
        P(),
        P(),
        P(None, ("groups", "ctx"), None),
        P("groups"),
    )
    out_specs = (P(("groups", "ctx"), None), P(("groups", "ctx"), None))

    return jax.shard_map(per_device, mesh=mesh, in_specs=in_specs, out_specs=out_specs, check_vma=False)
```

time: 856 us -> 172 us (0.20)
  blocking collectives: 301 us -> 0 us
  local copies, waits for them, and re-layouts: 179 us -> 8.51 us
  starting transfers between devices: 153 us -> 45.5 us
  matrix products: 71.8 us -> 0 us
  Pallas kernels: 0 us -> 57.2 us
  loops' own time: 35.4 us -> 0 us
  other arithmetic: 30.3 us -> 1.53 us
  waiting for transfers between devices: 83.7 us -> 57.1 us
    all_gather x1 -> x0, blocking collectives: 301 us -> none  [per_device(): gathered = lax.all_gather(cont_qkv[0], 'ctx', axis=0, tiled=True)]
    slice x35 -> x0, local copies, waits for them, and re-layouts: 135 us -> none  [the longest x16 130 us: one_head(): values = lax.dynamic_slice_in_dim(band[1], offset, head_dim, 1)]
    all_to_all x3 -> x2, starting transfers between devices: 124 us -> 15.4 us  [the longest x1 9.33 us: per_device(): lax.all_to_all(cross, axis, 0, 0, tiled=True)]
    dot_general x36 -> x0, matrix products: 71.8 us -> none  [the longest x16 39.7 us: one_head(): jnp.dot(weights, values, preferred_element_type=jnp.float32)]
    pallas_call x0 -> x12, Pallas kernels: none -> 57.2 us  [the longest x7 35.3 us: call(): pl.pallas_call(kernel, out_shape=shapes, in_specs=[SMEM] * smem + [VMEM]...]
    another operation x1 -> x0, loops' own time: 35.4 us -> none  [per_device(): attended = lax.map(one_head, jnp.arange(head_count, dtype=jnp.int32))]
    reduce_sum x21 -> x2, other arithmetic: 29.9 us -> 1.51 us  [the longest x1 0.91 us: per_device(): rank = jnp.sum(above.astype(jnp.int32), axis=1)]
    all_to_all x3 -> x2, waiting for transfers between devices: 20.3 us -> 0.01 us  [the longest x1 0.01 us: per_device(): lax.all_to_all(cross, axis, 0, 0, tiled=True)]
  transfers between devices with their start and end apart: 11 -> 23, of which waited for: 5 -> 11; matrix products, arithmetic and copies ran while one was open for 2% -> 2% of each run, Pallas kernels for 0% -> 25%
where the time goes in v1:
time: 172 us; the launch traced here: 171 us
  Pallas kernels  57.2 us (33%)
  waiting for transfers between devices  57.1 us (33%)
  starting transfers between devices  45.5 us (26%)
  local copies, waits for them, and re-layouts  8.51 us (5%)
    pallas_call x7, Pallas kernels, call(): pl.pallas_call(kernel, out_shape=shapes, in_specs=[SMEM] * smem + [VMEM]...  35.3 us
    ppermute x15, waiting for transfers between devices, exchange(): lax.ppermute(blocks[k], axis, [(source, source ^ k) for source in range(d...  31.3 us
    ppermute x4, waiting for transfers between devices, up(): lax.ppermute(value, axis, [(k, k + group) for k in range(devices - group)])  25.9 us
    ppermute x4, starting transfers between devices, up(): lax.ppermute(value, axis, [(k, k + group) for k in range(devices - group)])  15.7 us
    ppermute x15, starting transfers between devices, exchange(): lax.ppermute(blocks[k], axis, [(source, source ^ k) for source in range(d...  11.8 us
    pallas_call x1, Pallas kernels, per_device(): pl.pallas_call(functools.partial(far_kernel, big, axis), out_shape=(shape...  9.51 us
    all_to_all x1, starting transfers between devices, per_device(): lax.all_to_all(cross, axis, 0, 0, tiled=True)  9.33 us
    pallas_call x3, Pallas kernels, gather(): pl.pallas_call(functools.partial(gather_kernel, axis), out_shape=jax.Shap...  6.66 us
  transfers between devices with their start and end apart: 23, of which 11 were waited for; matrix products, arithmetic and copies ran while one was open for 2% of the time, Pallas kernels for 25%

profile of v1, /device:TPU:0, one launch (start us, length us, event | category | flops | bytes accessed | tf_op | source)
XLA Modules:
  0.0 170.7 jit_solution(11788928997815814974)
XLA Ops:
  2.2 5.7 %pack.1 = (bf16[2,256,256]{2,1,0:T(8,128)(2,1)}, bf16[2,256,256]{2,1,0:T(8,128)(2,1)}, bf16[2,256,256]{2,1,0:T(8,128)(2,1)}, bf16[2,256,256]{2,1,0:T(8,128)(2,1)...) custom-call(s32[16]{0:T(128)} %select_reduce_fusion.order, ...), custom_call_target="tpu_custom_call" | custom-call | flops 4600000000 | tf_op jit(solution)/shard_map/pack/pallas_call | solution.py:418
  8.5 2.9 %collective-permute-start.1 = (bf16[256,256]{1,0:T(8,128)(2,1)}, bf16[256,256]{1,0:T(8,128)(2,1)S(1)}, u32[]{:S(2)}, u32[]{:S(2)}) collective-permute-start(bf16[256,256]{1,0:T(8,128)(2,1)} %get-tuple-element.30), channel_id=1, source_target_pairs={{0,2},{1,3},{2,0},{3,1},{4,6},{5,7},{6,4},{7,5},{8,10},{9,11},{10,... | collective-permute-start | bytes 393224 | tf_op jit(solution)/shard_map/ppermute | solution.py:386
  11.6 2.0 %collective-permute-start.6 = (bf16[3,256,256]{2,1,0:T(8,128)(2,1)}, bf16[3,256,256]{2,1,0:T(8,128)(2,1)S(1)}, u32[]{:S(2)}, u32[]{:S(2)}) collective-permute-start(bf16[3,256,256]{2,1,0:T(8,128)(2,1)} %get-tuple-element.34), channel_id=1, source_target_pairs={{0,2},{1,3},{2,0},{3,1},{4,6},{5,7},{6,4},{7,5},{8,10},{9,11},{10,... | collective-permute-start | bytes 1179656 | tf_op jit(solution)/shard_map/ppermute | solution.py:386
  13.6 2.4 %collective-permute-done.1.refs_2_ = bf16[256,256]{1,0:T(8,128)(2,1)S(1)} collective-permute-done((bf16[256,256]{1,0:T(8,128)(2,1)}, bf16[256,256]{1,0:T(8,128)(2,1)S(1)}, u32[]{:S(2)}, u32[]{:S(2)}) %collective-permute-start.1) | collective-permute-done | bytes 131104 | tf_op jit(solution)/shard_map/ppermute | solution.py:386
  16.0 2.5 %collective-permute-done.2.refs_3_ = bf16[256,256]{1,0:T(8,128)(2,1)S(1)} collective-permute-done((bf16[256,256]{1,0:T(8,128)(2,1)}, bf16[256,256]{1,0:T(8,128)(2,1)S(1)}, u32[]{:S(2)}, u32[]{:S(2)}) %collective-permute-start.2) | collective-permute-done | bytes 131104 | tf_op jit(solution)/shard_map/ppermute | solution.py:386
  22.0 6.1 %all-to-all-start = ((bf16[16,8,512]{2,1,0:T(8,128)(2,1)}), bf16[16,8,512]{2,1,0:T(8,128)(2,1)S(1)}, u32[]{:S(2)}, u32[]{:S(2)}) async-start(bf16[16,8,512]{2,1,0:T(8,128)(2,1)} %shard_map.74), calls=%async_computation | async-start | bytes 262144 | tf_op jit(solution)/shard_map/all_to_all | solution.py:443
  28.9 1.9 %shard_map.68.q = bf16[4,256,256]{2,1,0:T(8,128)(2,1)} custom-call(bf16[256,256]{1,0:T(8,128)(2,1)} %get-tuple-element.28.refs_0_, bf16[256,256]{1,0:T(8,128)(2,1)} %copy-done.18, bf16[256,256]{1,0:T(8,128)(2,1)} %copy-done.20, bf16[256,256]{1,0:T(8,128)(2,1)} %copy-done.23), custom_call_target="tpu_custom_call" | custom-call | flops 1150000000 | tf_op jit(solution)/shard_map/pallas_call | solution.py:390
  30.8 11.6 %collective-permute-done.11.refs_2_ = bf16[2,256,256]{2,1,0:T(8,128)(2,1)S(1)} collective-permute-done((bf16[2,256,256]{2,1,0:T(8,128)(2,1)}, bf16[2,256,256]{2,1,0:T(8,128)(2,1)S(1)}, u32[]{:S(2)}, u32[]{:S(2)}) %collective-permute-start.11) | collective-permute-done | bytes 262176 | tf_op jit(solution)/shard_map/ppermute | solution.py:386
  43.6 3.3 %collective-permute-done.12.refs_3_ = bf16[2,256,256]{2,1,0:T(8,128)(2,1)S(1)} collective-permute-done((bf16[2,256,256]{2,1,0:T(8,128)(2,1)}, bf16[2,256,256]{2,1,0:T(8,128)(2,1)S(1)}, u32[]{:S(2)}, u32[]{:S(2)}) %collective-permute-start.12) | collective-permute-done | bytes 262176 | tf_op jit(solution)/shard_map/ppermute | solution.py:386
  47.6 2.2 %shard_map.75.kv0 = bf16[4,2,256,256]{3,2,1,0:T(8,128)(2,1)} custom-call(bf16[2,256,256]{2,1,0:T(8,128)(2,1)} %get-tuple-element.40.refs_0_, bf16[2,256,256]{2,1,0:T(8,128)(2,1)} %copy-done.12, bf16[2,256,256]{2,1,0:T(8,128)(2,1)} %copy-done.13, bf16[2,256,256]{2,1,0:T(8,128)(2,1)} %copy-done.14), custom_call_target="tpu_custom_call" | custom-call | flops 2300000000 | tf_op jit(solution)/shard_map/pallas_call | solution.py:390
  49.8 3.5 %collective-permute-start.13 = (bf16[4,2,256,256]{3,2,1,0:T(8,128)(2,1)}, bf16[4,2,256,256]{3,2,1,0:T(8,128)(2,1)S(1)}, u32[]{:S(2)}, u32[]{:S(2)}) collective-permute-start(bf16[4,2,256,256]{3,2,1,0:T(8,128)(2,1)} %shard_map.75.kv0), channel_id=1, source_target_pairs={{0,4},{1,5},{2,6},{3,7},{4,8},{5,9},{6,10},{7,11},{8,12},{9,13},{1... | collective-permute-start | bytes 3145736 | tf_op jit(solution)/shard_map/ppermute | solution.py:400
  54.4 2.6 %shard_map.69.kv = bf16[4,3,256,256]{3,2,1,0:T(8,128)(2,1)} custom-call(bf16[3,256,256]{2,1,0:T(8,128)(2,1)} %get-tuple-element.32.refs_0_, bf16[3,256,256]{2,1,0:T(8,128)(2,1)} %copy-done.9, bf16[3,256,256]{2,1,0:T(8,128)(2,1)} %copy-done.10, bf16[3,256,256]{2,1,0:T(8,128)(2,1)} %copy-done.11), custom_call_target="tpu_custom_call" | custom-call | flops 2300000000 | tf_op jit(solution)/shard_map/pallas_call | solution.py:390
  56.9 1.9 %slice_bitcast_fusion.q = bf16[4,256,256]{2,1,0:T(8,128)(2,1)} fusion(bf16[4,3,256,256]{3,2,1,0:T(8,128)(2,1)} %shard_map.69.kv), kind=kLoop, calls=%fused_computation | loop fusion | bytes 1048576 | tf_op jit(solution)/shard_map/squeeze | solution.py:483
  60.1 7.0 %shard_map.73 = (f32[2,128,1024]{2,1,0:T(8,128)}, f32[2,8,1024]{2,1,0:T(8,128)}) custom-call(s32[16]{0:T(128)} %select_reduce_fusion.order, s32[16]{0:T(128)} %windows.7, bf16[4,256,256]{2,1,0:T(8,128)(2,1)} %shard_map.68.q, bf16[4,3,256,256]{3,2,1,0:T(8,128)(2,1)} %shard_map.69.kv), custom_call_target="tpu_custom_call" | custom-call | flops 8049999872 | tf_op jit(solution)/shard_map/pallas_call | solution.py:406
  67.1 9.7 %collective-permute-done.13.kv1 = bf16[4,2,256,256]{3,2,1,0:T(8,128)(2,1)S(1)} collective-permute-done((bf16[4,2,256,256]{3,2,1,0:T(8,128)(2,1)}, bf16[4,2,256,256]{3,2,1,0:T(8,128)(2,1)S(1)}, u32[]{:S(2)}, u32[]{:S(2)}) %collective-permute-start.13) | collective-permute-done | bytes 1048608 | tf_op jit(solution)/shard_map/ppermute | solution.py:400
  76.9 4.3 %collective-permute-start.14 = (bf16[4,2,256,256]{3,2,1,0:T(8,128)(2,1)S(1)}, bf16[4,2,256,256]{3,2,1,0:T(8,128)(2,1)S(1)}, u32[]{:S(2)}, u32[]{:S(2)}) collective-permute-start(bf16[4,2,256,256]{3,2,1,0:T(8,128)(2,1)S(1)} %collective-permute-done.13.kv1), channel_id=1, source_target_pairs={{0,4},{1,5},{2,6},{3,7},{4,8},{5,9},{6,10},{7,11},{8,12},{9,13},{1... | collective-permute-start | bytes 3145736 | tf_op jit(solution)/shard_map/ppermute | solution.py:400
  82.0 7.3 %shard_map.70 = bf16[2,144,1024]{2,1,0:T(8,128)(2,1)} custom-call(s32[16]{0:T(128)} %select_reduce_fusion.order, s32[16]{0:T(128)} %windows.7, bf16[4,256,256]{2,1,0:T(8,128)(2,1)} %copy-done.8, bf16[4,3,256,256]{3,2,1,0:T(8,128)(2,1)} %shard_map.69.kv), custom_call_target="tpu_custom_call" | custom-call | flops 8049999872 | tf_op jit(solution)/shard_map/pallas_call | solution.py:406
  89.3 3.5 %collective-permute-start.8 = (bf16[2,144,1024]{2,1,0:T(8,128)(2,1)}, bf16[2,144,1024]{2,1,0:T(8,128)(2,1)S(1)}, u32[]{:S(2)}, u32[]{:S(2)}) collective-permute-start(bf16[2,144,1024]{2,1,0:T(8,128)(2,1)} %shard_map.70), channel_id=1, source_target_pairs={{0,4},{1,5},{2,6},{3,7},{4,8},{5,9},{6,10},{7,11},{8,12},{9,13},{1... | collective-permute-start | bytes 1769480 | tf_op jit(solution)/shard_map/ppermute | solution.py:400
  92.8 8.9 %shard_map.71 = (f32[2,128,1024]{2,1,0:T(8,128)}, f32[2,8,1024]{2,1,0:T(8,128)}) custom-call(s32[16]{0:T(128)} %select_reduce_fusion.order, s32[16]{0:T(128)} %windows.7, bf16[4,256,256]{2,1,0:T(8,128)(2,1)} %copy-done.7, bf16[4,3,256,256]{3,2,1,0:T(8,128)(2,1)} %shard_map.69.kv), custom_call_target="tpu_custom_call" | custom-call | flops 8049999872 | tf_op jit(solution)/shard_map/pallas_call | solution.py:406
  101.6 14.7 %collective-permute-done.8.arrived = bf16[2,144,1024]{2,1,0:T(8,128)(2,1)S(1)} collective-permute-done((bf16[2,144,1024]{2,1,0:T(8,128)(2,1)}, bf16[2,144,1024]{2,1,0:T(8,128)(2,1)S(1)}, u32[]{:S(2)}, u32[]{:S(2)}) %collective-permute-start.8) | collective-permute-done | bytes 589856 | tf_op jit(solution)/shard_map/ppermute | solution.py:400
  117.1 2.6 %shard_map.72 = bf16[2,144,1024]{2,1,0:T(8,128)(2,1)} custom-call(bf16[2,144,1024]{2,1,0:T(8,128)(2,1)} %copy-done.6, f32[2,128,1024]{2,1,0:T(8,128)} %get-tuple-element.36.sums, f32[2,8,1024]{2,1,0:T(8,128)} %get-tuple-element.37.stats), custom_call_target="tpu_custom_call" | custom-call | flops 1150000000 | tf_op jit(solution)/shard_map/pallas_call | solution.py:406
  119.7 4.3 %collective-permute-start.9 = (bf16[2,144,1024]{2,1,0:T(8,128)(2,1)}, bf16[2,144,1024]{2,1,0:T(8,128)(2,1)S(1)}, u32[]{:S(2)}, u32[]{:S(2)}) collective-permute-start(bf16[2,144,1024]{2,1,0:T(8,128)(2,1)} %shard_map.72), channel_id=1, source_target_pairs={{0,4},{1,5},{2,6},{3,7},{4,8},{5,9},{6,10},{7,11},{8,12},{9,13},{1... | collective-permute-start | bytes 1769480 | tf_op jit(solution)/shard_map/ppermute | solution.py:400
  125.1 9.5 %far.1 = (bf16[256,256]{1,0:T(8,128)(2,1)}, bf16[256,256]{1,0:T(8,128)(2,1)}, bf16[256,256]{1,0:T(8,128)(2,1)}, bf16[256,256]{1,0:T(8,128)(2,1)}, bf16[16,8,384]{2,1,0:T(8,128)(2,1)}) custom-call(s32[16]{0:T(128)} %select_reduce_fusion.order, s32[16]{0:T(128)} %windows.7, bf16[4,256,256]{2,1,0:T(8,128)(2,1)} %slice_bitcast_fusion.q, ...), custom_call_target="tpu_custom_call" | custom-call | flops 16099999744 | tf_op jit(solution)/shard_map/far/pallas_call | solution.py:473
  136.9 4.0 %shard_map.76 = (bf16[256,256]{1,0:T(8,128)(2,1)}, bf16[256,256]{1,0:T(8,128)(2,1)}, bf16[256,256]{1,0:T(8,128)(2,1)}, bf16[256,256]{1,0:T(8,128)(2,1)}, bf16[16,8,768]{2,1,0:T(8,128)(2,1)}) custom-call(s32[16]{0:T(128)} %select_reduce_fusion.order, bf16[2,144,1024]{2,1,0:T(8,128)(2,1)} %copy-done.5, f32[2,128,1024]{2,1,0:T(8,128)} %get-tuple-element.38.sums, ...), custom_call_target="tpu_custom_call" | custom-call | flops 4600000000 | tf_op jit(solution)/shard_map/pallas_call | solution.py:406
  140.9 9.3 %all-to-all-start.1 = ((bf16[16,8,768]{2,1,0:T(8,128)(2,1)}), bf16[16,8,768]{2,1,0:T(8,128)(2,1)S(1)}, u32[]{:S(2)}, u32[]{:S(2)}) async-start(bf16[16,8,768]{2,1,0:T(8,128)(2,1)} %get-tuple-element.45), calls=%async_computation.1 | async-start | bytes 393216 | tf_op jit(solution)/shard_map/all_to_all | solution.py:492
  150.7 1.6 collective-permute-start.16
  152.8 1.6 collective-permute-start.19
  154.5 4.2 %collective-permute-done.16.refs_2_ = bf16[256,256]{1,0:T(8,128)(2,1)S(1)} collective-permute-done((bf16[256,256]{1,0:T(8,128)(2,1)S(1)}, bf16[256,256]{1,0:T(8,128)(2,1)S(1)}, u32[]{:S(2)}, u32[]{:S(2)}) %collective-permute-start.16) | collective-permute-done | bytes 131104 | tf_op jit(solution)/shard_map/ppermute | solution.py:386
  158.6 1.8 %collective-permute-done.17.refs_3_ = bf16[256,256]{1,0:T(8,128)(2,1)S(1)} collective-permute-done((bf16[256,256]{1,0:T(8,128)(2,1)S(1)}, bf16[256,256]{1,0:T(8,128)(2,1)S(1)}, u32[]{:S(2)}, u32[]{:S(2)}) %collective-permute-start.17) | collective-permute-done | bytes 131104 | tf_op jit(solution)/shard_map/ppermute | solution.py:386
  160.5 3.9 %collective-permute-done.19.refs_6_ = bf16[256,256]{1,0:T(8,128)(2,1)S(1)} collective-permute-done((bf16[256,256]{1,0:T(8,128)(2,1)}, bf16[256,256]{1,0:T(8,128)(2,1)S(1)}, u32[]{:S(2)}, u32[]{:S(2)}) %collective-permute-start.19) | collective-permute-done | bytes 131104 | tf_op jit(solution)/shard_map/ppermute | solution.py:386
  164.4 1.7 collective-permute-done.20.refs_7_
  166.8 3.9 %shard_map.77 = (bf16[256,2048]{1,0:T(8,128)(2,1)}, bf16[8,2048]{1,0:T(8,128)(2,1)}) custom-call(s32[16]{0:T(128)} %select_reduce_fusion.order, bf16[4,4,8,768]{3,2,1,0:T(8,128)(2,1)} %bitcast.6, bf16[3,8,2048]{2,1,0:T(8,128)(2,1)} %cont.1, bf16[256,256]{1,0:T(8,128)(2,1)} %get-tuple-element.46.refs_0_, bf16[256,256]{1,0:T(8,128)(2,1)} %copy-done.16, ...), custom_call_target="tpu_custom_call" | custom-call | flops 4600000000 | tf_op jit(solution)/shard_map/pallas_call | solution.py:406
  (86 shorter events, 17.4 us)
Async XLA Ops:
  7.9 11.2 %collective-permute-start.10 = (bf16[2,256,256]{2,1,0:T(8,128)(2,1)}, bf16[2,256,256]{2,1,0:T(8,128)(2,1)S(1)}, u32[]{:S(2)}, u32[]{:S(2)}) collective-permute-start(bf16[2,256,256]{2,1,0:T(8,128)(2,1)} %get-tuple-element.41), channel_id=1, source_target_pairs={{0,1},{1,0},{2,3},{3,2},{4,5},{5,4},{6,7},{7,6},{8,9},{9,8},{10,11... | collective-permute-start | bytes 786440 | tf_op jit(solution)/shard_map/ppermute | solution.py:386
  8.5 3.1 %collective-permute-start = (bf16[256,256]{1,0:T(8,128)(2,1)}, bf16[256,256]{1,0:T(8,128)(2,1)S(1)}, u32[]{:S(2)}, u32[]{:S(2)}) collective-permute-start(bf16[256,256]{1,0:T(8,128)(2,1)} %get-tuple-element.29), channel_id=1, source_target_pairs={{0,1},{1,0},{2,3},{3,2},{4,5},{5,4},{6,7},{7,6},{8,9},{9,8},{10,11... | collective-permute-start | bytes 393224 | tf_op jit(solution)/shard_map/ppermute | solution.py:386
  8.5 7.5 %collective-permute-start.1 = (bf16[256,256]{1,0:T(8,128)(2,1)}, bf16[256,256]{1,0:T(8,128)(2,1)S(1)}, u32[]{:S(2)}, u32[]{:S(2)}) collective-permute-start(bf16[256,256]{1,0:T(8,128)(2,1)} %get-tuple-element.30), channel_id=1, source_target_pairs={{0,2},{1,3},{2,0},{3,1},{4,6},{5,7},{6,4},{7,5},{8,10},{9,11},{10,... | collective-permute-start | bytes 393224 | tf_op jit(solution)/shard_map/ppermute | solution.py:386
  11.4 7.0 %collective-permute-start.2 = (bf16[256,256]{1,0:T(8,128)(2,1)}, bf16[256,256]{1,0:T(8,128)(2,1)S(1)}, u32[]{:S(2)}, u32[]{:S(2)}) collective-permute-start(bf16[256,256]{1,0:T(8,128)(2,1)} %get-tuple-element.31), channel_id=1, source_target_pairs={{0,3},{1,2},{2,1},{3,0},{4,7},{5,6},{6,5},{7,4},{8,11},{9,10},{10,... | collective-permute-start | bytes 393224 | tf_op jit(solution)/shard_map/ppermute | solution.py:386
  11.4 41.9 %collective-permute-start.5 = (bf16[3,256,256]{2,1,0:T(8,128)(2,1)}, bf16[3,256,256]{2,1,0:T(8,128)(2,1)S(1)}, u32[]{:S(2)}, u32[]{:S(2)}) collective-permute-start(bf16[3,256,256]{2,1,0:T(8,128)(2,1)} %get-tuple-element.33), channel_id=1, source_target_pairs={{0,1},{1,0},{2,3},{3,2},{4,5},{5,4},{6,7},{7,6},{8,9},{9,8},{10,11... | collective-permute-start | bytes 1179656 | tf_op jit(solution)/shard_map/ppermute | solution.py:386
  11.6 10.4 %copy-start.18 = (bf16[256,256]{1,0:T(8,128)(2,1)}, bf16[256,256]{1,0:T(8,128)(2,1)S(1)}, u32[]{:S(2)}) copy-start(bf16[256,256]{1,0:T(8,128)(2,1)S(1)} %collective-permute-done.refs_1_) | copy-start | bytes 393220
  11.6 41.8 %collective-permute-start.6 = (bf16[3,256,256]{2,1,0:T(8,128)(2,1)}, bf16[3,256,256]{2,1,0:T(8,128)(2,1)S(1)}, u32[]{:S(2)}, u32[]{:S(2)}) collective-permute-start(bf16[3,256,256]{2,1,0:T(8,128)(2,1)} %get-tuple-element.34), channel_id=1, source_target_pairs={{0,2},{1,3},{2,0},{3,1},{4,6},{5,7},{6,4},{7,5},{8,10},{9,11},{10,... | collective-permute-start | bytes 1179656 | tf_op jit(solution)/shard_map/ppermute | solution.py:386
  16.0 37.4 %collective-permute-start.7 = (bf16[3,256,256]{2,1,0:T(8,128)(2,1)}, bf16[3,256,256]{2,1,0:T(8,128)(2,1)S(1)}, u32[]{:S(2)}, u32[]{:S(2)}) collective-permute-start(bf16[3,256,256]{2,1,0:T(8,128)(2,1)} %get-tuple-element.35), channel_id=1, source_target_pairs={{0,3},{1,2},{2,1},{3,0},{4,7},{5,6},{6,5},{7,4},{8,11},{9,10},{10,... | collective-permute-start | bytes 1179656 | tf_op jit(solution)/shard_map/ppermute | solution.py:386
  18.5 23.9 %collective-permute-start.11 = (bf16[2,256,256]{2,1,0:T(8,128)(2,1)}, bf16[2,256,256]{2,1,0:T(8,128)(2,1)S(1)}, u32[]{:S(2)}, u32[]{:S(2)}) collective-permute-start(bf16[2,256,256]{2,1,0:T(8,128)(2,1)} %get-tuple-element.42), channel_id=1, source_target_pairs={{0,2},{1,3},{2,0},{3,1},{4,6},{5,7},{6,4},{7,5},{8,10},{9,11},{10,... | collective-permute-start | bytes 786440 | tf_op jit(solution)/shard_map/ppermute | solution.py:386
  19.1 9.0 %copy-start.2 = (s32[16]{0:T(128)S(1)}, s32[16]{0:T(128)}, u32[]{:S(2)}) copy-start(s32[16]{0:T(128)} %param.9) | copy-start | bytes 196
  19.1 27.8 %collective-permute-start.12 = (bf16[2,256,256]{2,1,0:T(8,128)(2,1)}, bf16[2,256,256]{2,1,0:T(8,128)(2,1)S(1)}, u32[]{:S(2)}, u32[]{:S(2)}) collective-permute-start(bf16[2,256,256]{2,1,0:T(8,128)(2,1)} %get-tuple-element.43), channel_id=1, source_target_pairs={{0,3},{1,2},{2,1},{3,0},{4,7},{5,6},{6,5},{7,4},{8,11},{9,10},{10,... | collective-permute-start | bytes 786440 | tf_op jit(solution)/shard_map/ppermute | solution.py:386
  22.0 102.1 %all-to-all-start = ((bf16[16,8,512]{2,1,0:T(8,128)(2,1)}), bf16[16,8,512]{2,1,0:T(8,128)(2,1)S(1)}, u32[]{:S(2)}, u32[]{:S(2)}) async-start(bf16[16,8,512]{2,1,0:T(8,128)(2,1)} %shard_map.74), calls=%async_computation | async-start | bytes 262144 | tf_op jit(solution)/shard_map/all_to_all | solution.py:443
  42.3 16.5 %collective-permute-start.3 = (bf16[4,256,256]{2,1,0:T(8,128)(2,1)}, bf16[4,256,256]{2,1,0:T(8,128)(2,1)S(1)}, u32[]{:S(2)}, u32[]{:S(2)}) collective-permute-start(bf16[4,256,256]{2,1,0:T(8,128)(2,1)} %shard_map.68.q), channel_id=1, source_target_pairs={{4,0},{5,1},{6,2},{7,3},{8,4},{9,5},{10,6},{11,7},{12,8},{13,9},{1... | collective-permute-start | bytes 1572872 | tf_op jit(solution)/shard_map/ppermute | solution.py:403
  49.8 27.1 %collective-permute-start.13 = (bf16[4,2,256,256]{3,2,1,0:T(8,128)(2,1)}, bf16[4,2,256,256]{3,2,1,0:T(8,128)(2,1)S(1)}, u32[]{:S(2)}, u32[]{:S(2)}) collective-permute-start(bf16[4,2,256,256]{3,2,1,0:T(8,128)(2,1)} %shard_map.75.kv0), channel_id=1, source_target_pairs={{0,4},{1,5},{2,6},{3,7},{4,8},{5,9},{6,10},{7,11},{8,12},{9,13},{1... | collective-permute-start | bytes 3145736 | tf_op jit(solution)/shard_map/ppermute | solution.py:400
  58.8 8.3 %copy-start.7 = (bf16[4,256,256]{2,1,0:T(8,128)(2,1)}, bf16[4,256,256]{2,1,0:T(8,128)(2,1)S(1)}, u32[]{:S(2)}) copy-start(bf16[4,256,256]{2,1,0:T(8,128)(2,1)S(1)} %collective-permute-done.3.q) | copy-start | bytes 1572868
  58.9 22.4 %collective-permute-start.4 = (bf16[4,256,256]{2,1,0:T(8,128)(2,1)S(1)}, bf16[4,256,256]{2,1,0:T(8,128)(2,1)S(1)}, u32[]{:S(2)}, u32[]{:S(2)}) collective-permute-start(bf16[4,256,256]{2,1,0:T(8,128)(2,1)S(1)} %collective-permute-done.3.q), channel_id=1, source_target_pairs={{4,0},{5,1},{6,2},{7,3},{8,4},{9,5},{10,6},{11,7},{12,8},{13,9},{1... | collective-permute-start | bytes 1572872 | tf_op jit(solution)/shard_map/ppermute | solution.py:403
  76.9 12.4 %copy-start.3 = (bf16[4,2,256,256]{3,2,1,0:T(8,128)(2,1)}, bf16[4,2,256,256]{3,2,1,0:T(8,128)(2,1)S(1)}, u32[]{:S(2)}) copy-start(bf16[4,2,256,256]{3,2,1,0:T(8,128)(2,1)S(1)} %collective-permute-done.13.kv1) | copy-start | bytes 3145732
  76.9 47.2 %collective-permute-start.14 = (bf16[4,2,256,256]{3,2,1,0:T(8,128)(2,1)S(1)}, bf16[4,2,256,256]{3,2,1,0:T(8,128)(2,1)S(1)}, u32[]{:S(2)}, u32[]{:S(2)}) collective-permute-start(bf16[4,2,256,256]{3,2,1,0:T(8,128)(2,1)S(1)} %collective-permute-done.13.kv1), channel_id=1, source_target_pairs={{0,4},{1,5},{2,6},{3,7},{4,8},{5,9},{6,10},{7,11},{8,12},{9,13},{1... | collective-permute-start | bytes 3145736 | tf_op jit(solution)/shard_map/ppermute | solution.py:400
  89.3 27.0 %collective-permute-start.8 = (bf16[2,144,1024]{2,1,0:T(8,128)(2,1)}, bf16[2,144,1024]{2,1,0:T(8,128)(2,1)S(1)}, u32[]{:S(2)}, u32[]{:S(2)}) collective-permute-start(bf16[2,144,1024]{2,1,0:T(8,128)(2,1)} %shard_map.70), channel_id=1, source_target_pairs={{0,4},{1,5},{2,6},{3,7},{4,8},{5,9},{6,10},{7,11},{8,12},{9,13},{1... | collective-permute-start | bytes 1769480 | tf_op jit(solution)/shard_map/ppermute | solution.py:400
  119.7 16.3 %collective-permute-start.9 = (bf16[2,144,1024]{2,1,0:T(8,128)(2,1)}, bf16[2,144,1024]{2,1,0:T(8,128)(2,1)S(1)}, u32[]{:S(2)}, u32[]{:S(2)}) collective-permute-start(bf16[2,144,1024]{2,1,0:T(8,128)(2,1)} %shard_map.72), channel_id=1, source_target_pairs={{0,4},{1,5},{2,6},{3,7},{4,8},{5,9},{6,10},{7,11},{8,12},{9,13},{1... | collective-permute-start | bytes 1769480 | tf_op jit(solution)/shard_map/ppermute | solution.py:400
  136.8 13.4 %copy-start.22 = (bf16[256,256]{1,0:T(8,128)(2,1)S(1)}, bf16[256,256]{1,0:T(8,128)(2,1)}, u32[]{:S(2)}) copy-start(bf16[256,256]{1,0:T(8,128)(2,1)} %get-tuple-element.47) | copy-start | bytes 393220
  136.8 13.8 %copy-start.17 = (bf16[256,256]{1,0:T(8,128)(2,1)S(1)}, bf16[256,256]{1,0:T(8,128)(2,1)}, u32[]{:S(2)}) copy-start(bf16[256,256]{1,0:T(8,128)(2,1)} %get-tuple-element.48) | copy-start | bytes 393220
  136.9 15.5 %copy-start.15 = (bf16[256,256]{1,0:T(8,128)(2,1)S(1)}, bf16[256,256]{1,0:T(8,128)(2,1)}, u32[]{:S(2)}) copy-start(bf16[256,256]{1,0:T(8,128)(2,1)} %get-tuple-element.49) | copy-start | bytes 393220
  140.9 25.2 %all-to-all-start.1 = ((bf16[16,8,768]{2,1,0:T(8,128)(2,1)}), bf16[16,8,768]{2,1,0:T(8,128)(2,1)S(1)}, u32[]{:S(2)}, u32[]{:S(2)}) async-start(bf16[16,8,768]{2,1,0:T(8,128)(2,1)} %get-tuple-element.45), calls=%async_computation.1 | async-start | bytes 393216 | tf_op jit(solution)/shard_map/all_to_all | solution.py:492
  150.2 4.3 %collective-permute-start.15 = (bf16[256,256]{1,0:T(8,128)(2,1)S(1)}, bf16[256,256]{1,0:T(8,128)(2,1)S(1)}, u32[]{:S(2)}, u32[]{:S(2)}) collective-permute-start(bf16[256,256]{1,0:T(8,128)(2,1)S(1)} %copy-done.22), channel_id=1, source_target_pairs={{0,1},{1,0},{2,3},{3,2},{4,5},{5,4},{6,7},{7,6},{8,9},{9,8},{10,11... | collective-permute-start | bytes 393224 | tf_op jit(solution)/shard_map/ppermute | solution.py:386
  150.7 8.0 %collective-permute-start.16 = (bf16[256,256]{1,0:T(8,128)(2,1)S(1)}, bf16[256,256]{1,0:T(8,128)(2,1)S(1)}, u32[]{:S(2)}, u32[]{:S(2)}) collective-permute-start(bf16[256,256]{1,0:T(8,128)(2,1)S(1)} %copy-done.17), channel_id=1, source_target_pairs={{0,2},{1,3},{2,0},{3,1},{4,6},{5,7},{6,4},{7,5},{8,10},{9,11},{10,... | collective-permute-start | bytes 393224 | tf_op jit(solution)/shard_map/ppermute | solution.py:386
  152.3 8.1 %collective-permute-start.17 = (bf16[256,256]{1,0:T(8,128)(2,1)S(1)}, bf16[256,256]{1,0:T(8,128)(2,1)S(1)}, u32[]{:S(2)}, u32[]{:S(2)}) collective-permute-start(bf16[256,256]{1,0:T(8,128)(2,1)S(1)} %copy-done.15), channel_id=1, source_target_pairs={{0,3},{1,2},{2,1},{3,0},{4,7},{5,6},{6,5},{7,4},{8,11},{9,10},{10,... | collective-permute-start | bytes 393224 | tf_op jit(solution)/shard_map/ppermute | solution.py:386
  152.4 8.1 %collective-permute-start.18 = (bf16[256,256]{1,0:T(8,128)(2,1)}, bf16[256,256]{1,0:T(8,128)(2,1)S(1)}, u32[]{:S(2)}, u32[]{:S(2)}) collective-permute-start(bf16[256,256]{1,0:T(8,128)(2,1)} %get-tuple-element.51), channel_id=1, source_target_pairs={{0,1},{1,0},{2,3},{3,2},{4,5},{5,4},{6,7},{7,6},{8,9},{9,8},{10,11... | collective-permute-start | bytes 393224 | tf_op jit(solution)/shard_map/ppermute | solution.py:386
  152.8 11.6 %collective-permute-start.19 = (bf16[256,256]{1,0:T(8,128)(2,1)}, bf16[256,256]{1,0:T(8,128)(2,1)S(1)}, u32[]{:S(2)}, u32[]{:S(2)}) collective-permute-start(bf16[256,256]{1,0:T(8,128)(2,1)} %get-tuple-element.52), channel_id=1, source_target_pairs={{0,2},{1,3},{2,0},{3,1},{4,6},{5,7},{6,4},{7,5},{8,10},{9,11},{10,... | collective-permute-start | bytes 393224 | tf_op jit(solution)/shard_map/ppermute | solution.py:386
  154.5 11.6 %copy-start.16 = (bf16[256,256]{1,0:T(8,128)(2,1)}, bf16[256,256]{1,0:T(8,128)(2,1)S(1)}, u32[]{:S(2)}) copy-start(bf16[256,256]{1,0:T(8,128)(2,1)S(1)} %collective-permute-done.15.refs_1_) | copy-start | bytes 393220
  154.5 11.6 %collective-permute-start.20 = (bf16[256,256]{1,0:T(8,128)(2,1)}, bf16[256,256]{1,0:T(8,128)(2,1)S(1)}, u32[]{:S(2)}, u32[]{:S(2)}) collective-permute-start(bf16[256,256]{1,0:T(8,128)(2,1)} %get-tuple-element.53), channel_id=1, source_target_pairs={{0,3},{1,2},{2,1},{3,0},{4,7},{5,6},{6,5},{7,4},{8,11},{9,10},{10,... | collective-permute-start | bytes 393224 | tf_op jit(solution)/shard_map/ppermute | solution.py:386
  158.6 7.4 %copy-start.19 = (bf16[256,256]{1,0:T(8,128)(2,1)}, bf16[256,256]{1,0:T(8,128)(2,1)S(1)}, u32[]{:S(2)}) copy-start(bf16[256,256]{1,0:T(8,128)(2,1)S(1)} %collective-permute-done.16.refs_2_) | copy-start | bytes 393220
  (18 other events, 38.7 us)

commit v2 on v1

--- a/solution.py
+++ b/solution.py
@@ -90,34 +90,35 @@
             ]
 
 
-def attend(kv, queries, window, head, part, base, high_limit, key_parts, state, block, head_dim):
+def attend(kv, queries, windows, part, base, high_limit, key_parts, state, block, head_dim):
     peak, total, acc = state
     shards = block // kv.shape[2]
     factor = math.log2(math.e) / math.sqrt(head_dim)
-    column = lanes(head, head_dim)
     row_index = lax.broadcasted_iota(jnp.int32, (block, block), 1)
     key_index = lax.broadcasted_iota(jnp.int32, (block, block), 0)
 
     def step(distance, diagonal):
         spot = pl.ds((base + part - distance) * shards, shards)
-        keys = kv[spot, 0, :, column].reshape(block, head_dim)
-        values = kv[spot, 1, :, column].reshape(block, head_dim)
-        q = queries[pl.ds(part * shards, shards), :, column].reshape(block, head_dim)
-        scores = dot(keys, q, (1, 1))
-        gap = row_index - key_index
-        visible = gap < window - distance * block
-        if diagonal:
-            visible = visible & (gap >= 0)
-        scores = jnp.where(visible, scores, NEGATIVE)
-        old = peak[0:1, :]
-        new = jnp.maximum(old, jnp.max(scores, axis=0, keepdims=True))
-        fade = jnp.exp2((old - new) * factor)
-        expo = jnp.exp2((scores - new) * factor)
-        total[0:1, :] = total[0:1, :] * fade + jnp.sum(expo, axis=0, keepdims=True)
-        peak[0:1, :] = new
-        acc[...] = acc[...] * fade + dot(values, expo.astype(BF16), (0, 0))
-
-    reach = jnp.minimum((window + block - 2) // block, high_limit)
+        for head, window in enumerate(windows):
+            column = slice(head * head_dim, (head + 1) * head_dim)
+            keys = kv[spot, 0, :, column].reshape(block, head_dim)
+            values = kv[spot, 1, :, column].reshape(block, head_dim)
+            q = queries(part * shards, shards, column).reshape(block, head_dim)
+            scores = dot(keys, q, (1, 1))
+            visible = row_index < key_index + (window - distance * block)
+            if diagonal:
+                visible = visible & (row_index >= key_index)
+            scores = jnp.where(visible, scores, NEGATIVE)
+            old = peak[head, 0:1, :]
+            new = jnp.maximum(old, jnp.max(scores, axis=0, keepdims=True))
+            fade = jnp.exp2((old - new) * factor)
+            expo = jnp.exp2((scores - new) * factor)
+            total[head, 0:1, :] = total[head, 0:1, :] * fade + jnp.sum(expo, axis=0, keepdims=True)
+            peak[head, 0:1, :] = new
+            acc[head] = acc[head] * fade + dot(values, expo.astype(BF16), (0, 0))
+
+    longest = functools.reduce(jnp.maximum, windows)
+    reach = jnp.minimum((longest + block - 2) // block, high_limit)
     low = jnp.maximum(base + part - (key_parts - 1), 0)
 
     if base - (key_parts - 1) <= 0:
@@ -188,16 +189,16 @@
     acc[...] = jnp.zeros(acc.shape, F32)
 
 
-def far_kernel(dims, axis, order, windows, q, kv0, kv1, kv2, rows, starts, gain, *refs):
+def far_kernel(dims, axis, order, windows, rest, kv0, kv1, kv2, kv3, rows, starts, gain, *refs):
     group, slots, near, head_dim, block = dims
     outs, (result, out, kv, peak, total, acc, sems) = refs[:group], refs[group:]
     device = lax.axis_index(axis)
     row = device // group
     mine = lax.rem(device, group) * slots + near
-    copies = [
-        pltpu.make_async_copy(source, kv.at[pl.ds(k * group, group)], sems.at[k])
-        for k, source in enumerate((kv2, kv1, kv0))
-    ]
+    copies, start = [], 0
+    for k, source in enumerate((kv3, kv2, kv1, kv0)):
+        copies.append(pltpu.make_async_copy(source, kv.at[pl.ds(start, source.shape[0])], sems.at[k]))
+        start += source.shape[0]
     for copy in copies:
         copy.start()
     for copy in copies:
@@ -206,19 +207,22 @@
     parts = group * length // block
     shards = block // length
 
-    def one(index, carry):
-        head = index // parts
-        part = lax.rem(index, parts)
-        window = windows[order[mine + head]]
+    heads = slots - near
+    spans = [windows[order[mine + head]] for head in range(heads)]
+
+    def pick(start, size, column):
+        return rest[pl.ds(start, size), 2, :, column]
+
+    def one(part, carry):
         reset(peak, total, acc)
-        attend(
-            kv, q, window, head, part, 2 * parts, row * parts + part, 3 * parts, (peak, total, acc), block, head_dim
-        )
-        done = (acc[...] / total[0:1, :]).astype(BF16).T
-        out[pl.ds(part * shards, shards), :, lanes(head, head_dim)] = done.reshape(shards, length, head_dim)
+        attend(kv, pick, spans, part, 2 * parts, row * parts + part, 3 * parts, (peak, total, acc), block, head_dim)
+        for head in range(heads):
+            done = (acc[head] / total[head, 0:1, :]).astype(BF16).T
+            column = slice(head * head_dim, (head + 1) * head_dim)
+            out[pl.ds(part * shards, shards), :, column] = done.reshape(shards, length, head_dim)
         return carry
 
-    lax.fori_loop(0, parts * (slots - near), one, 0)
+    lax.fori_loop(0, parts, one, 0)
     scatter_blocks(axis, out, outs)
     cross_part(out, rows, starts, gain, order, mine, near * head_dim, row * group * length, result, head_dim)
 
@@ -235,23 +239,26 @@
     else:
         sums, stats_out, peak, total, acc = refs
 
-    def one(index, carry):
-        head = index // parts
-        part = lax.rem(index, parts)
-        window = windows[order[mine + head]]
+    spans = [windows[order[mine + head]] for head in range(near)]
+
+    def pick(start, size, column):
+        return q[pl.ds(start, size), :, column]
+
+    def one(part, carry):
         span = pl.ds(pl.multiple_of(part * block, block), block)
         reset(peak, total, acc)
         limit = jnp.where(row + delta < count, 2 * WIN, -1) if delta > 0 else 2 * WIN
-        attend(kv, q, window, head, part, delta * parts, limit, parts, (peak, total, acc), block, head_dim)
-        if delta == 2:
-            write_state(state, head, span, peak[0:1, :], total[0:1, :], acc[...], head_dim)
-        else:
-            sums[head, :, span] = acc[...]
-            stats_out[head, 0:1, span] = peak[0:1, :]
-            stats_out[head, 1:2, span] = total[0:1, :]
+        attend(kv, pick, spans, part, delta * parts, limit, parts, (peak, total, acc), block, head_dim)
+        for head in range(near):
+            if delta == 2:
+                write_state(state, head, span, peak[head, 0:1, :], total[head, 0:1, :], acc[head], head_dim)
+            else:
+                sums[head, :, span] = acc[head]
+                stats_out[head, 0:1, span] = peak[head, 0:1, :]
+                stats_out[head, 1:2, span] = total[head, 0:1, :]
         return carry
 
-    lax.fori_loop(0, parts * near, one, 0)
+    lax.fori_loop(0, parts, one, 0)
 
 
 def write_state(state, head, span, peak, total, acc, head_dim):
@@ -446,13 +453,16 @@
 
     kv_far1 = up(kv_far0)
     q_near1 = down(q_near0)
-    kv_far2 = up(kv_far1)
+    half = group // 2
+    kv_far2 = up(kv_far1[half:])
+    deep = jnp.sum((windows > (group + group - half) * length + 1).astype(jnp.int32)) > group * near
+    kv_far3 = lax.cond(deep, lambda value: up(value), lambda value: value, kv_far1[:half])
     q_near2 = down(q_near1)
 
     state_scratch = [
-        pltpu.VMEM((8, block), F32),
-        pltpu.VMEM((8, block), F32),
-        pltpu.VMEM((head_dim, block), F32),
+        pltpu.VMEM((far, 8, block), F32),
+        pltpu.VMEM((far, 8, block), F32),
+        pltpu.VMEM((far, head_dim, block), F32),
     ]
     state_shape = shape(near, head_dim + 16, group * length)
     local_shape = (shape(near, head_dim, group * length, dtype=F32), shape(near, 8, group * length, dtype=F32))
@@ -473,14 +483,14 @@
     *far_out, far_cross = pl.pallas_call(
         functools.partial(far_kernel, big, axis),
         out_shape=(shape(length, distant),) * group + (shape(devices, rows_here, distant + head_dim),),
-        in_specs=[SMEM, SMEM, VMEM, ANY, ANY, ANY, VMEM, VMEM, VMEM],
+        in_specs=[SMEM, SMEM, VMEM, ANY, ANY, ANY, ANY, VMEM, VMEM, VMEM],
         out_specs=(VMEM,) * (group + 1),
         scratch_shapes=[pltpu.VMEM((group, length, distant), BF16), pltpu.VMEM((3 * group, 2, length, distant), BF16)]
         + state_scratch
-        + [pltpu.SemaphoreType.DMA((3,))],
+        + [pltpu.SemaphoreType.DMA((4,))],
         name="far",
         cost_estimate=cost(14),
-    )(order, windows, rest0[:, 2], kv_far0, kv_far1, kv_far2, rows, row_starts, gain)
+    )(order, windows, rest0, kv_far0, kv_far1, kv_far2, kv_far3, rows, row_starts, gain)
     far_back = exchange(far_out)
     *near_out, cross = merge(
         last_kernel, 4,
@@ -489,7 +499,8 @@
         scratch_shapes=[pltpu.VMEM((group, length, nearby), BF16)],
     )
     near_back = exchange(near_out)
-    cross = lax.all_to_all(cross, axis, 0, 0, tiled=True).reshape((count, group) + cross.shape[1:])
+    cross = lax.all_to_all(cross, axis, 0, 0, tiled=True)
+    cross = cross.reshape((count, group) + cross.shape[1:])
     return call(
         functools.partial(finish_kernel, dims, axis), 4, (shape(length, features), shape(rows_here, features)),
         order, cross, cont_qkv, *far_back, *near_back, smem=1,

time: 172 us -> 151 us (0.88)
  waiting for transfers between devices: 57.1 us -> 42.5 us
  Pallas kernels: 57.2 us -> 54.1 us
  local copies, waits for them, and re-layouts: 8.51 us -> 5.5 us
    ppermute x4, waiting for transfers between devices: 25.9 us -> 8.69 us  [up(): lax.ppermute(value, axis, [(k, k + group) for k in range(devices - group)])]
    ppermute x2, waiting for transfers between devices: 0.01 us -> 8.71 us  [down(): lax.ppermute(value, axis, [(k + group, k) for k in range(devices - group)])]
    ppermute x15, waiting for transfers between devices: 31.3 us -> 25.1 us  [exchange(): lax.ppermute(blocks[k], axis, [(source, source ^ k) for source in range(d...]
    pallas_call x7, Pallas kernels: 35.3 us -> 32.7 us  [call(): pl.pallas_call(kernel, out_shape=shapes, in_specs=[SMEM] * smem + [VMEM]...]
    squeeze x1 -> x0, local copies, waits for them, and re-layouts: 1.9 us -> none  [per_device(): rest0[:, 2]]
    unnamed x54 -> x58, local copies, waits for them, and re-layouts: 5.84 us -> 4.66 us
  transfers between devices with their start and end apart: 23 -> 23, of which waited for: 11 -> 11; matrix products, arithmetic and copies ran while one was open for 2% -> 1% of each run, Pallas kernels for 25% -> 27%
where the time goes in v2:
time: 151 us; the launch traced here: 150 us
  Pallas kernels  54.1 us (36%)
  starting transfers between devices  44.3 us (29%)
  waiting for transfers between devices  42.5 us (28%)
  local copies, waits for them, and re-layouts  5.5 us (4%)
  other arithmetic  2.27 us (2%)
  between operations  1.6 us (1%)
    pallas_call x7, Pallas kernels, call(): pl.pallas_call(kernel, out_shape=shapes, in_specs=[SMEM] * smem + [VMEM]...  32.7 us
    ppermute x15, waiting for transfers between devices, exchange(): lax.ppermute(blocks[k], axis, [(source, source ^ k) for source in range(d...  25.1 us
    ppermute x4, starting transfers between devices, up(): lax.ppermute(value, axis, [(k, k + group) for k in range(devices - group)])  14.7 us
    ppermute x15, starting transfers between devices, exchange(): lax.ppermute(blocks[k], axis, [(source, source ^ k) for source in range(d...  11.5 us
    all_to_all x1, starting transfers between devices, per_device(): cross = lax.all_to_all(cross, axis, 0, 0, tiled=True)  9.28 us
    pallas_call x1, Pallas kernels, per_device(): pl.pallas_call(functools.partial(far_kernel, big, axis), out_shape=(shape...  9.05 us
    ppermute x2, waiting for transfers between devices, down(): lax.ppermute(value, axis, [(k + group, k) for k in range(devices - group)])  8.71 us
    ppermute x4, waiting for transfers between devices, up(): lax.ppermute(value, axis, [(k, k + group) for k in range(devices - group)])  8.69 us
  transfers between devices with their start and end apart: 23, of which 11 were waited for; matrix products, arithmetic and copies ran while one was open for 1% of the time, Pallas kernels for 27%

profile of v2, /device:TPU:0, one launch (start us, length us, event | category | flops | bytes accessed | tf_op | source)
XLA Modules:
  0.0 150.4 jit_solution(15277423841248754780)
XLA Ops:
  2.3 5.7 %pack.1 = (bf16[2,256,256]{2,1,0:T(8,128)(2,1)}, bf16[2,256,256]{2,1,0:T(8,128)(2,1)}, bf16[2,256,256]{2,1,0:T(8,128)(2,1)}, bf16[2,256,256]{2,1,0:T(8,128)(2,1)...) custom-call(s32[16]{0:T(128)} %select_reduce_fusion.order, ...), custom_call_target="tpu_custom_call" | custom-call | flops 4600000000 | tf_op jit(solution)/shard_map/pack/pallas_call | solution.py:425
  8.6 2.9 %collective-permute-start.12 = (bf16[2,256,256]{2,1,0:T(8,128)(2,1)}, bf16[2,256,256]{2,1,0:T(8,128)(2,1)S(1)}, u32[]{:S(2)}, u32[]{:S(2)}) collective-permute-start(bf16[2,256,256]{2,1,0:T(8,128)(2,1)} %get-tuple-element.47), channel_id=1, source_target_pairs={{0,2},{1,3},{2,0},{3,1},{4,6},{5,7},{6,4},{7,5},{8,10},{9,11},{10,... | collective-permute-start | bytes 786440 | tf_op jit(solution)/shard_map/ppermute | solution.py:393
  11.5 1.4 collective-permute-start.2
  13.4 1.6 %shard_map.74 = bf16[16,8,512]{2,1,0:T(8,128)(2,1)} custom-call(s32[16]{0:T(128)} %select_reduce_fusion.order, bf16[3,8,2048]{2,1,0:T(8,128)(2,1)} %cont.1), custom_call_target="tpu_custom_call" | custom-call | flops 2300000000 | tf_op jit(solution)/shard_map/pallas_call | solution.py:413
  15.0 6.3 %all-to-all-start = ((bf16[16,8,512]{2,1,0:T(8,128)(2,1)}), bf16[16,8,512]{2,1,0:T(8,128)(2,1)S(1)}, u32[]{:S(2)}, u32[]{:S(2)}) async-start(bf16[16,8,512]{2,1,0:T(8,128)(2,1)} %shard_map.74), calls=%async_computation | async-start | bytes 262144 | tf_op jit(solution)/shard_map/all_to_all | solution.py:450
  21.3 6.8 %collective-permute-done.2.refs_2_ = bf16[256,256]{1,0:T(8,128)(2,1)S(1)} collective-permute-done((bf16[256,256]{1,0:T(8,128)(2,1)}, bf16[256,256]{1,0:T(8,128)(2,1)S(1)}, u32[]{:S(2)}, u32[]{:S(2)}) %collective-permute-start.2) | collective-permute-done | bytes 131104 | tf_op jit(solution)/shard_map/ppermute | solution.py:393
  28.1 2.1 %collective-permute-done.3.refs_3_ = bf16[256,256]{1,0:T(8,128)(2,1)S(1)} collective-permute-done((bf16[256,256]{1,0:T(8,128)(2,1)}, bf16[256,256]{1,0:T(8,128)(2,1)S(1)}, u32[]{:S(2)}, u32[]{:S(2)}) %collective-permute-start.3) | collective-permute-done | bytes 131104 | tf_op jit(solution)/shard_map/ppermute | solution.py:393
  32.0 1.9 %shard_map.68.q = bf16[4,256,256]{2,1,0:T(8,128)(2,1)} custom-call(bf16[256,256]{1,0:T(8,128)(2,1)} %get-tuple-element.33.refs_0_, bf16[256,256]{1,0:T(8,128)(2,1)} %copy-done.19, bf16[256,256]{1,0:T(8,128)(2,1)} %copy-done.25, bf16[256,256]{1,0:T(8,128)(2,1)} %copy-done.27), custom_call_target="tpu_custom_call" | custom-call | flops 1150000000 | tf_op jit(solution)/shard_map/pallas_call | solution.py:397
  38.1 2.2 %shard_map.75.kv0 = bf16[4,2,256,256]{3,2,1,0:T(8,128)(2,1)} custom-call(bf16[2,256,256]{2,1,0:T(8,128)(2,1)} %get-tuple-element.45.refs_0_, bf16[2,256,256]{2,1,0:T(8,128)(2,1)} %copy-done.13, bf16[2,256,256]{2,1,0:T(8,128)(2,1)} %copy-done.14, bf16[2,256,256]{2,1,0:T(8,128)(2,1)} %copy-done.15), custom_call_target="tpu_custom_call" | custom-call | flops 2300000000 | tf_op jit(solution)/shard_map/pallas_call | solution.py:397
  40.3 4.6 %collective-permute-start.14 = (bf16[4,2,256,256]{3,2,1,0:T(8,128)(2,1)}, bf16[4,2,256,256]{3,2,1,0:T(8,128)(2,1)S(1)}, u32[]{:S(2)}, u32[]{:S(2)}) collective-permute-start(bf16[4,2,256,256]{3,2,1,0:T(8,128)(2,1)} %shard_map.75.kv0), channel_id=1, source_target_pairs={{0,4},{1,5},{2,6},{3,7},{4,8},{5,9},{6,10},{7,11},{8,12},{9,13},{1... | collective-permute-start | bytes 3145736 | tf_op jit(solution)/shard_map/ppermute | solution.py:407
  44.9 4.7 %collective-permute-done.8.refs_3_ = bf16[3,256,256]{2,1,0:T(8,128)(2,1)} collective-permute-done((bf16[3,256,256]{2,1,0:T(8,128)(2,1)S(1)}, bf16[3,256,256]{2,1,0:T(8,128)(2,1)}, u32[]{:S(2)}, u32[]{:S(2)}) %collective-permute-start.8) | collective-permute-done | bytes 393248 | tf_op jit(solution)/shard_map/ppermute | solution.py:393
  49.6 2.6 %shard_map.69.kv.rest = bf16[4,3,256,256]{3,2,1,0:T(8,128)(2,1)} custom-call(bf16[3,256,256]{2,1,0:T(8,128)(2,1)} %get-tuple-element.37.refs_0_, bf16[3,256,256]{2,1,0:T(8,128)(2,1)} %copy-done.12, bf16[3,256,256]{2,1,0:T(8,128)(2,1)} %collective-permute-done.7.refs_2_, bf16[3,256,256]{2,1,0:T(8,128)(2,1)} %collective-permute-done.8.refs_3_), custom_call_target="tpu_custom_call" | custom-call | flops 2300000000 | tf_op jit(solution)/shard_map/pallas_call | solution.py:397
  53.5 6.3 %shard_map.73 = (f32[2,128,1024]{2,1,0:T(8,128)}, f32[2,8,1024]{2,1,0:T(8,128)}) custom-call(s32[16]{0:T(128)} %select_reduce_fusion.order, s32[16]{0:T(128)} %windows.7, bf16[4,256,256]{2,1,0:T(8,128)(2,1)} %shard_map.68.q, bf16[4,3,256,256]{3,2,1,0:T(8,128)(2,1)} %shard_map.69.kv.rest), custom_call_target="tpu_custom_call" | custom-call | flops 8049999872 | tf_op jit(solution)/shard_map/pallas_call | solution.py:413
  59.8 8.7 %collective-permute-done.5.q = bf16[4,256,256]{2,1,0:T(8,128)(2,1)S(1)} collective-permute-done((bf16[4,256,256]{2,1,0:T(8,128)(2,1)S(1)}, bf16[4,256,256]{2,1,0:T(8,128)(2,1)S(1)}, u32[]{:S(2)}, u32[]{:S(2)}) %collective-permute-start.5) | collective-permute-done | bytes 524320 | tf_op jit(solution)/shard_map/ppermute | solution.py:410
  69.3 6.4 %shard_map.70 = bf16[2,144,1024]{2,1,0:T(8,128)(2,1)} custom-call(s32[16]{0:T(128)} %select_reduce_fusion.order, s32[16]{0:T(128)} %windows.7, bf16[4,256,256]{2,1,0:T(8,128)(2,1)} %copy-done.8, bf16[4,3,256,256]{3,2,1,0:T(8,128)(2,1)} %shard_map.69.kv.rest), custom_call_target="tpu_custom_call" | custom-call | flops 8049999872 | tf_op jit(solution)/shard_map/pallas_call | solution.py:413
  75.8 3.7 %collective-permute-start.9 = (bf16[2,144,1024]{2,1,0:T(8,128)(2,1)}, bf16[2,144,1024]{2,1,0:T(8,128)(2,1)S(1)}, u32[]{:S(2)}, u32[]{:S(2)}) collective-permute-start(bf16[2,144,1024]{2,1,0:T(8,128)(2,1)} %shard_map.70), channel_id=1, source_target_pairs={{0,4},{1,5},{2,6},{3,7},{4,8},{5,9},{6,10},{7,11},{8,12},{9,13},{1... | collective-permute-start | bytes 1769480 | tf_op jit(solution)/shard_map/ppermute | solution.py:407
  79.5 1.9 %collective-permute-start.15 = (bf16[2,2,256,256]{3,2,1,0:T(8,128)(2,1)S(1)}, bf16[2,2,256,256]{3,2,1,0:T(8,128)(2,1)S(1)}, u32[]{:S(2)}, u32[]{:S(2)}) collective-permute-start(bf16[2,2,256,256]{3,2,1,0:T(8,128)(2,1)S(1)} %get-tuple-element.60), channel_id=1, source_target_pairs={{0,4},{1,5},{2,6},{3,7},{4,8},{5,9},{6,10},{7,11},{8,12},{9,13},{1... | collective-permute-start | bytes 1572872 | tf_op jit(solution)/shard_map/ppermute | solution.py:407
  81.5 7.8 %shard_map.71 = (f32[2,128,1024]{2,1,0:T(8,128)}, f32[2,8,1024]{2,1,0:T(8,128)}) custom-call(s32[16]{0:T(128)} %select_reduce_fusion.order, s32[16]{0:T(128)} %windows.7, bf16[4,256,256]{2,1,0:T(8,128)(2,1)} %copy-done.6, bf16[4,3,256,256]{3,2,1,0:T(8,128)(2,1)} %shard_map.69.kv.rest), custom_call_target="tpu_custom_call" | custom-call | flops 8049999872 | tf_op jit(solution)/shard_map/pallas_call | solution.py:413
  89.3 4.1 %collective-permute-done.9.arrived = bf16[2,144,1024]{2,1,0:T(8,128)(2,1)S(1)} collective-permute-done((bf16[2,144,1024]{2,1,0:T(8,128)(2,1)}, bf16[2,144,1024]{2,1,0:T(8,128)(2,1)S(1)}, u32[]{:S(2)}, u32[]{:S(2)}) %collective-permute-start.9) | collective-permute-done | bytes 589856 | tf_op jit(solution)/shard_map/ppermute | solution.py:407
  94.3 2.6 %shard_map.72 = bf16[2,144,1024]{2,1,0:T(8,128)(2,1)} custom-call(bf16[2,144,1024]{2,1,0:T(8,128)(2,1)} %copy-done.4, f32[2,128,1024]{2,1,0:T(8,128)} %get-tuple-element.41.sums, f32[2,8,1024]{2,1,0:T(8,128)} %get-tuple-element.42.stats), custom_call_target="tpu_custom_call" | custom-call | flops 1150000000 | tf_op jit(solution)/shard_map/pallas_call | solution.py:413
  96.8 4.5 %collective-permute-start.10 = (bf16[2,144,1024]{2,1,0:T(8,128)(2,1)}, bf16[2,144,1024]{2,1,0:T(8,128)(2,1)S(1)}, u32[]{:S(2)}, u32[]{:S(2)}) collective-permute-start(bf16[2,144,1024]{2,1,0:T(8,128)(2,1)} %shard_map.72), channel_id=1, source_target_pairs={{0,4},{1,5},{2,6},{3,7},{4,8},{5,9},{6,10},{7,11},{8,12},{9,13},{1... | collective-permute-start | bytes 1769480 | tf_op jit(solution)/shard_map/ppermute | solution.py:407
  101.4 3.2 %collective-permute-done.15.kv2 = bf16[2,2,256,256]{3,2,1,0:T(8,128)(2,1)S(1)} collective-permute-done((bf16[2,2,256,256]{3,2,1,0:T(8,128)(2,1)S(1)}, bf16[2,2,256,256]{3,2,1,0:T(8,128)(2,1)S(1)}, u32[]{:S(2)}, u32[]{:S(2)}) %collective-permute-start.15) | collective-permute-done | bytes 524320 | tf_op jit(solution)/shard_map/ppermute | solution.py:407
  105.4 9.0 %far.1 = (bf16[256,256]{1,0:T(8,128)(2,1)}, bf16[256,256]{1,0:T(8,128)(2,1)}, bf16[256,256]{1,0:T(8,128)(2,1)}, bf16[256,256]{1,0:T(8,128)(2,1)}, bf16[16,8,384]{2,1,0:T(8,128)(2,1)}) custom-call(s32[16]{0:T(128)} %select_reduce_fusion.order, s32[16]{0:T(128)} %windows.7, bf16[4,3,256,256]{3,2,1,0:T(8,128)(2,1)} %shard_map.69.kv.rest, ...), custom_call_target="tpu_custom_call" | custom-call | flops 16099999744 | tf_op jit(solution)/shard_map/far/pallas_call | solution.py:483
  116.6 4.0 %shard_map.76 = (bf16[256,256]{1,0:T(8,128)(2,1)}, bf16[256,256]{1,0:T(8,128)(2,1)}, bf16[256,256]{1,0:T(8,128)(2,1)}, bf16[256,256]{1,0:T(8,128)(2,1)}, bf16[16,8,768]{2,1,0:T(8,128)(2,1)}) custom-call(s32[16]{0:T(128)} %select_reduce_fusion.order, bf16[2,144,1024]{2,1,0:T(8,128)(2,1)} %copy-done.5, f32[2,128,1024]{2,1,0:T(8,128)} %get-tuple-element.43.sums, ...), custom_call_target="tpu_custom_call" | custom-call | flops 4600000000 | tf_op jit(solution)/shard_map/pallas_call | solution.py:413
  120.5 9.3 %all-to-all-start.1 = ((bf16[16,8,768]{2,1,0:T(8,128)(2,1)}), bf16[16,8,768]{2,1,0:T(8,128)(2,1)S(1)}, u32[]{:S(2)}, u32[]{:S(2)}) async-start(bf16[16,8,768]{2,1,0:T(8,128)(2,1)} %get-tuple-element.50), calls=%async_computation.1 | async-start | bytes 393216 | tf_op jit(solution)/shard_map/all_to_all | solution.py:502
  130.3 1.6 %collective-permute-start.17 = (bf16[256,256]{1,0:T(8,128)(2,1)S(1)}, bf16[256,256]{1,0:T(8,128)(2,1)S(1)}, u32[]{:S(2)}, u32[]{:S(2)}) collective-permute-start(bf16[256,256]{1,0:T(8,128)(2,1)S(1)} %copy-done.17), channel_id=1, source_target_pairs={{0,2},{1,3},{2,0},{3,1},{4,6},{5,7},{6,4},{7,5},{8,10},{9,11},{10,... | collective-permute-start | bytes 393224 | tf_op jit(solution)/shard_map/ppermute | solution.py:393
  132.5 1.6 %collective-permute-start.20 = (bf16[256,256]{1,0:T(8,128)(2,1)}, bf16[256,256]{1,0:T(8,128)(2,1)S(1)}, u32[]{:S(2)}, u32[]{:S(2)}) collective-permute-start(bf16[256,256]{1,0:T(8,128)(2,1)} %get-tuple-element.57), channel_id=1, source_target_pairs={{0,2},{1,3},{2,0},{3,1},{4,6},{5,7},{6,4},{7,5},{8,10},{9,11},{10,... | collective-permute-start | bytes 393224 | tf_op jit(solution)/shard_map/ppermute | solution.py:393
  134.1 4.2 %collective-permute-done.17.refs_2_ = bf16[256,256]{1,0:T(8,128)(2,1)S(1)} collective-permute-done((bf16[256,256]{1,0:T(8,128)(2,1)S(1)}, bf16[256,256]{1,0:T(8,128)(2,1)S(1)}, u32[]{:S(2)}, u32[]{:S(2)}) %collective-permute-start.17) | collective-permute-done | bytes 131104 | tf_op jit(solution)/shard_map/ppermute | solution.py:393
  138.3 1.8 %collective-permute-done.18.refs_3_ = bf16[256,256]{1,0:T(8,128)(2,1)S(1)} collective-permute-done((bf16[256,256]{1,0:T(8,128)(2,1)S(1)}, bf16[256,256]{1,0:T(8,128)(2,1)S(1)}, u32[]{:S(2)}, u32[]{:S(2)}) %collective-permute-start.18) | collective-permute-done | bytes 131104 | tf_op jit(solution)/shard_map/ppermute | solution.py:393
  140.1 3.9 %collective-permute-done.20.refs_6_ = bf16[256,256]{1,0:T(8,128)(2,1)S(1)} collective-permute-done((bf16[256,256]{1,0:T(8,128)(2,1)}, bf16[256,256]{1,0:T(8,128)(2,1)S(1)}, u32[]{:S(2)}, u32[]{:S(2)}) %collective-permute-start.20) | collective-permute-done | bytes 131104 | tf_op jit(solution)/shard_map/ppermute | solution.py:393
  144.0 1.7 %collective-permute-done.21.refs_7_ = bf16[256,256]{1,0:T(8,128)(2,1)S(1)} collective-permute-done((bf16[256,256]{1,0:T(8,128)(2,1)}, bf16[256,256]{1,0:T(8,128)(2,1)S(1)}, u32[]{:S(2)}, u32[]{:S(2)}) %collective-permute-start.21) | collective-permute-done | bytes 131104 | tf_op jit(solution)/shard_map/ppermute | solution.py:393
  146.4 3.9 %shard_map.77 = (bf16[256,2048]{1,0:T(8,128)(2,1)}, bf16[8,2048]{1,0:T(8,128)(2,1)}) custom-call(s32[16]{0:T(128)} %select_reduce_fusion.order, bf16[4,4,8,768]{3,2,1,0:T(8,128)(2,1)} %bitcast.2, bf16[3,8,2048]{2,1,0:T(8,128)(2,1)} %cont.1, bf16[256,256]{1,0:T(8,128)(2,1)} %get-tuple-element.51.refs_0_, bf16[256,256]{1,0:T(8,128)(2,1)} %copy-done.18, ...), custom_call_target="tpu_custom_call" | custom-call | flops 4600000000 | tf_op jit(solution)/shard_map/pallas_call | solution.py:413
  (92 shorter events, 15.7 us)
Async XLA Ops:
  8.0 5.0 %collective-permute-start.1 = (bf16[256,256]{1,0:T(8,128)(2,1)}, bf16[256,256]{1,0:T(8,128)(2,1)S(1)}, u32[]{:S(2)}, u32[]{:S(2)}) collective-permute-start(bf16[256,256]{1,0:T(8,128)(2,1)} %get-tuple-element.34), channel_id=1, source_target_pairs={{0,1},{1,0},{2,3},{3,2},{4,5},{5,4},{6,7},{7,6},{8,9},{9,8},{10,11... | collective-permute-start | bytes 393224 | tf_op jit(solution)/shard_map/ppermute | solution.py:393
  8.6 22.9 %collective-permute-start.11 = (bf16[2,256,256]{2,1,0:T(8,128)(2,1)}, bf16[2,256,256]{2,1,0:T(8,128)(2,1)S(1)}, u32[]{:S(2)}, u32[]{:S(2)}) collective-permute-start(bf16[2,256,256]{2,1,0:T(8,128)(2,1)} %get-tuple-element.46), channel_id=1, source_target_pairs={{0,1},{1,0},{2,3},{3,2},{4,5},{5,4},{6,7},{7,6},{8,9},{9,8},{10,11... | collective-permute-start | bytes 786440 | tf_op jit(solution)/shard_map/ppermute | solution.py:393
  8.6 25.3 %collective-permute-start.12 = (bf16[2,256,256]{2,1,0:T(8,128)(2,1)}, bf16[2,256,256]{2,1,0:T(8,128)(2,1)S(1)}, u32[]{:S(2)}, u32[]{:S(2)}) collective-permute-start(bf16[2,256,256]{2,1,0:T(8,128)(2,1)} %get-tuple-element.47), channel_id=1, source_target_pairs={{0,2},{1,3},{2,0},{3,1},{4,6},{5,7},{6,4},{7,5},{8,10},{9,11},{10,... | collective-permute-start | bytes 786440 | tf_op jit(solution)/shard_map/ppermute | solution.py:393
  11.5 25.8 %collective-permute-start.13 = (bf16[2,256,256]{2,1,0:T(8,128)(2,1)}, bf16[2,256,256]{2,1,0:T(8,128)(2,1)S(1)}, u32[]{:S(2)}, u32[]{:S(2)}) collective-permute-start(bf16[2,256,256]{2,1,0:T(8,128)(2,1)} %get-tuple-element.48), channel_id=1, source_target_pairs={{0,3},{1,2},{2,1},{3,0},{4,7},{5,6},{6,5},{7,4},{8,11},{9,10},{10,... | collective-permute-start | bytes 786440 | tf_op jit(solution)/shard_map/ppermute | solution.py:393
  11.5 16.5 %collective-permute-start.2 = (bf16[256,256]{1,0:T(8,128)(2,1)}, bf16[256,256]{1,0:T(8,128)(2,1)S(1)}, u32[]{:S(2)}, u32[]{:S(2)}) collective-permute-start(bf16[256,256]{1,0:T(8,128)(2,1)} %get-tuple-element.35), channel_id=1, source_target_pairs={{0,2},{1,3},{2,0},{3,1},{4,6},{5,7},{6,4},{7,5},{8,10},{9,11},{10,... | collective-permute-start | bytes 393224 | tf_op jit(solution)/shard_map/ppermute | solution.py:393
  13.0 15.1 %copy-start.11 = (bf16[3,256,256]{2,1,0:T(8,128)(2,1)S(1)}, bf16[3,256,256]{2,1,0:T(8,128)(2,1)}, u32[]{:S(2)}) copy-start(bf16[3,256,256]{2,1,0:T(8,128)(2,1)} %get-tuple-element.38) | copy-start | bytes 1179652
  13.0 17.2 %copy-start.10 = (bf16[3,256,256]{2,1,0:T(8,128)(2,1)S(1)}, bf16[3,256,256]{2,1,0:T(8,128)(2,1)}, u32[]{:S(2)}) copy-start(bf16[3,256,256]{2,1,0:T(8,128)(2,1)} %get-tuple-element.39) | copy-start | bytes 1179652
  13.0 18.5 %copy-start.9 = (bf16[3,256,256]{2,1,0:T(8,128)(2,1)S(1)}, bf16[3,256,256]{2,1,0:T(8,128)(2,1)}, u32[]{:S(2)}) copy-start(bf16[3,256,256]{2,1,0:T(8,128)(2,1)} %get-tuple-element.40) | copy-start | bytes 1179652
  13.0 17.1 %collective-permute-start.3 = (bf16[256,256]{1,0:T(8,128)(2,1)}, bf16[256,256]{1,0:T(8,128)(2,1)S(1)}, u32[]{:S(2)}, u32[]{:S(2)}) collective-permute-start(bf16[256,256]{1,0:T(8,128)(2,1)} %get-tuple-element.36), channel_id=1, source_target_pairs={{0,3},{1,2},{2,1},{3,0},{4,7},{5,6},{6,5},{7,4},{8,11},{9,10},{10,... | collective-permute-start | bytes 393224 | tf_op jit(solution)/shard_map/ppermute | solution.py:393
  15.0 20.3 %copy-start.28 = (s32[16]{0:T(128)S(1)}, s32[16]{0:T(128)}, u32[]{:S(2)}) copy-start(s32[16]{0:T(128)} %windows.7) | copy-start | bytes 196
  15.0 21.6 %copy-start.3 = (s32[16]{0:T(128)S(1)}, s32[16]{0:T(128)}, u32[]{:S(2)}) copy-start(s32[16]{0:T(128)} %param.11) | copy-start | bytes 196
  15.0 86.3 %all-to-all-start = ((bf16[16,8,512]{2,1,0:T(8,128)(2,1)}), bf16[16,8,512]{2,1,0:T(8,128)(2,1)S(1)}, u32[]{:S(2)}, u32[]{:S(2)}) async-start(bf16[16,8,512]{2,1,0:T(8,128)(2,1)} %shard_map.74), calls=%async_computation | async-start | bytes 262144 | tf_op jit(solution)/shard_map/all_to_all | solution.py:450
  28.1 16.8 %collective-permute-start.6 = (bf16[3,256,256]{2,1,0:T(8,128)(2,1)S(1)}, bf16[3,256,256]{2,1,0:T(8,128)(2,1)S(1)}, u32[]{:S(2)}, u32[]{:S(2)}) collective-permute-start(bf16[3,256,256]{2,1,0:T(8,128)(2,1)S(1)} %copy-done.11), channel_id=1, source_target_pairs={{0,1},{1,0},{2,3},{3,2},{4,5},{5,4},{6,7},{7,6},{8,9},{9,8},{10,11... | collective-permute-start | bytes 1179656 | tf_op jit(solution)/shard_map/ppermute | solution.py:393
  30.1 14.8 %collective-permute-start.7 = (bf16[3,256,256]{2,1,0:T(8,128)(2,1)S(1)}, bf16[3,256,256]{2,1,0:T(8,128)(2,1)}, u32[]{:S(2)}, u32[]{:S(2)}) collective-permute-start(bf16[3,256,256]{2,1,0:T(8,128)(2,1)S(1)} %copy-done.10), channel_id=1, source_target_pairs={{0,2},{1,3},{2,0},{3,1},{4,6},{5,7},{6,4},{7,5},{8,10},{9,11},{10,... | collective-permute-start | bytes 1179656 | tf_op jit(solution)/shard_map/ppermute | solution.py:393
  31.4 18.2 %collective-permute-start.8 = (bf16[3,256,256]{2,1,0:T(8,128)(2,1)S(1)}, bf16[3,256,256]{2,1,0:T(8,128)(2,1)}, u32[]{:S(2)}, u32[]{:S(2)}) collective-permute-start(bf16[3,256,256]{2,1,0:T(8,128)(2,1)S(1)} %copy-done.9), channel_id=1, source_target_pairs={{0,3},{1,2},{2,1},{3,0},{4,7},{5,6},{6,5},{7,4},{8,11},{9,10},{10,... | collective-permute-start | bytes 1179656 | tf_op jit(solution)/shard_map/ppermute | solution.py:393
  34.0 18.2 %collective-permute-start.4 = (bf16[4,256,256]{2,1,0:T(8,128)(2,1)}, bf16[4,256,256]{2,1,0:T(8,128)(2,1)S(1)}, u32[]{:S(2)}, u32[]{:S(2)}) collective-permute-start(bf16[4,256,256]{2,1,0:T(8,128)(2,1)} %shard_map.68.q), channel_id=1, source_target_pairs={{4,0},{5,1},{6,2},{7,3},{8,4},{9,5},{10,6},{11,7},{12,8},{13,9},{1... | collective-permute-start | bytes 1572872 | tf_op jit(solution)/shard_map/ppermute | solution.py:410
  40.3 39.2 %collective-permute-start.14 = (bf16[4,2,256,256]{3,2,1,0:T(8,128)(2,1)}, bf16[4,2,256,256]{3,2,1,0:T(8,128)(2,1)S(1)}, u32[]{:S(2)}, u32[]{:S(2)}) collective-permute-start(bf16[4,2,256,256]{3,2,1,0:T(8,128)(2,1)} %shard_map.75.kv0), channel_id=1, source_target_pairs={{0,4},{1,5},{2,6},{3,7},{4,8},{5,9},{6,10},{7,11},{8,12},{9,13},{1... | collective-permute-start | bytes 3145736 | tf_op jit(solution)/shard_map/ppermute | solution.py:407
  52.2 16.3 %collective-permute-start.5 = (bf16[4,256,256]{2,1,0:T(8,128)(2,1)S(1)}, bf16[4,256,256]{2,1,0:T(8,128)(2,1)S(1)}, u32[]{:S(2)}, u32[]{:S(2)}) collective-permute-start(bf16[4,256,256]{2,1,0:T(8,128)(2,1)S(1)} %collective-permute-done.4.q), channel_id=1, source_target_pairs={{4,0},{5,1},{6,2},{7,3},{8,4},{9,5},{10,6},{11,7},{12,8},{13,9},{1... | collective-permute-start | bytes 1572872 | tf_op jit(solution)/shard_map/ppermute | solution.py:410
  75.8 17.6 %collective-permute-start.9 = (bf16[2,144,1024]{2,1,0:T(8,128)(2,1)}, bf16[2,144,1024]{2,1,0:T(8,128)(2,1)S(1)}, u32[]{:S(2)}, u32[]{:S(2)}) collective-permute-start(bf16[2,144,1024]{2,1,0:T(8,128)(2,1)} %shard_map.70), channel_id=1, source_target_pairs={{0,4},{1,5},{2,6},{3,7},{4,8},{5,9},{6,10},{7,11},{8,12},{9,13},{1... | collective-permute-start | bytes 1769480 | tf_op jit(solution)/shard_map/ppermute | solution.py:407
  79.5 25.0 %collective-permute-start.15 = (bf16[2,2,256,256]{3,2,1,0:T(8,128)(2,1)S(1)}, bf16[2,2,256,256]{3,2,1,0:T(8,128)(2,1)S(1)}, u32[]{:S(2)}, u32[]{:S(2)}) collective-permute-start(bf16[2,2,256,256]{3,2,1,0:T(8,128)(2,1)S(1)} %get-tuple-element.60), channel_id=1, source_target_pairs={{0,4},{1,5},{2,6},{3,7},{4,8},{5,9},{6,10},{7,11},{8,12},{9,13},{1... | collective-permute-start | bytes 1572872 | tf_op jit(solution)/shard_map/ppermute | solution.py:407
  96.8 18.9 %collective-permute-start.10 = (bf16[2,144,1024]{2,1,0:T(8,128)(2,1)}, bf16[2,144,1024]{2,1,0:T(8,128)(2,1)S(1)}, u32[]{:S(2)}, u32[]{:S(2)}) collective-permute-start(bf16[2,144,1024]{2,1,0:T(8,128)(2,1)} %shard_map.72), channel_id=1, source_target_pairs={{0,4},{1,5},{2,6},{3,7},{4,8},{5,9},{6,10},{7,11},{8,12},{9,13},{1... | collective-permute-start | bytes 1769480 | tf_op jit(solution)/shard_map/ppermute | solution.py:407
  116.6 13.3 %copy-start.22 = (bf16[256,256]{1,0:T(8,128)(2,1)S(1)}, bf16[256,256]{1,0:T(8,128)(2,1)}, u32[]{:S(2)}) copy-start(bf16[256,256]{1,0:T(8,128)(2,1)} %get-tuple-element.52) | copy-start | bytes 393220
  116.6 13.7 %copy-start.17 = (bf16[256,256]{1,0:T(8,128)(2,1)S(1)}, bf16[256,256]{1,0:T(8,128)(2,1)}, u32[]{:S(2)}) copy-start(bf16[256,256]{1,0:T(8,128)(2,1)} %get-tuple-element.53) | copy-start | bytes 393220
  116.6 15.4 %copy-start.16 = (bf16[256,256]{1,0:T(8,128)(2,1)S(1)}, bf16[256,256]{1,0:T(8,128)(2,1)}, u32[]{:S(2)}) copy-start(bf16[256,256]{1,0:T(8,128)(2,1)} %get-tuple-element.54) | copy-start | bytes 393220
  120.5 25.2 %all-to-all-start.1 = ((bf16[16,8,768]{2,1,0:T(8,128)(2,1)}), bf16[16,8,768]{2,1,0:T(8,128)(2,1)S(1)}, u32[]{:S(2)}, u32[]{:S(2)}) async-start(bf16[16,8,768]{2,1,0:T(8,128)(2,1)} %get-tuple-element.50), calls=%async_computation.1 | async-start | bytes 393216 | tf_op jit(solution)/shard_map/all_to_all | solution.py:502
  129.8 4.3 %collective-permute-start.16 = (bf16[256,256]{1,0:T(8,128)(2,1)S(1)}, bf16[256,256]{1,0:T(8,128)(2,1)S(1)}, u32[]{:S(2)}, u32[]{:S(2)}) collective-permute-start(bf16[256,256]{1,0:T(8,128)(2,1)S(1)} %copy-done.22), channel_id=1, source_target_pairs={{0,1},{1,0},{2,3},{3,2},{4,5},{5,4},{6,7},{7,6},{8,9},{9,8},{10,11... | collective-permute-start | bytes 393224 | tf_op jit(solution)/shard_map/ppermute | solution.py:393
  130.3 8.0 %collective-permute-start.17 = (bf16[256,256]{1,0:T(8,128)(2,1)S(1)}, bf16[256,256]{1,0:T(8,128)(2,1)S(1)}, u32[]{:S(2)}, u32[]{:S(2)}) collective-permute-start(bf16[256,256]{1,0:T(8,128)(2,1)S(1)} %copy-done.17), channel_id=1, source_target_pairs={{0,2},{1,3},{2,0},{3,1},{4,6},{5,7},{6,4},{7,5},{8,10},{9,11},{10,... | collective-permute-start | bytes 393224 | tf_op jit(solution)/shard_map/ppermute | solution.py:393
  132.0 8.1 %collective-permute-start.18 = (bf16[256,256]{1,0:T(8,128)(2,1)S(1)}, bf16[256,256]{1,0:T(8,128)(2,1)S(1)}, u32[]{:S(2)}, u32[]{:S(2)}) collective-permute-start(bf16[256,256]{1,0:T(8,128)(2,1)S(1)} %copy-done.16), channel_id=1, source_target_pairs={{0,3},{1,2},{2,1},{3,0},{4,7},{5,6},{6,5},{7,4},{8,11},{9,10},{10,... | collective-permute-start | bytes 393224 | tf_op jit(solution)/shard_map/ppermute | solution.py:393
  132.0 8.1 %collective-permute-start.19 = (bf16[256,256]{1,0:T(8,128)(2,1)}, bf16[256,256]{1,0:T(8,128)(2,1)S(1)}, u32[]{:S(2)}, u32[]{:S(2)}) collective-permute-start(bf16[256,256]{1,0:T(8,128)(2,1)} %get-tuple-element.56), channel_id=1, source_target_pairs={{0,1},{1,0},{2,3},{3,2},{4,5},{5,4},{6,7},{7,6},{8,9},{9,8},{10,11... | collective-permute-start | bytes 393224 | tf_op jit(solution)/shard_map/ppermute | solution.py:393
  132.5 11.6 %collective-permute-start.20 = (bf16[256,256]{1,0:T(8,128)(2,1)}, bf16[256,256]{1,0:T(8,128)(2,1)S(1)}, u32[]{:S(2)}, u32[]{:S(2)}) collective-permute-start(bf16[256,256]{1,0:T(8,128)(2,1)} %get-tuple-element.57), channel_id=1, source_target_pairs={{0,2},{1,3},{2,0},{3,1},{4,6},{5,7},{6,4},{7,5},{8,10},{9,11},{10,... | collective-permute-start | bytes 393224 | tf_op jit(solution)/shard_map/ppermute | solution.py:393
  134.1 11.6 %copy-start.18 = (bf16[256,256]{1,0:T(8,128)(2,1)}, bf16[256,256]{1,0:T(8,128)(2,1)S(1)}, u32[]{:S(2)}) copy-start(bf16[256,256]{1,0:T(8,128)(2,1)S(1)} %collective-permute-done.16.refs_1_) | copy-start | bytes 393220
  134.1 11.6 %collective-permute-start.21 = (bf16[256,256]{1,0:T(8,128)(2,1)}, bf16[256,256]{1,0:T(8,128)(2,1)S(1)}, u32[]{:S(2)}, u32[]{:S(2)}) collective-permute-start(bf16[256,256]{1,0:T(8,128)(2,1)} %get-tuple-element.58), channel_id=1, source_target_pairs={{0,3},{1,2},{2,1},{3,0},{4,7},{5,6},{6,5},{7,4},{8,11},{9,10},{10,... | collective-permute-start | bytes 393224 | tf_op jit(solution)/shard_map/ppermute | solution.py:393
  (20 other events, 68.4 us)

commit v3 on v2

--- a/solution.py
+++ b/solution.py
@@ -21,6 +21,9 @@
 SMEM = pl.BlockSpec(memory_space=pltpu.SMEM)
 VMEM = pl.BlockSpec(memory_space=pltpu.VMEM)
 ANY = pl.BlockSpec(memory_space=pl.ANY)
+
+
+GRANT = pltpu.CompilerParams(vmem_limit_bytes=20 * 2**20)
 
 
 def cost(micros):
@@ -97,9 +100,10 @@
     row_index = lax.broadcasted_iota(jnp.int32, (block, block), 1)
     key_index = lax.broadcasted_iota(jnp.int32, (block, block), 0)
 
-    def step(distance, diagonal):
+    def step(distance, diagonal, heads):
         spot = pl.ds((base + part - distance) * shards, shards)
-        for head, window in enumerate(windows):
+        for head in range(heads):
+            window = windows[head]
             column = slice(head * head_dim, (head + 1) * head_dim)
             keys = kv[spot, 0, :, column].reshape(block, head_dim)
             values = kv[spot, 1, :, column].reshape(block, head_dim)
@@ -117,21 +121,25 @@
             peak[head, 0:1, :] = new
             acc[head] = acc[head] * fade + dot(values, expo.astype(BF16), (0, 0))
 
-    longest = functools.reduce(jnp.maximum, windows)
-    reach = jnp.minimum((longest + block - 2) // block, high_limit)
+    limit = jnp.minimum(base + part, high_limit)
+    ends = [jnp.minimum((window + block - 2) // block, limit) + 1 for window in windows]
     low = jnp.maximum(base + part - (key_parts - 1), 0)
 
     if base - (key_parts - 1) <= 0:
 
         @pl.when(low == 0)
         def _():
-            step(0, True)
-
-    def loop(distance, carry):
-        step(distance, False)
-        return carry
-
-    lax.fori_loop(jnp.maximum(low, 1), jnp.minimum(reach, base + part) + 1, loop, 0)
+            step(0, True, len(windows))
+
+    start = jnp.maximum(low, 1)
+    for heads in range(len(windows), 0, -1):
+
+        def loop(distance, carry, heads=heads):
+            step(distance, False, heads)
+            return carry
+
+        lax.fori_loop(start, ends[heads - 1], loop, 0)
+        start = jnp.maximum(start, ends[heads - 1])
 
 
 def cross_part(out, rows, starts, gain, order, first, offset, anchor, result, head_dim, base=0):
@@ -155,7 +163,11 @@
             q = rows[spot, :, offset + c * head_dim : offset + (c + 1) * head_dim].reshape(block, head_dim)
             scores = dot(q, keys, (1, 1))
             position = anchor + lax.broadcasted_iota(jnp.int32, (block, keys_here), 1)
-            seen = position < starts[pl.ds(index * block, block), :]
+            which = lax.broadcasted_iota(jnp.int32, (block, 1), 0) // CLEN
+            limits = jnp.zeros((block, 1), jnp.int32)
+            for k in range(block // CLEN):
+                limits = jnp.where(which == k, starts[index * (block // CLEN) + k], limits)
+            seen = position < limits
             scores = jnp.where(seen, scores, NEGATIVE)
             high = jnp.maximum(jnp.max(scores, axis=1, keepdims=True), FLOOR)
             expo = jnp.exp2((scores - high) * factor)
@@ -199,9 +211,9 @@
     for k, source in enumerate((kv3, kv2, kv1, kv0)):
         copies.append(pltpu.make_async_copy(source, kv.at[pl.ds(start, source.shape[0])], sems.at[k]))
         start += source.shape[0]
-    for copy in copies:
+    for copy in copies[::-1]:
         copy.start()
-    for copy in copies:
+    for copy in copies[::-1]:
         copy.wait()
     length = out.shape[1]
     parts = group * length // block
@@ -300,7 +312,7 @@
     lax.fori_loop(0, near * (width // block), one, 0)
 
 
-def last_kernel(dims, axis, order, arrived, sums, stats, rows, starts, gain, other, *refs):
+def last_kernel(dims, axis, order, starts, arrived, sums, stats, rows, gain, other, *refs):
     group, slots, near, head_dim, block = dims
     outs, (result, out) = refs[:group], refs[group:]
     row = lax.axis_index(axis) // group
@@ -375,7 +387,6 @@
     count = devices // group
     block = 2 * length
     rows_here = cont_qkv.shape[1]
-    rows_all = rows_here * devices
     nearby, distant = near * head_dim, far * head_dim
     dims = (group, slots, near, head_dim)
     big = dims + (block,)
@@ -401,6 +412,7 @@
             out_specs=VMEM,
             scratch_shapes=[pltpu.SemaphoreType.DMA((group,))],
             cost_estimate=cost(micros),
+        compiler_params=GRANT,
         )(*blocks)
 
     def up(value):
@@ -416,6 +428,7 @@
             in_specs=[SMEM] * smem + [VMEM] * (len(operands) - smem),
             out_specs=jax.tree.map(lambda _: VMEM, shapes),
             cost_estimate=cost(micros),
+        compiler_params=GRANT,
             **more,
         )(*operands)
 
@@ -439,6 +452,7 @@
         + (pl.BlockSpec((1, length // 2, nearby), lambda i, j: (i, j, 0)),) * group,
         name="pack",
         cost_estimate=cost(4),
+        compiler_params=GRANT,
     )(order, self_qkv)
     q_near0 = gather(exchange(packed[group : 2 * group]), 1)
     kv_far0 = gather(exchange(packed[:group]), 2)
@@ -448,7 +462,6 @@
         cont_qkv, smem=1,
     )
     rows = lax.all_to_all(rows_sent, axis, 0, 0, tiled=True)
-    row_starts = jnp.broadcast_to(starts[:, None], (starts.shape[0], rows_all // starts.shape[0])).reshape(rows_all, 1)
     gain = k_gain.reshape(head_count, head_dim)
 
     kv_far1 = up(kv_far0)
@@ -483,19 +496,20 @@
     *far_out, far_cross = pl.pallas_call(
         functools.partial(far_kernel, big, axis),
         out_shape=(shape(length, distant),) * group + (shape(devices, rows_here, distant + head_dim),),
-        in_specs=[SMEM, SMEM, VMEM, ANY, ANY, ANY, ANY, VMEM, VMEM, VMEM],
+        in_specs=[SMEM, SMEM, VMEM, ANY, ANY, ANY, ANY, VMEM, SMEM, VMEM],
         out_specs=(VMEM,) * (group + 1),
         scratch_shapes=[pltpu.VMEM((group, length, distant), BF16), pltpu.VMEM((3 * group, 2, length, distant), BF16)]
         + state_scratch
         + [pltpu.SemaphoreType.DMA((4,))],
         name="far",
         cost_estimate=cost(14),
-    )(order, windows, rest0, kv_far0, kv_far1, kv_far2, kv_far3, rows, row_starts, gain)
+        compiler_params=GRANT,
+    )(order, windows, rest0, kv_far0, kv_far1, kv_far2, kv_far3, rows, starts, gain)
     far_back = exchange(far_out)
     *near_out, cross = merge(
         last_kernel, 4,
         (shape(length, nearby),) * group + (shape(devices, rows_here, distant + nearby + 2 * head_dim),),
-        order, state1, *local0, rows, row_starts, gain, far_cross, smem=1,
+        order, starts, state1, *local0, rows, gain, far_cross, smem=2,
         scratch_shapes=[pltpu.VMEM((group, length, nearby), BF16)],
     )
     near_back = exchange(near_out)

time: 151 us -> 142 us (0.940)
  Pallas kernels: 54.1 us -> 35 us
  waiting for transfers between devices: 42.5 us -> 48.8 us
  local copies, waits for them, and re-layouts: 5.5 us -> 11.2 us
    pallas_call x7, Pallas kernels: 32.7 us -> 22.4 us  [call(): pl.pallas_call(kernel, out_shape=shapes, in_specs=[SMEM] * smem + [VMEM]...]
    unnamed x58 -> x54, local copies, waits for them, and re-layouts: 4.66 us -> 10.1 us
    ppermute x15, waiting for transfers between devices: 25.1 us -> 29.9 us  [exchange(): lax.ppermute(blocks[k], axis, [(source, source ^ k) for source in range(d...]
    pallas_call x3, Pallas kernels: 6.66 us -> 2.24 us  [gather(): pl.pallas_call(functools.partial(gather_kernel, axis), out_shape=jax.Shap...]
    pallas_call x1, Pallas kernels: 5.72 us -> 3.38 us  [per_device(): pl.pallas_call(functools.partial(pack_kernel, dims, axis), grid=(3, 2), o...]
    pallas_call x1, Pallas kernels: 9.05 us -> 6.92 us  [per_device(): pl.pallas_call(functools.partial(far_kernel, big, axis), out_shape=(shape...]
  transfers between devices with their start and end apart: 23 -> 23, of which waited for: 11 -> 12; matrix products, arithmetic and copies ran while one was open for 1% -> 1% of each run, Pallas kernels for 27% -> 18%
where the time goes in v3:
time: 142 us
  waiting for transfers between devices  48.8 us (34%)
  starting transfers between devices  43.7 us (31%)
  Pallas kernels  35 us (25%)
  local copies, waits for them, and re-layouts  11.2 us (8%)
  other arithmetic  1.68 us (1%)
  between operations  1.51 us (1%)
    ppermute x15, waiting for transfers between devices, exchange(): lax.ppermute(blocks[k], axis, [(source, source ^ k) for source in range(d...  29.9 us
    pallas_call x7, Pallas kernels, call(): pl.pallas_call(kernel, out_shape=shapes, in_specs=[SMEM] * smem + [VMEM]...  22.4 us
    ppermute x4, starting transfers between devices, up(): lax.ppermute(value, axis, [(k, k + group) for k in range(devices - group)])  15.6 us
    ppermute x15, starting transfers between devices, exchange(): lax.ppermute(blocks[k], axis, [(source, source ^ k) for source in range(d...  11.3 us
    unnamed x54, local copies, waits for them, and re-layouts  10.1 us
    ppermute x2, waiting for transfers between devices, down(): lax.ppermute(value, axis, [(k + group, k) for k in range(devices - group)])  9.97 us
    ppermute x4, waiting for transfers between devices, up(): lax.ppermute(value, axis, [(k, k + group) for k in range(devices - group)])  8.87 us
    all_to_all x1, starting transfers between devices, per_device(): cross = lax.all_to_all(cross, axis, 0, 0, tiled=True)  7.89 us
  transfers between devices with their start and end apart: 23, of which 12 were waited for; matrix products, arithmetic and copies ran while one was open for 1% of the time, Pallas kernels for 18%

profile of v3, /device:TPU:0, one launch (start us, length us, event | category | flops | bytes accessed | tf_op | source)
XLA Modules:
  0.0 141.7 jit_solution(12926565770531333888)
XLA Ops:
  1.7 1.9 %copy-done = bf16[3,256,2048]{2,1,0:T(8,128)(2,1)S(1)} copy-done((bf16[3,256,2048]{2,1,0:T(8,128)(2,1)S(1)}, bf16[3,256,2048]{2,1,0:T(8,128)(2,1)}, u32[]{:S(2)}) %copy-start) | copy-done | bytes 3145752
  3.6 3.4 %pack.1 = (bf16[2,256,256]{2,1,0:T(8,128)(2,1)S(1)}, bf16[2,256,256]{2,1,0:T(8,128)(2,1)S(1)}, bf16[2,256,256]{2,1,0:T(8,128)(2,1)S(1)}, bf16[2,256,256]{2,1,0:T...) custom-call(s32[16]{0:T(128)S(1)} %select_reduce_fusion.order, ...), custom_call_target="tpu_custom_call" | custom-call | flops 4600000000 | tf_op jit(solution)/shard_map/pack/pallas_call | solution.py:438
  8.9 3.0 %collective-permute-start.12 = (bf16[2,256,256]{2,1,0:T(8,128)(2,1)S(1)}, bf16[2,256,256]{2,1,0:T(8,128)(2,1)S(1)}, u32[]{:S(2)}, u32[]{:S(2)}) collective-permute-start(bf16[2,256,256]{2,1,0:T(8,128)(2,1)S(1)} %get-tuple-element.47), channel_id=1, source_target_pairs={{0,2},{1,3},{2,0},{3,1},{4,6},{5,7},{6,4},{7,5},{8,10},{9,11},{10,... | collective-permute-start | bytes 786440 | tf_op jit(solution)/shard_map/ppermute | solution.py:404
  11.9 1.4 collective-permute-start.2
  14.9 6.3 %all-to-all-start = ((bf16[16,8,512]{2,1,0:T(8,128)(2,1)}), bf16[16,8,512]{2,1,0:T(8,128)(2,1)S(1)}, u32[]{:S(2)}, u32[]{:S(2)}) async-start(bf16[16,8,512]{2,1,0:T(8,128)(2,1)} %shard_map.74), calls=%async_computation | async-start | bytes 262144 | tf_op jit(solution)/shard_map/all_to_all | solution.py:464
  21.2 7.1 %collective-permute-done.2.refs_2_ = bf16[256,256]{1,0:T(8,128)(2,1)S(1)} collective-permute-done((bf16[256,256]{1,0:T(8,128)(2,1)S(1)}, bf16[256,256]{1,0:T(8,128)(2,1)S(1)}, u32[]{:S(2)}, u32[]{:S(2)}) %collective-permute-start.2) | collective-permute-done | bytes 131104 | tf_op jit(solution)/shard_map/ppermute | solution.py:404
  28.2 1.8 %collective-permute-done.3.refs_3_ = bf16[256,256]{1,0:T(8,128)(2,1)S(1)} collective-permute-done((bf16[256,256]{1,0:T(8,128)(2,1)S(1)}, bf16[256,256]{1,0:T(8,128)(2,1)S(1)}, u32[]{:S(2)}, u32[]{:S(2)}) %collective-permute-start.3) | collective-permute-done | bytes 131104 | tf_op jit(solution)/shard_map/ppermute | solution.py:404
  30.1 1.3 collective-permute-start.7
  36.3 4.6 %collective-permute-start.14 = (bf16[4,2,256,256]{3,2,1,0:T(8,128)(2,1)S(1)}, bf16[4,2,256,256]{3,2,1,0:T(8,128)(2,1)S(1)}, u32[]{:S(2)}, u32[]{:S(2)}) collective-permute-start(bf16[4,2,256,256]{3,2,1,0:T(8,128)(2,1)S(1)} %shard_map.75.kv0), channel_id=1, source_target_pairs={{0,4},{1,5},{2,6},{3,7},{4,8},{5,9},{6,10},{7,11},{8,12},{9,13},{1... | collective-permute-start | bytes 3145736 | tf_op jit(solution)/shard_map/ppermute | solution.py:419
  40.9 1.5 %collective-permute-done.7.refs_2_ = bf16[3,256,256]{2,1,0:T(8,128)(2,1)} collective-permute-done((bf16[3,256,256]{2,1,0:T(8,128)(2,1)}, bf16[3,256,256]{2,1,0:T(8,128)(2,1)}, u32[]{:S(2)}, u32[]{:S(2)}) %collective-permute-start.7) | collective-permute-done | bytes 393248 | tf_op jit(solution)/shard_map/ppermute | solution.py:404
  42.4 7.6 %collective-permute-done.8.refs_3_ = bf16[3,256,256]{2,1,0:T(8,128)(2,1)} collective-permute-done((bf16[3,256,256]{2,1,0:T(8,128)(2,1)}, bf16[3,256,256]{2,1,0:T(8,128)(2,1)}, u32[]{:S(2)}, u32[]{:S(2)}) %collective-permute-start.8) | collective-permute-done | bytes 393248 | tf_op jit(solution)/shard_map/ppermute | solution.py:404
  50.0 1.4 %shard_map.69.kv.rest = bf16[4,3,256,256]{3,2,1,0:T(8,128)(2,1)S(1)} custom-call(bf16[3,256,256]{2,1,0:T(8,128)(2,1)S(1)} %copy-done.18, bf16[3,256,256]{2,1,0:T(8,128)(2,1)} %collective-permute-done.6.refs_1_, bf16[3,256,256]{2,1,0:T(8,128)(2,1)} %collective-permute-done.7.refs_2_, bf16[3,256,256]{2,1,0:T(8,128)(2,1)} %collective-permute-done.8.refs_3_), custom_call_target="tpu_custom_call" | custom-call | flops 2300000000 | tf_op jit(solution)/shard_map/pallas_call | solution.py:408
  52.8 4.3 %shard_map.73 = (f32[2,128,1024]{2,1,0:T(8,128)S(1)}, f32[2,8,1024]{2,1,0:T(8,128)S(1)}) custom-call(s32[16]{0:T(128)S(1)} %select_reduce_fusion.order, s32[16]{0:T(128)S(1)} %copy-done.8, bf16[4,256,256]{2,1,0:T(8,128)(2,1)S(1)} %shard_map.68.q, bf16[4,3,256,256]{3,2,1,0:T(8,128)(2,1)S(1)} %shard_map.69.kv.rest), custom_call_target="tpu_custom_call" | custom-call | flops 8049999872 | tf_op jit(solution)/shard_map/pallas_call | solution.py:425
  57.7 10.0 %collective-permute-done.5.q = bf16[4,256,256]{2,1,0:T(8,128)(2,1)S(1)} collective-permute-done((bf16[4,256,256]{2,1,0:T(8,128)(2,1)S(1)}, bf16[4,256,256]{2,1,0:T(8,128)(2,1)S(1)}, u32[]{:S(2)}, u32[]{:S(2)}) %collective-permute-start.5) | collective-permute-done | bytes 524320 | tf_op jit(solution)/shard_map/ppermute | solution.py:422
  67.7 4.6 %shard_map.70 = bf16[2,144,1024]{2,1,0:T(8,128)(2,1)S(1)} custom-call(s32[16]{0:T(128)S(1)} %select_reduce_fusion.order, s32[16]{0:T(128)S(1)} %copy-done.8, bf16[4,256,256]{2,1,0:T(8,128)(2,1)S(1)} %collective-permute-done.5.q, bf16[4,3,256,256]{3,2,1,0:T(8,128)(2,1)S(1)} %shard_map.69.kv.rest), custom_call_target="tpu_custom_call" | custom-call | flops 8049999872 | tf_op jit(solution)/shard_map/pallas_call | solution.py:425
  72.4 3.7 %collective-permute-start.9 = (bf16[2,144,1024]{2,1,0:T(8,128)(2,1)S(1)}, bf16[2,144,1024]{2,1,0:T(8,128)(2,1)S(1)}, u32[]{:S(2)}, u32[]{:S(2)}) collective-permute-start(bf16[2,144,1024]{2,1,0:T(8,128)(2,1)S(1)} %shard_map.70), channel_id=1, source_target_pairs={{0,4},{1,5},{2,6},{3,7},{4,8},{5,9},{6,10},{7,11},{8,12},{9,13},{1... | collective-permute-start | bytes 1769480 | tf_op jit(solution)/shard_map/ppermute | solution.py:419
  77.1 2.7 %collective-permute-start.15 = (bf16[2,2,256,256]{3,2,1,0:T(8,128)(2,1)}, bf16[2,2,256,256]{3,2,1,0:T(8,128)(2,1)}, u32[]{:S(2)}, u32[]{:S(2)}) collective-permute-start(bf16[2,2,256,256]{3,2,1,0:T(8,128)(2,1)} %get-tuple-element.60), channel_id=1, source_target_pairs={{0,4},{1,5},{2,6},{3,7},{4,8},{5,9},{6,10},{7,11},{8,12},{9,13},{1... | collective-permute-start | bytes 1572872 | tf_op jit(solution)/shard_map/ppermute | solution.py:419
  79.8 5.9 %shard_map.71 = (f32[2,128,1024]{2,1,0:T(8,128)S(1)}, f32[2,8,1024]{2,1,0:T(8,128)S(1)}) custom-call(s32[16]{0:T(128)S(1)} %select_reduce_fusion.order, s32[16]{0:T(128)S(1)} %copy-done.8, bf16[4,256,256]{2,1,0:T(8,128)(2,1)S(1)} %copy-done.2, bf16[4,3,256,256]{3,2,1,0:T(8,128)(2,1)S(1)} %shard_map.69.kv.rest), custom_call_target="tpu_custom_call" | custom-call | flops 8049999872 | tf_op jit(solution)/shard_map/pallas_call | solution.py:425
  86.7 3.0 %collective-permute-done.9.arrived = bf16[2,144,1024]{2,1,0:T(8,128)(2,1)S(1)} collective-permute-done((bf16[2,144,1024]{2,1,0:T(8,128)(2,1)S(1)}, bf16[2,144,1024]{2,1,0:T(8,128)(2,1)S(1)}, u32[]{:S(2)}, u32[]{:S(2)}) %collective-permute-start.9) | collective-permute-done | bytes 589856 | tf_op jit(solution)/shard_map/ppermute | solution.py:419
  91.3 4.6 %collective-permute-start.10 = (bf16[2,144,1024]{2,1,0:T(8,128)(2,1)S(1)}, bf16[2,144,1024]{2,1,0:T(8,128)(2,1)S(1)}, u32[]{:S(2)}, u32[]{:S(2)}) collective-permute-start(bf16[2,144,1024]{2,1,0:T(8,128)(2,1)S(1)} %shard_map.72), channel_id=1, source_target_pairs={{0,4},{1,5},{2,6},{3,7},{4,8},{5,9},{6,10},{7,11},{8,12},{9,13},{1... | collective-permute-start | bytes 1769480 | tf_op jit(solution)/shard_map/ppermute | solution.py:419
  96.0 5.1 %collective-permute-done.15.kv2 = bf16[2,2,256,256]{3,2,1,0:T(8,128)(2,1)} collective-permute-done((bf16[2,2,256,256]{3,2,1,0:T(8,128)(2,1)}, bf16[2,2,256,256]{3,2,1,0:T(8,128)(2,1)}, u32[]{:S(2)}, u32[]{:S(2)}) %collective-permute-start.15) | collective-permute-done | bytes 524320 | tf_op jit(solution)/shard_map/ppermute | solution.py:419
  101.7 1.4 copy-done.16
  103.1 6.9 %far.1 = (bf16[256,256]{1,0:T(8,128)(2,1)S(1)}, bf16[256,256]{1,0:T(8,128)(2,1)S(1)}, bf16[256,256]{1,0:T(8,128)(2,1)S(1)}, bf16[256,256]{1,0:T(8,128)(2,1)S(1)}, bf16[16,8,384]{2,1,0:T(8,128)(2,1)S(1)}) custom-call(s32[16]{0:T(128)S(1)} %copy-done.11, s32[16]{0:T(128)S(1)} %copy-done.8, bf16[4,3,256,256]{3,2,1,0:T(8,128)(2,1)S(1)} %copy-done.16, ...), custom_call_target="tpu_custom_call" | custom-call | flops 16099999744 | tf_op jit(solution)/shard_map/far/pallas_call | solution.py:496
  110.8 2.9 %shard_map.76 = (bf16[256,256]{1,0:T(8,128)(2,1)S(1)}, bf16[256,256]{1,0:T(8,128)(2,1)S(1)}, bf16[256,256]{1,0:T(8,128)(2,1)S(1)}, bf16[256,256]{1,0:T(8,128)(2,1)S(1)}, bf16[16,8,768]{2,1,0:T(8,128)(2,1)}) custom-call(s32[16]{0:T(128)S(1)} %copy-done.11, s32[16]{0:T(128)S(1)} %copy-done.9, bf16[2,144,1024]{2,1,0:T(8,128)(2,1)S(1)} %collective-permute-done.10.arrived, ...), custom_call_target="tpu_custom_call" | custom-call | flops 4600000000 | tf_op jit(solution)/shard_map/pallas_call | solution.py:425
  113.7 7.9 %all-to-all-start.1 = ((bf16[16,8,768]{2,1,0:T(8,128)(2,1)}), bf16[16,8,768]{2,1,0:T(8,128)(2,1)S(1)}, u32[]{:S(2)}, u32[]{:S(2)}) async-start(bf16[16,8,768]{2,1,0:T(8,128)(2,1)} %get-tuple-element.50), calls=%async_computation.1 | async-start | bytes 393216 | tf_op jit(solution)/shard_map/all_to_all | solution.py:516
  122.0 1.6 %collective-permute-start.17 = (bf16[256,256]{1,0:T(8,128)(2,1)}, bf16[256,256]{1,0:T(8,128)(2,1)S(1)}, u32[]{:S(2)}, u32[]{:S(2)}) collective-permute-start(bf16[256,256]{1,0:T(8,128)(2,1)} %copy-done.3), channel_id=1, source_target_pairs={{0,2},{1,3},{2,0},{3,1},{4,6},{5,7},{6,4},{7,5},{8,10},{9,11},{10,... | collective-permute-start | bytes 393224 | tf_op jit(solution)/shard_map/ppermute | solution.py:404
  124.1 1.6 %collective-permute-start.20 = (bf16[256,256]{1,0:T(8,128)(2,1)S(1)}, bf16[256,256]{1,0:T(8,128)(2,1)S(1)}, u32[]{:S(2)}, u32[]{:S(2)}) collective-permute-start(bf16[256,256]{1,0:T(8,128)(2,1)S(1)} %get-tuple-element.57), channel_id=1, source_target_pairs={{0,2},{1,3},{2,0},{3,1},{4,6},{5,7},{6,4},{7,5},{8,10},{9,11},{10,... | collective-permute-start | bytes 393224 | tf_op jit(solution)/shard_map/ppermute | solution.py:404
  125.8 4.2 %collective-permute-done.17.refs_2_ = bf16[256,256]{1,0:T(8,128)(2,1)S(1)} collective-permute-done((bf16[256,256]{1,0:T(8,128)(2,1)}, bf16[256,256]{1,0:T(8,128)(2,1)S(1)}, u32[]{:S(2)}, u32[]{:S(2)}) %collective-permute-start.17) | collective-permute-done | bytes 131104 | tf_op jit(solution)/shard_map/ppermute | solution.py:404
  130.0 2.1 %collective-permute-done.18.refs_3_ = bf16[256,256]{1,0:T(8,128)(2,1)S(1)} collective-permute-done((bf16[256,256]{1,0:T(8,128)(2,1)S(1)}, bf16[256,256]{1,0:T(8,128)(2,1)S(1)}, u32[]{:S(2)}, u32[]{:S(2)}) %collective-permute-start.18) | collective-permute-done | bytes 131104 | tf_op jit(solution)/shard_map/ppermute | solution.py:404
  132.1 3.7 %collective-permute-done.20.refs_6_ = bf16[256,256]{1,0:T(8,128)(2,1)S(1)} collective-permute-done((bf16[256,256]{1,0:T(8,128)(2,1)S(1)}, bf16[256,256]{1,0:T(8,128)(2,1)S(1)}, u32[]{:S(2)}, u32[]{:S(2)}) %collective-permute-start.20) | collective-permute-done | bytes 131104 | tf_op jit(solution)/shard_map/ppermute | solution.py:404
  135.8 1.9 %collective-permute-done.21.refs_7_ = bf16[256,256]{1,0:T(8,128)(2,1)S(1)} collective-permute-done((bf16[256,256]{1,0:T(8,128)(2,1)S(1)}, bf16[256,256]{1,0:T(8,128)(2,1)S(1)}, u32[]{:S(2)}, u32[]{:S(2)}) %collective-permute-start.21) | collective-permute-done | bytes 131104 | tf_op jit(solution)/shard_map/ppermute | solution.py:404
  138.6 3.1 %shard_map.77 = (bf16[256,2048]{1,0:T(8,128)(2,1)}, bf16[8,2048]{1,0:T(8,128)(2,1)}) custom-call(s32[16]{0:T(128)S(1)} %copy-done.12, bf16[4,4,8,768]{3,2,1,0:T(8,128)(2,1)S(1)} %bitcast.2, bf16[3,8,2048]{2,1,0:T(8,128)(2,1)S(1)} %copy-done.6, bf16[256,256]{1,0:T(8,128)(2,1)S(1)} %copy-done.24, bf16[256,256]{1,0:T(8,128)(2,1)S(1)} %collective-permute-done.16.refs_1_, ...), custom_call_target="tpu_custom_call" | custom-call | flops 4600000000 | tf_op jit(solution)/shard_map/pallas_call | solution.py:425
  (86 shorter events, 17.7 us)
Async XLA Ops:
  3.6 76.2 %copy-start.10 = (s32[16]{0:T(128)}, s32[16]{0:T(128)S(1)}, u32[]{:S(2)}) copy-start(s32[16]{0:T(128)S(1)} %select_reduce_fusion.order) | copy-start | bytes 196
  8.4 4.8 %collective-permute-start.1 = (bf16[256,256]{1,0:T(8,128)(2,1)S(1)}, bf16[256,256]{1,0:T(8,128)(2,1)S(1)}, u32[]{:S(2)}, u32[]{:S(2)}) collective-permute-start(bf16[256,256]{1,0:T(8,128)(2,1)S(1)} %get-tuple-element.34), channel_id=1, source_target_pairs={{0,1},{1,0},{2,3},{3,2},{4,5},{5,4},{6,7},{7,6},{8,9},{9,8},{10,11... | collective-permute-start | bytes 393224 | tf_op jit(solution)/shard_map/ppermute | solution.py:404
  8.9 22.5 %collective-permute-start.11 = (bf16[2,256,256]{2,1,0:T(8,128)(2,1)S(1)}, bf16[2,256,256]{2,1,0:T(8,128)(2,1)S(1)}, u32[]{:S(2)}, u32[]{:S(2)}) collective-permute-start(bf16[2,256,256]{2,1,0:T(8,128)(2,1)S(1)} %get-tuple-element.46), channel_id=1, source_target_pairs={{0,1},{1,0},{2,3},{3,2},{4,5},{5,4},{6,7},{7,6},{8,9},{9,8},{10,11... | collective-permute-start | bytes 786440 | tf_op jit(solution)/shard_map/ppermute | solution.py:404
  8.9 23.8 %collective-permute-start.12 = (bf16[2,256,256]{2,1,0:T(8,128)(2,1)S(1)}, bf16[2,256,256]{2,1,0:T(8,128)(2,1)S(1)}, u32[]{:S(2)}, u32[]{:S(2)}) collective-permute-start(bf16[2,256,256]{2,1,0:T(8,128)(2,1)S(1)} %get-tuple-element.47), channel_id=1, source_target_pairs={{0,2},{1,3},{2,0},{3,1},{4,6},{5,7},{6,4},{7,5},{8,10},{9,11},{10,... | collective-permute-start | bytes 786440 | tf_op jit(solution)/shard_map/ppermute | solution.py:404
  11.9 23.3 %collective-permute-start.13 = (bf16[2,256,256]{2,1,0:T(8,128)(2,1)S(1)}, bf16[2,256,256]{2,1,0:T(8,128)(2,1)S(1)}, u32[]{:S(2)}, u32[]{:S(2)}) collective-permute-start(bf16[2,256,256]{2,1,0:T(8,128)(2,1)S(1)} %get-tuple-element.48), channel_id=1, source_target_pairs={{0,3},{1,2},{2,1},{3,0},{4,7},{5,6},{6,5},{7,4},{8,11},{9,10},{10,... | collective-permute-start | bytes 786440 | tf_op jit(solution)/shard_map/ppermute | solution.py:404
  11.9 16.4 %collective-permute-start.2 = (bf16[256,256]{1,0:T(8,128)(2,1)S(1)}, bf16[256,256]{1,0:T(8,128)(2,1)S(1)}, u32[]{:S(2)}, u32[]{:S(2)}) collective-permute-start(bf16[256,256]{1,0:T(8,128)(2,1)S(1)} %get-tuple-element.35), channel_id=1, source_target_pairs={{0,2},{1,3},{2,0},{3,1},{4,6},{5,7},{6,4},{7,5},{8,10},{9,11},{10,... | collective-permute-start | bytes 393224 | tf_op jit(solution)/shard_map/ppermute | solution.py:404
  13.2 16.8 %collective-permute-start.3 = (bf16[256,256]{1,0:T(8,128)(2,1)S(1)}, bf16[256,256]{1,0:T(8,128)(2,1)S(1)}, u32[]{:S(2)}, u32[]{:S(2)}) collective-permute-start(bf16[256,256]{1,0:T(8,128)(2,1)S(1)} %get-tuple-element.36), channel_id=1, source_target_pairs={{0,3},{1,2},{2,1},{3,0},{4,7},{5,6},{6,5},{7,4},{8,11},{9,10},{10,... | collective-permute-start | bytes 393224 | tf_op jit(solution)/shard_map/ppermute | solution.py:404
  14.9 19.1 %copy-start.8 = (s32[16]{0:T(128)S(1)}, s32[16]{0:T(128)}, u32[]{:S(2)}) copy-start(s32[16]{0:T(128)} %windows.7) | copy-start | bytes 196
  14.9 81.1 %all-to-all-start = ((bf16[16,8,512]{2,1,0:T(8,128)(2,1)}), bf16[16,8,512]{2,1,0:T(8,128)(2,1)S(1)}, u32[]{:S(2)}, u32[]{:S(2)}) async-start(bf16[16,8,512]{2,1,0:T(8,128)(2,1)} %shard_map.74), calls=%async_computation | async-start | bytes 262144 | tf_op jit(solution)/shard_map/all_to_all | solution.py:464
  28.2 12.7 %collective-permute-start.6 = (bf16[3,256,256]{2,1,0:T(8,128)(2,1)}, bf16[3,256,256]{2,1,0:T(8,128)(2,1)}, u32[]{:S(2)}, u32[]{:S(2)}) collective-permute-start(bf16[3,256,256]{2,1,0:T(8,128)(2,1)} %get-tuple-element.38), channel_id=1, source_target_pairs={{0,1},{1,0},{2,3},{3,2},{4,5},{5,4},{6,7},{7,6},{8,9},{9,8},{10,11... | collective-permute-start | bytes 1179656 | tf_op jit(solution)/shard_map/ppermute | solution.py:404
  30.1 12.3 %collective-permute-start.7 = (bf16[3,256,256]{2,1,0:T(8,128)(2,1)}, bf16[3,256,256]{2,1,0:T(8,128)(2,1)}, u32[]{:S(2)}, u32[]{:S(2)}) collective-permute-start(bf16[3,256,256]{2,1,0:T(8,128)(2,1)} %get-tuple-element.39), channel_id=1, source_target_pairs={{0,2},{1,3},{2,0},{3,1},{4,6},{5,7},{6,4},{7,5},{8,10},{9,11},{10,... | collective-permute-start | bytes 1179656 | tf_op jit(solution)/shard_map/ppermute | solution.py:404
  31.4 18.6 %collective-permute-start.8 = (bf16[3,256,256]{2,1,0:T(8,128)(2,1)}, bf16[3,256,256]{2,1,0:T(8,128)(2,1)}, u32[]{:S(2)}, u32[]{:S(2)}) collective-permute-start(bf16[3,256,256]{2,1,0:T(8,128)(2,1)} %get-tuple-element.40), channel_id=1, source_target_pairs={{0,3},{1,2},{2,1},{3,0},{4,7},{5,6},{6,5},{7,4},{8,11},{9,10},{10,... | collective-permute-start | bytes 1179656 | tf_op jit(solution)/shard_map/ppermute | solution.py:404
  32.7 18.8 %collective-permute-start.4 = (bf16[4,256,256]{2,1,0:T(8,128)(2,1)S(1)}, bf16[4,256,256]{2,1,0:T(8,128)(2,1)S(1)}, u32[]{:S(2)}, u32[]{:S(2)}) collective-permute-start(bf16[4,256,256]{2,1,0:T(8,128)(2,1)S(1)} %shard_map.68.q), channel_id=1, source_target_pairs={{4,0},{5,1},{6,2},{7,3},{8,4},{9,5},{10,6},{11,7},{12,8},{13,9},{1... | collective-permute-start | bytes 1572872 | tf_op jit(solution)/shard_map/ppermute | solution.py:422
  36.2 13.8 %copy-start.18 = (bf16[3,256,256]{2,1,0:T(8,128)(2,1)S(1)}, bf16[3,256,256]{2,1,0:T(8,128)(2,1)}, u32[]{:S(2)}) copy-start(bf16[3,256,256]{2,1,0:T(8,128)(2,1)} %copy-done.17) | copy-start | bytes 1179652
  36.3 39.8 %collective-permute-start.14 = (bf16[4,2,256,256]{3,2,1,0:T(8,128)(2,1)S(1)}, bf16[4,2,256,256]{3,2,1,0:T(8,128)(2,1)S(1)}, u32[]{:S(2)}, u32[]{:S(2)}) collective-permute-start(bf16[4,2,256,256]{3,2,1,0:T(8,128)(2,1)S(1)} %shard_map.75.kv0), channel_id=1, source_target_pairs={{0,4},{1,5},{2,6},{3,7},{4,8},{5,9},{6,10},{7,11},{8,12},{9,13},{1... | collective-permute-start | bytes 3145736 | tf_op jit(solution)/shard_map/ppermute | solution.py:419
  51.4 28.4 %copy-start.15 = (bf16[4,3,256,256]{3,2,1,0:T(8,128)(2,1)}, bf16[4,3,256,256]{3,2,1,0:T(8,128)(2,1)S(1)}, u32[]{:S(2)}) copy-start(bf16[4,3,256,256]{3,2,1,0:T(8,128)(2,1)S(1)} %shard_map.69.kv.rest) | copy-start | bytes 4718596
  51.5 16.2 %collective-permute-start.5 = (bf16[4,256,256]{2,1,0:T(8,128)(2,1)S(1)}, bf16[4,256,256]{2,1,0:T(8,128)(2,1)S(1)}, u32[]{:S(2)}, u32[]{:S(2)}) collective-permute-start(bf16[4,256,256]{2,1,0:T(8,128)(2,1)S(1)} %collective-permute-done.4.q), channel_id=1, source_target_pairs={{4,0},{5,1},{6,2},{7,3},{8,4},{9,5},{10,6},{11,7},{12,8},{13,9},{1... | collective-permute-start | bytes 1572872 | tf_op jit(solution)/shard_map/ppermute | solution.py:422
  57.7 14.6 %copy-start.21 = (f32[2,128,1024]{2,1,0:T(8,128)}, f32[2,128,1024]{2,1,0:T(8,128)S(1)}, u32[]{:S(2)}) copy-start(f32[2,128,1024]{2,1,0:T(8,128)S(1)} %get-tuple-element.43.sums) | copy-start | bytes 3145732
  72.4 17.3 %collective-permute-start.9 = (bf16[2,144,1024]{2,1,0:T(8,128)(2,1)S(1)}, bf16[2,144,1024]{2,1,0:T(8,128)(2,1)S(1)}, u32[]{:S(2)}, u32[]{:S(2)}) collective-permute-start(bf16[2,144,1024]{2,1,0:T(8,128)(2,1)S(1)} %shard_map.70), channel_id=1, source_target_pairs={{0,4},{1,5},{2,6},{3,7},{4,8},{5,9},{6,10},{7,11},{8,12},{9,13},{1... | collective-permute-start | bytes 1769480 | tf_op jit(solution)/shard_map/ppermute | solution.py:419
  77.1 23.9 %collective-permute-start.15 = (bf16[2,2,256,256]{3,2,1,0:T(8,128)(2,1)}, bf16[2,2,256,256]{3,2,1,0:T(8,128)(2,1)}, u32[]{:S(2)}, u32[]{:S(2)}) collective-permute-start(bf16[2,2,256,256]{3,2,1,0:T(8,128)(2,1)} %get-tuple-element.60), channel_id=1, source_target_pairs={{0,4},{1,5},{2,6},{3,7},{4,8},{5,9},{6,10},{7,11},{8,12},{9,13},{1... | collective-permute-start | bytes 1572872 | tf_op jit(solution)/shard_map/ppermute | solution.py:419
  86.7 14.4 %copy-start.7 = (f32[2048]{0:T(1024)S(1)}, f32[2048]{0:T(1024)}, u32[]{:S(2)}) copy-start(f32[2048]{0:T(1024)} %param.9) | copy-start | bytes 24580
  86.7 14.4 %copy-start.9 = (s32[16]{0:T(128)S(1)}, s32[16]{0:T(128)}, u32[]{:S(2)}) copy-start(s32[16]{0:T(128)} %starts.3) | copy-start | bytes 196
  91.3 19.5 %collective-permute-start.10 = (bf16[2,144,1024]{2,1,0:T(8,128)(2,1)S(1)}, bf16[2,144,1024]{2,1,0:T(8,128)(2,1)S(1)}, u32[]{:S(2)}, u32[]{:S(2)}) collective-permute-start(bf16[2,144,1024]{2,1,0:T(8,128)(2,1)S(1)} %shard_map.72), channel_id=1, source_target_pairs={{0,4},{1,5},{2,6},{3,7},{4,8},{5,9},{6,10},{7,11},{8,12},{9,13},{1... | collective-permute-start | bytes 1769480 | tf_op jit(solution)/shard_map/ppermute | solution.py:419
  110.8 26.9 %copy-start.6 = (bf16[3,8,2048]{2,1,0:T(8,128)(2,1)S(1)}, bf16[3,8,2048]{2,1,0:T(8,128)(2,1)}, u32[]{:S(2)}) copy-start(bf16[3,8,2048]{2,1,0:T(8,128)(2,1)} %cont.1) | copy-start | bytes 294916
  110.8 26.9 %copy-start.12 = (s32[16]{0:T(128)S(1)}, s32[16]{0:T(128)}, u32[]{:S(2)}) copy-start(s32[16]{0:T(128)} %copy-done.10) | copy-start | bytes 196
  113.7 24.0 %all-to-all-start.1 = ((bf16[16,8,768]{2,1,0:T(8,128)(2,1)}), bf16[16,8,768]{2,1,0:T(8,128)(2,1)S(1)}, u32[]{:S(2)}, u32[]{:S(2)}) async-start(bf16[16,8,768]{2,1,0:T(8,128)(2,1)} %get-tuple-element.50), calls=%async_computation.1 | async-start | bytes 393216 | tf_op jit(solution)/shard_map/all_to_all | solution.py:516
  121.6 4.2 %collective-permute-start.16 = (bf16[256,256]{1,0:T(8,128)(2,1)}, bf16[256,256]{1,0:T(8,128)(2,1)S(1)}, u32[]{:S(2)}, u32[]{:S(2)}) collective-permute-start(bf16[256,256]{1,0:T(8,128)(2,1)} %copy-done.4), channel_id=1, source_target_pairs={{0,1},{1,0},{2,3},{3,2},{4,5},{5,4},{6,7},{7,6},{8,9},{9,8},{10,11... | collective-permute-start | bytes 393224 | tf_op jit(solution)/shard_map/ppermute | solution.py:404
  122.0 8.0 %collective-permute-start.17 = (bf16[256,256]{1,0:T(8,128)(2,1)}, bf16[256,256]{1,0:T(8,128)(2,1)S(1)}, u32[]{:S(2)}, u32[]{:S(2)}) collective-permute-start(bf16[256,256]{1,0:T(8,128)(2,1)} %copy-done.3), channel_id=1, source_target_pairs={{0,2},{1,3},{2,0},{3,1},{4,6},{5,7},{6,4},{7,5},{8,10},{9,11},{10,... | collective-permute-start | bytes 393224 | tf_op jit(solution)/shard_map/ppermute | solution.py:404
  123.6 8.5 %collective-permute-start.18 = (bf16[256,256]{1,0:T(8,128)(2,1)S(1)}, bf16[256,256]{1,0:T(8,128)(2,1)S(1)}, u32[]{:S(2)}, u32[]{:S(2)}) collective-permute-start(bf16[256,256]{1,0:T(8,128)(2,1)S(1)} %get-tuple-element.54), channel_id=1, source_target_pairs={{0,3},{1,2},{2,1},{3,0},{4,7},{5,6},{6,5},{7,4},{8,11},{9,10},{10,... | collective-permute-start | bytes 393224 | tf_op jit(solution)/shard_map/ppermute | solution.py:404
  123.6 8.5 %collective-permute-start.19 = (bf16[256,256]{1,0:T(8,128)(2,1)S(1)}, bf16[256,256]{1,0:T(8,128)(2,1)S(1)}, u32[]{:S(2)}, u32[]{:S(2)}) collective-permute-start(bf16[256,256]{1,0:T(8,128)(2,1)S(1)} %get-tuple-element.56), channel_id=1, source_target_pairs={{0,1},{1,0},{2,3},{3,2},{4,5},{5,4},{6,7},{7,6},{8,9},{9,8},{10,11... | collective-permute-start | bytes 393224 | tf_op jit(solution)/shard_map/ppermute | solution.py:404
  124.1 11.6 %collective-permute-start.20 = (bf16[256,256]{1,0:T(8,128)(2,1)S(1)}, bf16[256,256]{1,0:T(8,128)(2,1)S(1)}, u32[]{:S(2)}, u32[]{:S(2)}) collective-permute-start(bf16[256,256]{1,0:T(8,128)(2,1)S(1)} %get-tuple-element.57), channel_id=1, source_target_pairs={{0,2},{1,3},{2,0},{3,1},{4,6},{5,7},{6,4},{7,5},{8,10},{9,11},{10,... | collective-permute-start | bytes 393224 | tf_op jit(solution)/shard_map/ppermute | solution.py:404
  125.8 11.9 %collective-permute-start.21 = (bf16[256,256]{1,0:T(8,128)(2,1)S(1)}, bf16[256,256]{1,0:T(8,128)(2,1)S(1)}, u32[]{:S(2)}, u32[]{:S(2)}) collective-permute-start(bf16[256,256]{1,0:T(8,128)(2,1)S(1)} %get-tuple-element.58), channel_id=1, source_target_pairs={{0,3},{1,2},{2,1},{3,0},{4,7},{5,6},{6,5},{7,4},{8,11},{9,10},{10,... | collective-permute-start | bytes 393224 | tf_op jit(solution)/shard_map/ppermute | solution.py:404
  (18 other events, 64.1 us)

commit v4 on v3

--- a/solution.py
+++ b/solution.py
@@ -201,24 +201,53 @@
     acc[...] = jnp.zeros(acc.shape, F32)
 
 
-def far_kernel(dims, axis, order, windows, rest, kv0, kv1, kv2, kv3, rows, starts, gain, *refs):
+def load(sources, kv, sems):
+    copies, start = [], 0
+    for k, source in enumerate(sources):
+        copies.append(pltpu.make_async_copy(source, kv.at[pl.ds(start, source.shape[0])], sems.at[k]))
+        start += source.shape[0]
+    for copy in copies:
+        copy.start()
+    for copy in copies:
+        copy.wait()
+
+
+def far_start_kernel(dims, axis, order, windows, rest, kv0, kv1, sums, stats, kv, peak, total, acc, sems):
+    group, slots, near, head_dim, block = dims
+    device = lax.axis_index(axis)
+    row = device // group
+    mine = lax.rem(device, group) * slots + near
+    load((kv1, kv0), kv, sems)
+    parts = sums.shape[2] // block
+    heads = slots - near
+    spans = [windows[order[mine + head]] for head in range(heads)]
+
+    def pick(start, size, column):
+        return rest[pl.ds(start, size), 2, :, column]
+
+    def one(part, carry):
+        span = pl.ds(pl.multiple_of(part * block, block), block)
+        reset(peak, total, acc)
+        attend(kv, pick, spans, part, parts, row * parts + part, 2 * parts, (peak, total, acc), block, head_dim)
+        for head in range(heads):
+            sums[head, :, span] = acc[head]
+            stats[head, 0:1, span] = peak[head, 0:1, :]
+            stats[head, 1:2, span] = total[head, 0:1, :]
+        return carry
+
+    lax.fori_loop(0, parts, one, 0)
+
+
+def far_kernel(dims, axis, order, windows, starts, rest, rows, gain, sums, stats, kv2, kv3, *refs):
     group, slots, near, head_dim, block = dims
     outs, (result, out, kv, peak, total, acc, sems) = refs[:group], refs[group:]
     device = lax.axis_index(axis)
     row = device // group
     mine = lax.rem(device, group) * slots + near
-    copies, start = [], 0
-    for k, source in enumerate((kv3, kv2, kv1, kv0)):
-        copies.append(pltpu.make_async_copy(source, kv.at[pl.ds(start, source.shape[0])], sems.at[k]))
-        start += source.shape[0]
-    for copy in copies[::-1]:
-        copy.start()
-    for copy in copies[::-1]:
-        copy.wait()
+    load((kv3, kv2), kv, sems)
     length = out.shape[1]
     parts = group * length // block
     shards = block // length
-
     heads = slots - near
     spans = [windows[order[mine + head]] for head in range(heads)]
 
@@ -226,8 +255,12 @@
         return rest[pl.ds(start, size), 2, :, column]
 
     def one(part, carry):
-        reset(peak, total, acc)
-        attend(kv, pick, spans, part, 2 * parts, row * parts + part, 3 * parts, (peak, total, acc), block, head_dim)
+        span = pl.ds(pl.multiple_of(part * block, block), block)
+        for head in range(heads):
+            peak[head, 0:1, :] = stats[head, 0:1, span]
+            total[head, 0:1, :] = stats[head, 1:2, span]
+            acc[head] = sums[head, :, span]
+        attend(kv, pick, spans, part, 2 * parts, row * parts + part, parts, (peak, total, acc), block, head_dim)
         for head in range(heads):
             done = (acc[head] / total[head, 0:1, :]).astype(BF16).T
             column = slice(head * head_dim, (head + 1) * head_dim)
@@ -246,6 +279,8 @@
     mine = lax.rem(device, group) * slots
     length = q.shape[1]
     parts = group * length // block
+    if delta == 1:
+        refs = refs[1:]
     if delta == 2:
         state, peak, total, acc = refs
     else:
@@ -480,31 +515,45 @@
     state_shape = shape(near, head_dim + 16, group * length)
     local_shape = (shape(near, head_dim, group * length, dtype=F32), shape(near, 8, group * length, dtype=F32))
 
-    def near_step(delta, q):
+    def near_step(delta, q, *more):
         return call(
             functools.partial(near_kernel, big, axis, delta, count), 7,
-            state_shape if delta == 2 else local_shape, order, windows, q, rest0, scratch_shapes=state_scratch,
+            state_shape if delta == 2 else local_shape, order, windows, q, rest0, *more, scratch_shapes=state_scratch,
         )
 
     def merge(kernel, micros, shapes, *operands, **more):
         return call(functools.partial(kernel, big, axis), micros, shapes, *operands, **more)
 
     state2 = up(near_step(2, q_near2))
-    state1 = up(merge(merge_kernel, 1, state_shape, state2, *near_step(1, q_near1), smem=0))
+    state1 = up(merge(merge_kernel, 1, state_shape, state2, *near_step(1, q_near1, rows), smem=0))
     local0 = near_step(0, q_near0)
 
-    *far_out, far_cross = pl.pallas_call(
-        functools.partial(far_kernel, big, axis),
-        out_shape=(shape(length, distant),) * group + (shape(devices, rows_here, distant + head_dim),),
-        in_specs=[SMEM, SMEM, VMEM, ANY, ANY, ANY, ANY, VMEM, SMEM, VMEM],
-        out_specs=(VMEM,) * (group + 1),
-        scratch_shapes=[pltpu.VMEM((group, length, distant), BF16), pltpu.VMEM((3 * group, 2, length, distant), BF16)]
-        + state_scratch
-        + [pltpu.SemaphoreType.DMA((4,))],
-        name="far",
-        cost_estimate=cost(14),
-        compiler_params=GRANT,
-    )(order, windows, rest0, kv_far0, kv_far1, kv_far2, kv_far3, rows, starts, gain)
+    def far_call(kernel, micros, shapes, specs, pieces_here, more, *operands):
+        return pl.pallas_call(
+            functools.partial(kernel, big, axis),
+            out_shape=shapes,
+            in_specs=specs,
+            out_specs=jax.tree.map(lambda _: VMEM, shapes),
+            scratch_shapes=more
+            + [pltpu.VMEM((pieces_here * group, 2, length, distant), BF16)]
+            + state_scratch
+            + [pltpu.SemaphoreType.DMA((2,))],
+            cost_estimate=cost(micros),
+            compiler_params=GRANT,
+        )(*operands)
+
+    begun = far_call(
+        far_start_kernel, 8,
+        (shape(far, head_dim, group * length, dtype=F32), shape(far, 8, group * length, dtype=F32)),
+        [SMEM, SMEM, VMEM, ANY, ANY], 2, [], order, windows, rest0, kv_far0, kv_far1,
+    )
+    *far_out, far_cross = far_call(
+        far_kernel, 5,
+        (shape(length, distant),) * group + (shape(devices, rows_here, distant + head_dim),),
+        [SMEM, SMEM, SMEM, VMEM, VMEM, VMEM, VMEM, VMEM, ANY, ANY], 1,
+        [pltpu.VMEM((group, length, distant), BF16)],
+        order, windows, starts, rest0, rows, gain, *begun, kv_far2, kv_far3,
+    )
     far_back = exchange(far_out)
     *near_out, cross = merge(
         last_kernel, 4,

time: 142 us -> 138 us (0.972)
  waiting for transfers between devices: 48.8 us -> 45.3 us
  starting transfers between devices: 43.7 us -> 40.4 us
  local copies, waits for them, and re-layouts: 11.2 us -> 12.8 us
    ppermute x4, waiting for transfers between devices: 8.87 us -> 5.8 us  [up(): lax.ppermute(value, axis, [(k, k + group) for k in range(devices - group)])]
    all_to_all x1, starting transfers between devices: 7.89 us -> 4.84 us  [per_device(): cross = lax.all_to_all(cross, axis, 0, 0, tiled=True)]
    unnamed x54 -> x48, local copies, waits for them, and re-layouts: 10.1 us -> 11.8 us
    pallas_call x1 -> x2, Pallas kernels: 6.92 us -> 7.63 us  [far_call(): pl.pallas_call(functools.partial(kernel, big, axis), out_shape=shapes, in...]
  transfers between devices with their start and end apart: 23 -> 23, of which waited for: 12 -> 12; matrix products, arithmetic and copies ran while one was open for 1% -> 1% of each run, Pallas kernels for 18% -> 19%
where the time goes in v4:
time: 138 us; the launch traced here: 137 us
  waiting for transfers between devices  45.3 us (33%)
  starting transfers between devices  40.4 us (29%)
  Pallas kernels  35.6 us (26%)
  local copies, waits for them, and re-layouts  12.8 us (9%)
  other arithmetic  1.68 us (1%)
  between operations  1.61 us (1%)
    ppermute x15, waiting for transfers between devices, exchange(): lax.ppermute(blocks[k], axis, [(source, source ^ k) for source in range(d...  29.6 us
    pallas_call x7, Pallas kernels, call(): pl.pallas_call(kernel, out_shape=shapes, in_specs=[SMEM] * smem + [VMEM]...  22.3 us
    ppermute x4, starting transfers between devices, up(): lax.ppermute(value, axis, [(k, k + group) for k in range(devices - group)])  15.4 us
    unnamed x48, local copies, waits for them, and re-layouts  11.8 us
    ppermute x15, starting transfers between devices, exchange(): lax.ppermute(blocks[k], axis, [(source, source ^ k) for source in range(d...  11.3 us
    ppermute x2, waiting for transfers between devices, down(): lax.ppermute(value, axis, [(k + group, k) for k in range(devices - group)])  9.97 us
    pallas_call x2, Pallas kernels, far_call(): pl.pallas_call(functools.partial(kernel, big, axis), out_shape=shapes, in...  7.63 us
    all_to_all x1, starting transfers between devices, per_device(): rows = lax.all_to_all(rows_sent, axis, 0, 0, tiled=True)  6.29 us
  transfers between devices with their start and end apart: 23, of which 12 were waited for; matrix products, arithmetic and copies ran while one was open for 1% of the time, Pallas kernels for 19%

profile of v4, /device:TPU:0, one launch (start us, length us, event | category | flops | bytes accessed | tf_op | source)
XLA Modules:
  0.0 137.5 jit_solution(16074222373828575475)
XLA Ops:
  1.7 1.9 %copy-done = bf16[3,256,2048]{2,1,0:T(8,128)(2,1)S(1)} copy-done((bf16[3,256,2048]{2,1,0:T(8,128)(2,1)S(1)}, bf16[3,256,2048]{2,1,0:T(8,128)(2,1)}, u32[]{:S(2)}) %copy-start) | copy-done | bytes 3145752
  3.6 3.4 %pack.1 = (bf16[2,256,256]{2,1,0:T(8,128)(2,1)S(1)}, bf16[2,256,256]{2,1,0:T(8,128)(2,1)S(1)}, bf16[2,256,256]{2,1,0:T(8,128)(2,1)S(1)}, bf16[2,256,256]{2,1,0:T...) custom-call(s32[16]{0:T(128)S(1)} %select_reduce_fusion.order, ...), custom_call_target="tpu_custom_call" | custom-call | flops 4600000000 | tf_op jit(solution)/shard_map/pack/pallas_call | solution.py:473
  8.9 3.0 %collective-permute-start.12 = (bf16[2,256,256]{2,1,0:T(8,128)(2,1)S(1)}, bf16[2,256,256]{2,1,0:T(8,128)(2,1)S(1)}, u32[]{:S(2)}, u32[]{:S(2)}) collective-permute-start(bf16[2,256,256]{2,1,0:T(8,128)(2,1)S(1)} %get-tuple-element.49), channel_id=1, source_target_pairs={{0,2},{1,3},{2,0},{3,1},{4,6},{5,7},{6,4},{7,5},{8,10},{9,11},{10,... | collective-permute-start | bytes 786440 | tf_op jit(solution)/shard_map/ppermute | solution.py:439
  14.9 6.3 %all-to-all-start = ((bf16[16,8,512]{2,1,0:T(8,128)(2,1)}), bf16[16,8,512]{2,1,0:T(8,128)(2,1)S(1)}, u32[]{:S(2)}, u32[]{:S(2)}) async-start(bf16[16,8,512]{2,1,0:T(8,128)(2,1)} %shard_map.71), calls=%async_computation | async-start | bytes 262144 | tf_op jit(solution)/shard_map/all_to_all | solution.py:499
  21.2 7.1 %collective-permute-done.2.refs_2_ = bf16[256,256]{1,0:T(8,128)(2,1)S(1)} collective-permute-done((bf16[256,256]{1,0:T(8,128)(2,1)S(1)}, bf16[256,256]{1,0:T(8,128)(2,1)S(1)}, u32[]{:S(2)}, u32[]{:S(2)}) %collective-permute-start.2) | collective-permute-done | bytes 131104 | tf_op jit(solution)/shard_map/ppermute | solution.py:439
  28.3 1.8 %collective-permute-done.3.refs_3_ = bf16[256,256]{1,0:T(8,128)(2,1)S(1)} collective-permute-done((bf16[256,256]{1,0:T(8,128)(2,1)S(1)}, bf16[256,256]{1,0:T(8,128)(2,1)S(1)}, u32[]{:S(2)}, u32[]{:S(2)}) %collective-permute-start.3) | collective-permute-done | bytes 131104 | tf_op jit(solution)/shard_map/ppermute | solution.py:439
  36.4 4.6 %collective-permute-start.14 = (bf16[4,2,256,256]{3,2,1,0:T(8,128)(2,1)S(1)}, bf16[4,2,256,256]{3,2,1,0:T(8,128)(2,1)S(1)}, u32[]{:S(2)}, u32[]{:S(2)}) collective-permute-start(bf16[4,2,256,256]{3,2,1,0:T(8,128)(2,1)S(1)} %shard_map.75.kv0), channel_id=1, source_target_pairs={{0,4},{1,5},{2,6},{3,7},{4,8},{5,9},{6,10},{7,11},{8,12},{9,13},{1... | collective-permute-start | bytes 3145736 | tf_op jit(solution)/shard_map/ppermute | solution.py:454
  41.0 1.4 collective-permute-done.7.refs_2_
  42.4 7.6 %collective-permute-done.8.refs_3_ = bf16[3,256,256]{2,1,0:T(8,128)(2,1)} collective-permute-done((bf16[3,256,256]{2,1,0:T(8,128)(2,1)}, bf16[3,256,256]{2,1,0:T(8,128)(2,1)}, u32[]{:S(2)}, u32[]{:S(2)}) %collective-permute-start.8) | collective-permute-done | bytes 393248 | tf_op jit(solution)/shard_map/ppermute | solution.py:439
  50.0 1.4 %shard_map.69.kv.rest = bf16[4,3,256,256]{3,2,1,0:T(8,128)(2,1)S(1)} custom-call(bf16[3,256,256]{2,1,0:T(8,128)(2,1)S(1)} %copy-done.13, bf16[3,256,256]{2,1,0:T(8,128)(2,1)} %collective-permute-done.6.refs_1_, bf16[3,256,256]{2,1,0:T(8,128)(2,1)} %collective-permute-done.7.refs_2_, bf16[3,256,256]{2,1,0:T(8,128)(2,1)} %collective-permute-done.8.refs_3_), custom_call_target="tpu_custom_call" | custom-call | flops 2300000000 | tf_op jit(solution)/shard_map/pallas_call | solution.py:443
  52.8 4.3 %shard_map.74 = (f32[2,128,1024]{2,1,0:T(8,128)S(1)}, f32[2,8,1024]{2,1,0:T(8,128)S(1)}) custom-call(s32[16]{0:T(128)S(1)} %select_reduce_fusion.order, s32[16]{0:T(128)S(1)} %copy-done.6, bf16[4,256,256]{2,1,0:T(8,128)(2,1)S(1)} %shard_map.68.q, bf16[4,3,256,256]{3,2,1,0:T(8,128)(2,1)S(1)} %shard_map.69.kv.rest), custom_call_target="tpu_custom_call" | custom-call | flops 8049999872 | tf_op jit(solution)/shard_map/pallas_call | solution.py:460
  57.8 10.0 %collective-permute-done.5.q = bf16[4,256,256]{2,1,0:T(8,128)(2,1)S(1)} collective-permute-done((bf16[4,256,256]{2,1,0:T(8,128)(2,1)S(1)}, bf16[4,256,256]{2,1,0:T(8,128)(2,1)S(1)}, u32[]{:S(2)}, u32[]{:S(2)}) %collective-permute-start.5) | collective-permute-done | bytes 524320 | tf_op jit(solution)/shard_map/ppermute | solution.py:457
  67.7 4.6 %shard_map.70 = bf16[2,144,1024]{2,1,0:T(8,128)(2,1)S(1)} custom-call(s32[16]{0:T(128)S(1)} %select_reduce_fusion.order, s32[16]{0:T(128)S(1)} %copy-done.6, bf16[4,256,256]{2,1,0:T(8,128)(2,1)S(1)} %collective-permute-done.5.q, bf16[4,3,256,256]{3,2,1,0:T(8,128)(2,1)S(1)} %shard_map.69.kv.rest), custom_call_target="tpu_custom_call" | custom-call | flops 8049999872 | tf_op jit(solution)/shard_map/pallas_call | solution.py:460
  72.4 3.7 %collective-permute-start.9 = (bf16[2,144,1024]{2,1,0:T(8,128)(2,1)S(1)}, bf16[2,144,1024]{2,1,0:T(8,128)(2,1)S(1)}, u32[]{:S(2)}, u32[]{:S(2)}) collective-permute-start(bf16[2,144,1024]{2,1,0:T(8,128)(2,1)S(1)} %shard_map.70), channel_id=1, source_target_pairs={{0,4},{1,5},{2,6},{3,7},{4,8},{5,9},{6,10},{7,11},{8,12},{9,13},{1... | collective-permute-start | bytes 1769480 | tf_op jit(solution)/shard_map/ppermute | solution.py:454
  77.1 1.4 %copy-done.9 = bf16[4,3,256,256]{3,2,1,0:T(8,128)(2,1)S(1)} copy-done((bf16[4,3,256,256]{3,2,1,0:T(8,128)(2,1)S(1)}, bf16[4,3,256,256]{3,2,1,0:T(8,128)(2,1)}, u32[]{:S(2)}) %copy-start.9) | copy-done | bytes 1572888
  78.5 5.8 %shard_map.72 = (f32[2,128,1024]{2,1,0:T(8,128)S(1)}, f32[2,8,1024]{2,1,0:T(8,128)S(1)}) custom-call(s32[16]{0:T(128)S(1)} %select_reduce_fusion.order, s32[16]{0:T(128)S(1)} %copy-done.6, bf16[4,256,256]{2,1,0:T(8,128)(2,1)S(1)} %copy-done.2, bf16[4,3,256,256]{3,2,1,0:T(8,128)(2,1)S(1)} %copy-done.9, bf16[16,8,512]{2,1,0:T(8,128)(2,1)S(1)} %all-to-all-done.refs_0_.rows), custom_call_target="tpu_custom_call" | custom-call | flops 8049999872 | tf_op jit(solution)/shard_map/pallas_call | solution.py:460
  85.4 2.7 %collective-permute-start.15 = (bf16[2,2,256,256]{3,2,1,0:T(8,128)(2,1)}, bf16[2,2,256,256]{3,2,1,0:T(8,128)(2,1)}, u32[]{:S(2)}, u32[]{:S(2)}) collective-permute-start(bf16[2,2,256,256]{3,2,1,0:T(8,128)(2,1)} %get-tuple-element.64), channel_id=1, source_target_pairs={{0,4},{1,5},{2,6},{3,7},{4,8},{5,9},{6,10},{7,11},{8,12},{9,13},{1... | collective-permute-start | bytes 1572872 | tf_op jit(solution)/shard_map/ppermute | solution.py:454
  88.6 4.4 %collective-permute-start.10 = (bf16[2,144,1024]{2,1,0:T(8,128)(2,1)S(1)}, bf16[2,144,1024]{2,1,0:T(8,128)(2,1)S(1)}, u32[]{:S(2)}, u32[]{:S(2)}) collective-permute-start(bf16[2,144,1024]{2,1,0:T(8,128)(2,1)S(1)} %shard_map.73), channel_id=1, source_target_pairs={{0,4},{1,5},{2,6},{3,7},{4,8},{5,9},{6,10},{7,11},{8,12},{9,13},{1... | collective-permute-start | bytes 1769480 | tf_op jit(solution)/shard_map/ppermute | solution.py:454
  93.0 4.4 %shard_map.76 = (f32[2,128,1024]{2,1,0:T(8,128)S(1)}, f32[2,8,1024]{2,1,0:T(8,128)S(1)}) custom-call(s32[16]{0:T(128)S(1)} %select_reduce_fusion.order, s32[16]{0:T(128)S(1)} %copy-done.6, bf16[4,3,256,256]{3,2,1,0:T(8,128)(2,1)S(1)} %copy-done.10, bf16[4,2,256,256]{3,2,1,0:T(8,128)(2,1)S(1)} %shard_map.75.kv0, ...), custom_call_target="tpu_custom_call" | custom-call | flops 9200000000 | tf_op jit(solution)/shard_map/pallas_call | solution.py:532
  98.4 1.5 %collective-permute-done.15.kv2 = bf16[2,2,256,256]{3,2,1,0:T(8,128)(2,1)} collective-permute-done((bf16[2,2,256,256]{3,2,1,0:T(8,128)(2,1)}, bf16[2,2,256,256]{3,2,1,0:T(8,128)(2,1)}, u32[]{:S(2)}, u32[]{:S(2)}) %collective-permute-start.15) | collective-permute-done | bytes 524320 | tf_op jit(solution)/shard_map/ppermute | solution.py:454
  99.9 1.4 %copy-done.11 = bf16[4,3,256,256]{3,2,1,0:T(8,128)(2,1)S(1)} copy-done((bf16[4,3,256,256]{3,2,1,0:T(8,128)(2,1)S(1)}, bf16[4,3,256,256]{3,2,1,0:T(8,128)(2,1)}, u32[]{:S(2)}) %copy-start.11) | copy-done | bytes 1572888
  103.4 3.2 %shard_map.77 = (bf16[256,256]{1,0:T(8,128)(2,1)S(1)}, bf16[256,256]{1,0:T(8,128)(2,1)S(1)}, bf16[256,256]{1,0:T(8,128)(2,1)S(1)}, bf16[256,256]{1,0:T(8,128)(2,1)S(1)}, bf16[16,8,384]{2,1,0:T(8,128)(2,1)S(1)}) custom-call(s32[16]{0:T(128)S(1)} %select_reduce_fusion.order, s32[16]{0:T(128)S(1)} %copy-done.6, s32[16]{0:T(128)S(1)} %copy-done.7, ...), custom_call_target="tpu_custom_call" | custom-call | flops 5750000128 | tf_op jit(solution)/shard_map/pallas_call | solution.py:532
  106.6 4.3 %collective-permute-done.10.arrived = bf16[2,144,1024]{2,1,0:T(8,128)(2,1)S(1)} collective-permute-done((bf16[2,144,1024]{2,1,0:T(8,128)(2,1)S(1)}, bf16[2,144,1024]{2,1,0:T(8,128)(2,1)S(1)}, u32[]{:S(2)}, u32[]{:S(2)}) %collective-permute-start.10) | collective-permute-done | bytes 589856 | tf_op jit(solution)/shard_map/ppermute | solution.py:454
  110.8 2.9 %shard_map.78 = (bf16[256,256]{1,0:T(8,128)(2,1)S(1)}, bf16[256,256]{1,0:T(8,128)(2,1)S(1)}, bf16[256,256]{1,0:T(8,128)(2,1)S(1)}, bf16[256,256]{1,0:T(8,128)(2,1)S(1)}, bf16[16,8,768]{2,1,0:T(8,128)(2,1)}) custom-call(s32[16]{0:T(128)S(1)} %select_reduce_fusion.order, s32[16]{0:T(128)S(1)} %copy-done.7, ...), custom_call_target="tpu_custom_call" | custom-call | flops 4600000000 | tf_op jit(solution)/shard_map/pallas_call | solution.py:460
  113.7 4.8 %all-to-all-start.1 = ((bf16[16,8,768]{2,1,0:T(8,128)(2,1)}), bf16[16,8,768]{2,1,0:T(8,128)(2,1)S(1)}, u32[]{:S(2)}, u32[]{:S(2)}) async-start(bf16[16,8,768]{2,1,0:T(8,128)(2,1)} %get-tuple-element.54), calls=%async_computation.1 | async-start | bytes 393216 | tf_op jit(solution)/shard_map/all_to_all | solution.py:565
  118.9 1.6 %collective-permute-start.17 = (bf16[256,256]{1,0:T(8,128)(2,1)S(1)}, bf16[256,256]{1,0:T(8,128)(2,1)S(1)}, u32[]{:S(2)}, u32[]{:S(2)}) collective-permute-start(bf16[256,256]{1,0:T(8,128)(2,1)S(1)} %get-tuple-element.57), channel_id=1, source_target_pairs={{0,2},{1,3},{2,0},{3,1},{4,6},{5,7},{6,4},{7,5},{8,10},{9,11},{10,... | collective-permute-start | bytes 393224 | tf_op jit(solution)/shard_map/ppermute | solution.py:439
  121.1 1.6 %collective-permute-start.20 = (bf16[256,256]{1,0:T(8,128)(2,1)S(1)}, bf16[256,256]{1,0:T(8,128)(2,1)S(1)}, u32[]{:S(2)}, u32[]{:S(2)}) collective-permute-start(bf16[256,256]{1,0:T(8,128)(2,1)S(1)} %get-tuple-element.61), channel_id=1, source_target_pairs={{0,2},{1,3},{2,0},{3,1},{4,6},{5,7},{6,4},{7,5},{8,10},{9,11},{10,... | collective-permute-start | bytes 393224 | tf_op jit(solution)/shard_map/ppermute | solution.py:439
  122.7 4.2 %collective-permute-done.17.refs_2_ = bf16[256,256]{1,0:T(8,128)(2,1)S(1)} collective-permute-done((bf16[256,256]{1,0:T(8,128)(2,1)S(1)}, bf16[256,256]{1,0:T(8,128)(2,1)S(1)}, u32[]{:S(2)}, u32[]{:S(2)}) %collective-permute-start.17) | collective-permute-done | bytes 131104 | tf_op jit(solution)/shard_map/ppermute | solution.py:439
  127.0 1.8 %collective-permute-done.18.refs_3_ = bf16[256,256]{1,0:T(8,128)(2,1)S(1)} collective-permute-done((bf16[256,256]{1,0:T(8,128)(2,1)S(1)}, bf16[256,256]{1,0:T(8,128)(2,1)S(1)}, u32[]{:S(2)}, u32[]{:S(2)}) %collective-permute-start.18) | collective-permute-done | bytes 131104 | tf_op jit(solution)/shard_map/ppermute | solution.py:439
  128.8 4.0 %collective-permute-done.20.refs_6_ = bf16[256,256]{1,0:T(8,128)(2,1)S(1)} collective-permute-done((bf16[256,256]{1,0:T(8,128)(2,1)S(1)}, bf16[256,256]{1,0:T(8,128)(2,1)S(1)}, u32[]{:S(2)}, u32[]{:S(2)}) %collective-permute-start.20) | collective-permute-done | bytes 131104 | tf_op jit(solution)/shard_map/ppermute | solution.py:439
  132.7 1.7 %collective-permute-done.21.refs_7_ = bf16[256,256]{1,0:T(8,128)(2,1)S(1)} collective-permute-done((bf16[256,256]{1,0:T(8,128)(2,1)S(1)}, bf16[256,256]{1,0:T(8,128)(2,1)S(1)}, u32[]{:S(2)}, u32[]{:S(2)}) %collective-permute-start.21) | collective-permute-done | bytes 131104 | tf_op jit(solution)/shard_map/ppermute | solution.py:439
  134.4 3.1 %shard_map.79 = (bf16[256,2048]{1,0:T(8,128)(2,1)}, bf16[8,2048]{1,0:T(8,128)(2,1)}) custom-call(s32[16]{0:T(128)S(1)} %select_reduce_fusion.order, bf16[4,4,8,768]{3,2,1,0:T(8,128)(2,1)S(1)} %bitcast.2, bf16[3,8,2048]{2,1,0:T(8,128)(2,1)S(1)} %copy-done.4, bf16[256,256]{1,0:T(8,128)(2,1)S(1)} %get-tuple-element.55.refs_0_, ...), custom_call_target="tpu_custom_call" | custom-call | flops 4600000000 | tf_op jit(solution)/shard_map/pallas_call | solution.py:460
  (81 shorter events, 20.0 us)
Async XLA Ops:
  3.6 10.1 %copy-start.3 = (bf16[3,8,2048]{2,1,0:T(8,128)(2,1)S(1)}, bf16[3,8,2048]{2,1,0:T(8,128)(2,1)}, u32[]{:S(2)}) copy-start(bf16[3,8,2048]{2,1,0:T(8,128)(2,1)} %cont.1) | copy-start | bytes 294916
  8.4 4.8 %collective-permute-start.1 = (bf16[256,256]{1,0:T(8,128)(2,1)S(1)}, bf16[256,256]{1,0:T(8,128)(2,1)S(1)}, u32[]{:S(2)}, u32[]{:S(2)}) collective-permute-start(bf16[256,256]{1,0:T(8,128)(2,1)S(1)} %get-tuple-element.36), channel_id=1, source_target_pairs={{0,1},{1,0},{2,3},{3,2},{4,5},{5,4},{6,7},{7,6},{8,9},{9,8},{10,11... | collective-permute-start | bytes 393224 | tf_op jit(solution)/shard_map/ppermute | solution.py:439
  8.9 22.5 %collective-permute-start.11 = (bf16[2,256,256]{2,1,0:T(8,128)(2,1)S(1)}, bf16[2,256,256]{2,1,0:T(8,128)(2,1)S(1)}, u32[]{:S(2)}, u32[]{:S(2)}) collective-permute-start(bf16[2,256,256]{2,1,0:T(8,128)(2,1)S(1)} %get-tuple-element.48), channel_id=1, source_target_pairs={{0,1},{1,0},{2,3},{3,2},{4,5},{5,4},{6,7},{7,6},{8,9},{9,8},{10,11... | collective-permute-start | bytes 786440 | tf_op jit(solution)/shard_map/ppermute | solution.py:439
  8.9 23.8 %collective-permute-start.12 = (bf16[2,256,256]{2,1,0:T(8,128)(2,1)S(1)}, bf16[2,256,256]{2,1,0:T(8,128)(2,1)S(1)}, u32[]{:S(2)}, u32[]{:S(2)}) collective-permute-start(bf16[2,256,256]{2,1,0:T(8,128)(2,1)S(1)} %get-tuple-element.49), channel_id=1, source_target_pairs={{0,2},{1,3},{2,0},{3,1},{4,6},{5,7},{6,4},{7,5},{8,10},{9,11},{10,... | collective-permute-start | bytes 786440 | tf_op jit(solution)/shard_map/ppermute | solution.py:439
  11.9 23.4 %collective-permute-start.13 = (bf16[2,256,256]{2,1,0:T(8,128)(2,1)S(1)}, bf16[2,256,256]{2,1,0:T(8,128)(2,1)S(1)}, u32[]{:S(2)}, u32[]{:S(2)}) collective-permute-start(bf16[2,256,256]{2,1,0:T(8,128)(2,1)S(1)} %get-tuple-element.50), channel_id=1, source_target_pairs={{0,3},{1,2},{2,1},{3,0},{4,7},{5,6},{6,5},{7,4},{8,11},{9,10},{10,... | collective-permute-start | bytes 786440 | tf_op jit(solution)/shard_map/ppermute | solution.py:439
  11.9 16.4 %collective-permute-start.2 = (bf16[256,256]{1,0:T(8,128)(2,1)S(1)}, bf16[256,256]{1,0:T(8,128)(2,1)S(1)}, u32[]{:S(2)}, u32[]{:S(2)}) collective-permute-start(bf16[256,256]{1,0:T(8,128)(2,1)S(1)} %get-tuple-element.37), channel_id=1, source_target_pairs={{0,2},{1,3},{2,0},{3,1},{4,6},{5,7},{6,4},{7,5},{8,10},{9,11},{10,... | collective-permute-start | bytes 393224 | tf_op jit(solution)/shard_map/ppermute | solution.py:439
  13.2 16.8 %collective-permute-start.3 = (bf16[256,256]{1,0:T(8,128)(2,1)S(1)}, bf16[256,256]{1,0:T(8,128)(2,1)S(1)}, u32[]{:S(2)}, u32[]{:S(2)}) collective-permute-start(bf16[256,256]{1,0:T(8,128)(2,1)S(1)} %get-tuple-element.38), channel_id=1, source_target_pairs={{0,3},{1,2},{2,1},{3,0},{4,7},{5,6},{6,5},{7,4},{8,11},{9,10},{10,... | collective-permute-start | bytes 393224 | tf_op jit(solution)/shard_map/ppermute | solution.py:439
  14.9 19.1 %copy-start.6 = (s32[16]{0:T(128)S(1)}, s32[16]{0:T(128)}, u32[]{:S(2)}) copy-start(s32[16]{0:T(128)} %windows.9) | copy-start | bytes 196
  14.9 61.2 %all-to-all-start = ((bf16[16,8,512]{2,1,0:T(8,128)(2,1)}), bf16[16,8,512]{2,1,0:T(8,128)(2,1)S(1)}, u32[]{:S(2)}, u32[]{:S(2)}) async-start(bf16[16,8,512]{2,1,0:T(8,128)(2,1)} %shard_map.71), calls=%async_computation | async-start | bytes 262144 | tf_op jit(solution)/shard_map/all_to_all | solution.py:499
  28.3 12.7 %collective-permute-start.6 = (bf16[3,256,256]{2,1,0:T(8,128)(2,1)}, bf16[3,256,256]{2,1,0:T(8,128)(2,1)}, u32[]{:S(2)}, u32[]{:S(2)}) collective-permute-start(bf16[3,256,256]{2,1,0:T(8,128)(2,1)} %get-tuple-element.40), channel_id=1, source_target_pairs={{0,1},{1,0},{2,3},{3,2},{4,5},{5,4},{6,7},{7,6},{8,9},{9,8},{10,11... | collective-permute-start | bytes 1179656 | tf_op jit(solution)/shard_map/ppermute | solution.py:439
  30.1 12.3 %collective-permute-start.7 = (bf16[3,256,256]{2,1,0:T(8,128)(2,1)}, bf16[3,256,256]{2,1,0:T(8,128)(2,1)}, u32[]{:S(2)}, u32[]{:S(2)}) collective-permute-start(bf16[3,256,256]{2,1,0:T(8,128)(2,1)} %get-tuple-element.41), channel_id=1, source_target_pairs={{0,2},{1,3},{2,0},{3,1},{4,6},{5,7},{6,4},{7,5},{8,10},{9,11},{10,... | collective-permute-start | bytes 1179656 | tf_op jit(solution)/shard_map/ppermute | solution.py:439
  31.4 18.6 %collective-permute-start.8 = (bf16[3,256,256]{2,1,0:T(8,128)(2,1)}, bf16[3,256,256]{2,1,0:T(8,128)(2,1)}, u32[]{:S(2)}, u32[]{:S(2)}) collective-permute-start(bf16[3,256,256]{2,1,0:T(8,128)(2,1)} %get-tuple-element.42), channel_id=1, source_target_pairs={{0,3},{1,2},{2,1},{3,0},{4,7},{5,6},{6,5},{7,4},{8,11},{9,10},{10,... | collective-permute-start | bytes 1179656 | tf_op jit(solution)/shard_map/ppermute | solution.py:439
  32.7 18.8 %collective-permute-start.4 = (bf16[4,256,256]{2,1,0:T(8,128)(2,1)S(1)}, bf16[4,256,256]{2,1,0:T(8,128)(2,1)S(1)}, u32[]{:S(2)}, u32[]{:S(2)}) collective-permute-start(bf16[4,256,256]{2,1,0:T(8,128)(2,1)S(1)} %shard_map.68.q), channel_id=1, source_target_pairs={{4,0},{5,1},{6,2},{7,3},{8,4},{9,5},{10,6},{11,7},{12,8},{13,9},{1... | collective-permute-start | bytes 1572872 | tf_op jit(solution)/shard_map/ppermute | solution.py:457
  36.3 13.7 %copy-start.13 = (bf16[3,256,256]{2,1,0:T(8,128)(2,1)S(1)}, bf16[3,256,256]{2,1,0:T(8,128)(2,1)}, u32[]{:S(2)}) copy-start(bf16[3,256,256]{2,1,0:T(8,128)(2,1)} %copy-done.12) | copy-start | bytes 1179652
  36.4 48.0 %collective-permute-start.14 = (bf16[4,2,256,256]{3,2,1,0:T(8,128)(2,1)S(1)}, bf16[4,2,256,256]{3,2,1,0:T(8,128)(2,1)S(1)}, u32[]{:S(2)}, u32[]{:S(2)}) collective-permute-start(bf16[4,2,256,256]{3,2,1,0:T(8,128)(2,1)S(1)} %shard_map.75.kv0), channel_id=1, source_target_pairs={{0,4},{1,5},{2,6},{3,7},{4,8},{5,9},{6,10},{7,11},{8,12},{9,13},{1... | collective-permute-start | bytes 3145736 | tf_op jit(solution)/shard_map/ppermute | solution.py:454
  51.5 16.3 %copy-start.8 = (bf16[4,3,256,256]{3,2,1,0:T(8,128)(2,1)}, bf16[4,3,256,256]{3,2,1,0:T(8,128)(2,1)S(1)}, u32[]{:S(2)}) copy-start(bf16[4,3,256,256]{3,2,1,0:T(8,128)(2,1)S(1)} %shard_map.69.kv.rest) | copy-start | bytes 4718596
  51.5 16.2 %collective-permute-start.5 = (bf16[4,256,256]{2,1,0:T(8,128)(2,1)S(1)}, bf16[4,256,256]{2,1,0:T(8,128)(2,1)S(1)}, u32[]{:S(2)}, u32[]{:S(2)}) collective-permute-start(bf16[4,256,256]{2,1,0:T(8,128)(2,1)S(1)} %collective-permute-done.4.q), channel_id=1, source_target_pairs={{4,0},{5,1},{6,2},{7,3},{8,4},{9,5},{10,6},{11,7},{12,8},{13,9},{1... | collective-permute-start | bytes 1572872 | tf_op jit(solution)/shard_map/ppermute | solution.py:457
  57.8 14.6 %copy-start.16 = (f32[2,128,1024]{2,1,0:T(8,128)}, f32[2,128,1024]{2,1,0:T(8,128)S(1)}, u32[]{:S(2)}) copy-start(f32[2,128,1024]{2,1,0:T(8,128)S(1)} %get-tuple-element.45.sums) | copy-start | bytes 3145732
  72.4 15.8 %collective-permute-start.9 = (bf16[2,144,1024]{2,1,0:T(8,128)(2,1)S(1)}, bf16[2,144,1024]{2,1,0:T(8,128)(2,1)S(1)}, u32[]{:S(2)}, u32[]{:S(2)}) collective-permute-start(bf16[2,144,1024]{2,1,0:T(8,128)(2,1)S(1)} %shard_map.70), channel_id=1, source_target_pairs={{0,4},{1,5},{2,6},{3,7},{4,8},{5,9},{6,10},{7,11},{8,12},{9,13},{1... | collective-permute-start | bytes 1769480 | tf_op jit(solution)/shard_map/ppermute | solution.py:454
  84.3 8.7 %copy-start.10 = (bf16[4,3,256,256]{3,2,1,0:T(8,128)(2,1)S(1)}, bf16[4,3,256,256]{3,2,1,0:T(8,128)(2,1)}, u32[]{:S(2)}) copy-start(bf16[4,3,256,256]{3,2,1,0:T(8,128)(2,1)} %copy-done.8) | copy-start | bytes 4718596
  85.4 14.5 %collective-permute-start.15 = (bf16[2,2,256,256]{3,2,1,0:T(8,128)(2,1)}, bf16[2,2,256,256]{3,2,1,0:T(8,128)(2,1)}, u32[]{:S(2)}, u32[]{:S(2)}) collective-permute-start(bf16[2,2,256,256]{3,2,1,0:T(8,128)(2,1)} %get-tuple-element.64), channel_id=1, source_target_pairs={{0,4},{1,5},{2,6},{3,7},{4,8},{5,9},{6,10},{7,11},{8,12},{9,13},{1... | collective-permute-start | bytes 1572872 | tf_op jit(solution)/shard_map/ppermute | solution.py:454
  88.5 11.4 %copy-start.5 = (f32[2048]{0:T(1024)S(1)}, f32[2048]{0:T(1024)}, u32[]{:S(2)}) copy-start(f32[2048]{0:T(1024)} %param.9) | copy-start | bytes 24580
  88.5 11.4 %copy-start.7 = (s32[16]{0:T(128)S(1)}, s32[16]{0:T(128)}, u32[]{:S(2)}) copy-start(s32[16]{0:T(128)} %starts.3) | copy-start | bytes 196
  88.6 22.3 %collective-permute-start.10 = (bf16[2,144,1024]{2,1,0:T(8,128)(2,1)S(1)}, bf16[2,144,1024]{2,1,0:T(8,128)(2,1)S(1)}, u32[]{:S(2)}, u32[]{:S(2)}) collective-permute-start(bf16[2,144,1024]{2,1,0:T(8,128)(2,1)S(1)} %shard_map.73), channel_id=1, source_target_pairs={{0,4},{1,5},{2,6},{3,7},{4,8},{5,9},{6,10},{7,11},{8,12},{9,13},{1... | collective-permute-start | bytes 1769480 | tf_op jit(solution)/shard_map/ppermute | solution.py:454
  110.8 23.6 %copy-start.4 = (bf16[3,8,2048]{2,1,0:T(8,128)(2,1)S(1)}, bf16[3,8,2048]{2,1,0:T(8,128)(2,1)}, u32[]{:S(2)}) copy-start(bf16[3,8,2048]{2,1,0:T(8,128)(2,1)} %cont.1) | copy-start | bytes 294916
  113.7 20.7 %all-to-all-start.1 = ((bf16[16,8,768]{2,1,0:T(8,128)(2,1)}), bf16[16,8,768]{2,1,0:T(8,128)(2,1)S(1)}, u32[]{:S(2)}, u32[]{:S(2)}) async-start(bf16[16,8,768]{2,1,0:T(8,128)(2,1)} %get-tuple-element.54), calls=%async_computation.1 | async-start | bytes 393216 | tf_op jit(solution)/shard_map/all_to_all | solution.py:565
  118.5 4.2 %collective-permute-start.16 = (bf16[256,256]{1,0:T(8,128)(2,1)S(1)}, bf16[256,256]{1,0:T(8,128)(2,1)S(1)}, u32[]{:S(2)}, u32[]{:S(2)}) collective-permute-start(bf16[256,256]{1,0:T(8,128)(2,1)S(1)} %get-tuple-element.56), channel_id=1, source_target_pairs={{0,1},{1,0},{2,3},{3,2},{4,5},{5,4},{6,7},{7,6},{8,9},{9,8},{10,11... | collective-permute-start | bytes 393224 | tf_op jit(solution)/shard_map/ppermute | solution.py:439
  118.9 8.0 %collective-permute-start.17 = (bf16[256,256]{1,0:T(8,128)(2,1)S(1)}, bf16[256,256]{1,0:T(8,128)(2,1)S(1)}, u32[]{:S(2)}, u32[]{:S(2)}) collective-permute-start(bf16[256,256]{1,0:T(8,128)(2,1)S(1)} %get-tuple-element.57), channel_id=1, source_target_pairs={{0,2},{1,3},{2,0},{3,1},{4,6},{5,7},{6,4},{7,5},{8,10},{9,11},{10,... | collective-permute-start | bytes 393224 | tf_op jit(solution)/shard_map/ppermute | solution.py:439
  120.6 8.2 %collective-permute-start.18 = (bf16[256,256]{1,0:T(8,128)(2,1)S(1)}, bf16[256,256]{1,0:T(8,128)(2,1)S(1)}, u32[]{:S(2)}, u32[]{:S(2)}) collective-permute-start(bf16[256,256]{1,0:T(8,128)(2,1)S(1)} %get-tuple-element.58), channel_id=1, source_target_pairs={{0,3},{1,2},{2,1},{3,0},{4,7},{5,6},{6,5},{7,4},{8,11},{9,10},{10,... | collective-permute-start | bytes 393224 | tf_op jit(solution)/shard_map/ppermute | solution.py:439
  120.6 8.2 %collective-permute-start.19 = (bf16[256,256]{1,0:T(8,128)(2,1)S(1)}, bf16[256,256]{1,0:T(8,128)(2,1)S(1)}, u32[]{:S(2)}, u32[]{:S(2)}) collective-permute-start(bf16[256,256]{1,0:T(8,128)(2,1)S(1)} %get-tuple-element.60), channel_id=1, source_target_pairs={{0,1},{1,0},{2,3},{3,2},{4,5},{5,4},{6,7},{7,6},{8,9},{9,8},{10,11... | collective-permute-start | bytes 393224 | tf_op jit(solution)/shard_map/ppermute | solution.py:439
  121.1 11.6 %collective-permute-start.20 = (bf16[256,256]{1,0:T(8,128)(2,1)S(1)}, bf16[256,256]{1,0:T(8,128)(2,1)S(1)}, u32[]{:S(2)}, u32[]{:S(2)}) collective-permute-start(bf16[256,256]{1,0:T(8,128)(2,1)S(1)} %get-tuple-element.61), channel_id=1, source_target_pairs={{0,2},{1,3},{2,0},{3,1},{4,6},{5,7},{6,4},{7,5},{8,10},{9,11},{10,... | collective-permute-start | bytes 393224 | tf_op jit(solution)/shard_map/ppermute | solution.py:439
  122.7 11.7 %collective-permute-start.21 = (bf16[256,256]{1,0:T(8,128)(2,1)S(1)}, bf16[256,256]{1,0:T(8,128)(2,1)S(1)}, u32[]{:S(2)}, u32[]{:S(2)}) collective-permute-start(bf16[256,256]{1,0:T(8,128)(2,1)S(1)} %get-tuple-element.62), channel_id=1, source_target_pairs={{0,3},{1,2},{2,1},{3,0},{4,7},{5,6},{6,5},{7,4},{8,11},{9,10},{10,... | collective-permute-start | bytes 393224 | tf_op jit(solution)/shard_map/ppermute | solution.py:439
  (15 other events, 33.8 us)
